TPU v7x, 32 devices: a whole 2x2x4 slice. The times are simulated.
32 devices in a mesh: parts: 1, seq: 32 (over z, y, x, core).
Axes of the slice: x: 2, y: 2, z: 4, core: 2. Of those that a mesh axis runs over, the one named last changes fastest.
Arguments:
- tokens: bfloat16 [1, 128, 3, 128, 3072], P('parts', 'seq'), may hold values from -6 to 6
- queries: bfloat16 [1, 128, 3, 128, 1536], P('parts', 'seq'), may hold values from -68 to 68
- key_weight: bfloat16 [3072, 1536], P('seq'), may hold values from -0.109375 to 0.109375
- value_weight: bfloat16 [3072, 1536], P('seq'), may hold values from -0.109375 to 0.109375
- halves: int32 [1, 128, 3, 2, 2], P('parts', 'seq'), may hold values from 1 to 3
Outputs:
- mixed: bfloat16 [1, 128, 3, 128, 1536], P('parts', 'seq')
Inputs may be any that keep to these rules, and one draw needn't show every extreme that they name: `halves`: 1 lists the first half of the partner lines, 2 the second half, 3 both.
All inputs are finite; a program needn't handle non-finite values.
Results may differ from a plain program's by a relative error of at most 0.012.
Values may be sent and summed in bfloat16 or wider, within the bound.
No kernel may reach another device: no remote copies, remote signals or barrier semaphores. Data moves between devices by JAX's collectives and lax.ppermute only.
A program may use at most 128 MiB of HBM per device.

v0:
```python
import math

import jax
import jax.numpy as jnp
from jax import lax
from jax.sharding import PartitionSpec as P

HEADS = 12
HDIM = 128


def split_heads(tensor_in):
    return tensor_in.reshape(tensor_in.shape[:-1] + (HEADS, HDIM))


def kept_keys(code_grid, grid_len):
    column = jnp.arange(grid_len)
    first_kept = (code_grid % 2 == 1)[..., None]
    second_kept = (code_grid >= 2)[..., None]
    return jnp.where(column < grid_len // 2, first_kept, second_kept)[..., None, :]


def codes_by_half(code_pairs, half_index):
    return jnp.where(half_index[None, None, :] == 0, code_pairs[..., 0:1], code_pairs[..., 1:2])


def partial_attention(queries_h, keys_h, values_h, score_form, value_form, kept_mask):
    scores = jnp.einsum(score_form, queries_h, keys_h, preferred_element_type=jnp.float32) * (
        1.0 / math.sqrt(HDIM)
    )
    masked = jnp.where(kept_mask, scores, -jnp.inf)
    peak_val = jnp.max(masked, axis=-1)
    weights = jnp.exp(masked - peak_val[..., None])
    totals = jnp.sum(weights, axis=-1)
    partial_out = jnp.einsum(
        value_form, weights.astype(jnp.bfloat16), values_h, preferred_element_type=jnp.float32
    )
    return (partial_out, peak_val, totals)


def merge_slots(near_part, far_part):
    peak_val = jnp.maximum(near_part[1], far_part[1])
    near_w = jnp.exp(near_part[1] - peak_val)
    far_w = jnp.exp(far_part[1] - peak_val) * far_part[2]
    upper = near_part[0] * near_w[..., None] + far_part[0] * far_w[..., None]
    return upper / (near_part[2] * near_w + far_w)[..., None]


def on_device(tokens, queries, key_weight, value_weight, halves):
    scenes, line_count, planes, grid_len, model_width = tokens.shape
    hidden_width = queries.shape[-1]
    home_rows = tokens.reshape(-1, model_width)

    def add_panel(weight_panel):
        return jnp.dot(home_rows, weight_panel, preferred_element_type=jnp.float32)

    key_sum = add_panel(lax.all_gather(key_weight, "seq", axis=0, tiled=True))
    value_sum = add_panel(lax.all_gather(value_weight, "seq", axis=0, tiled=True))
    home_shape = (scenes, line_count, planes, grid_len, hidden_width)
    keys_home = key_sum.astype(jnp.bfloat16).reshape(home_shape)
    values_home = value_sum.astype(jnp.bfloat16).reshape(home_shape)
    moved_q, moved_k, moved_v = (
        lax.all_to_all(queries, "seq", split_axis=3, concat_axis=1, tiled=True),
        lax.all_to_all(keys_home, "seq", split_axis=3, concat_axis=1, tiled=True),
        lax.all_to_all(values_home, "seq", split_axis=3, concat_axis=1, tiled=True),
    )
    code_table = lax.all_gather(halves, "seq", axis=1, tiled=True)
    half_len = grid_len // 2
    own_start = lax.axis_index("seq") * line_count
    moved_half = (own_start + jnp.arange(line_count)) // half_len
    home_half = jnp.arange(grid_len) // half_len
    remote_plan = (
        (0, keys_home[:, :, 2], values_home[:, :, 2], "sabhd,sbjhd->sabhj", "sabhj,sbjhd->sabhd"),
        (1, moved_k[:, :, 2], moved_v[:, :, 2], "sabhd,sjbhd->sabhj", "sabhj,sjbhd->sabhd"),
        (2, moved_k[:, :, 1], moved_v[:, :, 1], "sabhd,sjbhd->sabhj", "sabhj,sjbhd->sabhd"),
    )
    remote_results = []
    for plane_idx, keys_part, values_part, score_form, value_form in remote_plan:
        code_grid = codes_by_half(code_table[:, :, plane_idx, :, 1], moved_half)
        remote_results.append(
            partial_attention(
                split_heads(moved_q[:, :, plane_idx]),
                split_heads(keys_part),
                split_heads(values_part),
                score_form,
                value_form,
                kept_keys(code_grid, grid_len),
            )
        )
    remote_mean = jnp.stack([result[0] / result[2][..., None] for result in remote_results], axis=2)
    remote_mean = remote_mean.reshape(remote_mean.shape[:4] + (hidden_width,)).astype(jnp.bfloat16)
    remote_peak = jnp.stack([result[1] for result in remote_results], axis=2)
    remote_sum = jnp.stack([result[2] for result in remote_results], axis=2)
    back_mean = lax.all_to_all(remote_mean, "seq", split_axis=1, concat_axis=3, tiled=True)
    back_peak, back_sum = (
        lax.all_to_all(remote_peak, "seq", split_axis=1, concat_axis=3, tiled=True),
        lax.all_to_all(remote_sum, "seq", split_axis=1, concat_axis=3, tiled=True),
    )
    home_plan = (
        (0, keys_home[:, :, 1], values_home[:, :, 1], "sabhd,sajhd->sabhj", "sabhj,sajhd->sabhd"),
        (1, keys_home[:, :, 0], values_home[:, :, 0], "sabhd,sajhd->sabhj", "sabhj,sajhd->sabhd"),
        (2, moved_k[:, :, 0], moved_v[:, :, 0], "sabhd,sjahd->sabhj", "sabhj,sjahd->sabhd"),
    )
    home_results = []
    for plane_idx, keys_part, values_part, score_form, value_form in home_plan:
        code_grid = codes_by_half(halves[:, :, plane_idx, :, 0], home_half)
        home_results.append(
            partial_attention(
                split_heads(queries[:, :, plane_idx]),
                split_heads(keys_part),
                split_heads(values_part),
                score_form,
                value_form,
                kept_keys(code_grid, grid_len),
            )
        )
    home_out = jnp.stack([result[0] for result in home_results], axis=2)
    home_peak = jnp.stack([result[1] for result in home_results], axis=2)
    home_sum = jnp.stack([result[2] for result in home_results], axis=2)
    merged = merge_slots(
        (home_out, home_peak, home_sum),
        (split_heads(back_mean.astype(jnp.float32)), back_peak, back_sum),
    )
    return merged.reshape(home_shape).astype(jnp.bfloat16)


def solution(mesh):
    in_specs = (
        P("parts", "seq", None, None, None),
        P("parts", "seq", None, None, None),
        P("seq", None),
        P("seq", None),
        P("parts", "seq", None, None, None),
    )
    out_specs = P("parts", "seq", None, None, None)
    return jax.shard_map(
        on_device, mesh=mesh, in_specs=in_specs, out_specs=out_specs, check_vma=False
    )
```

profile of v0, /device:TPU:0, one launch (start us, length us, event | category | flops | bytes accessed | tf_op | source)
XLA Modules:
  0.0 732.5 jit_solution(9357103538851799629)
XLA Ops:
  8.0 8.2 %copy.418 = bf16[1,4,3,128,1536]{4,1,2,0,3:T(4,128)(2,1)} copy(bf16[1,4,3,128,1536]{4,3,2,1,0:T(8,128)(2,1)} %param.6) | data formatting | bytes 9437184 | tf_op args[1]
  16.2 7.4 %all-to-all-start.2 = ((bf16[1,4,3,128,1536]{4,1,2,0,3:T(4,128)(2,1)}), bf16[1,4,3,128,1536]{4,1,2,0,3:T(4,128)(2,1)}, u32[]{:S(2)}, u32[]{:S(2)}) async-start(bf16[1,4,3,128,1536]{4,1,2,0,3:T(4,128)(2,1)} %copy.418), calls=%async_computation.2 | async-start | bytes 9437184 | tf_op jit(solution)/shard_map/all_to_all | solution.py:63
  23.6 128.7 %all-gather.3.cloned.1.call-done = bf16[3072,1536]{1,0:T(8,128)(2,1)} async-done(((bf16[96,1536]{1,0:T(8,128)(2,1)}), bf16[3072,1536]{1,0:T(8,128)(2,1)}) %all-gather.3.cloned.1.call-update) | async-done | bytes 9437200 | tf_op jit(solution)/shard_map/all_gather | solution.py:58
  152.3 19.9 %convolution_convert_fusion.1 = bf16[1536,1536]{1,0:T(8,128)(2,1)S(1)} fusion(bf16[1536,3072]{1,0:T(8,128)(2,1)} %bitcast.326, bf16[3072,1536]{1,0:T(8,128)(2,1)} %all-gather.3.cloned.1.call-done), kind=kOutput, calls=%fused_computation.7 | convolution fusion | flops 14497873920 | bytes 23592960 | tf_op jit(solution)/shard_map/dot_general | solution.py:55
  174.3 5.8 copy.400
  184.0 105.3 %all-gather.5.cloned.1.call-done = bf16[3072,1536]{1,0:T(8,128)(2,1)} async-done(((bf16[96,1536]{1,0:T(8,128)(2,1)}), bf16[3072,1536]{1,0:T(8,128)(2,1)}) %all-gather.5.cloned.1.call-update) | async-done | bytes 9437200 | tf_op jit(solution)/shard_map/all_gather | solution.py:57
  289.3 19.9 %convolution_convert_fusion = bf16[1536,1536]{1,0:T(8,128)(2,1)S(1)} fusion(bf16[1536,3072]{1,0:T(8,128)(2,1)} %bitcast.327, bf16[3072,1536]{1,0:T(8,128)(2,1)} %all-gather.5.cloned.1.call-done), kind=kOutput, calls=%fused_computation.6 | convolution fusion | flops 14497873920 | bytes 23592960 | tf_op jit(solution)/shard_map/dot_general | solution.py:55
  311.4 5.8 copy.404
  317.2 7.0 all-to-all-done
  328.1 113.8 %all_gather.11 = s32[1,128,3,2,2]{2,4,3,0,1:T(2,128)S(1)} all-gather(s32[1,4,3,2,2]{2,4,3,0,1:T(2,128)S(1)} %copy.415), channel_id=1, replica_groups=mesh['parts'=1,'seq'=32] {'seq'}, dimensions={1}, use_global_device_ids=true | all-gather | bytes 6336 | tf_op jit(solution)/shard_map/all_gather | solution.py:67
  443.1 4.7 copy.419
  459.9 4.4 fusion.97
  465.9 4.5 fusion.96
  519.5 19.8 %all-to-all-start.3 = ((f32[32,1,576]{2,1,0:T(1,128)}), f32[32,1,576]{2,1,0:T(1,128)S(1)}, u32[]{:S(2)}, u32[]{:S(2)}) async-start(f32[32,1,576]{2,1,0:T(1,128)} %reshape.1497), calls=%async_computation.3 | async-start | bytes 163840 | tf_op jit(solution)/shard_map/all_to_all | solution.py:96
  554.8 5.9 all-to-all-start.5
  560.8 6.4 pad_maximum_fusion
  569.0 4.8 all-to-all-start.4
  605.9 4.2 copy.407
  635.6 43.3 %all-to-all-done.4 = bf16[1,128,3,4,1536]{4,3,2,0,1:T(4,128)(2,1)} async-done(((bf16[1,128,3,4,1536]{4,3,2,0,1:T(4,128)(2,1)}), bf16[1,128,3,4,1536]{4,3,2,0,1:T(4,128)(2,1)}, u32[]{:S(2)}, u32[]{:S(2)}) %all-to-all-start.4) | async-done | bytes 4718624 | tf_op jit(solution)/shard_map/all_to_all | solution.py:94
  678.9 7.4 %convert_bitcast_fusion = f32[1,4,3,32,4,1536]{5,4,2,1,3,0:T(4,128)} fusion(bf16[1,32,4,3,4,1536]{5,4,3,2,1,0:T(4,128)(2,1)} %bitcast.133), kind=kLoop, calls=%fused_computation.3 | loop fusion | flops 2359296 | bytes 14155776 | tf_op jit(solution)/shard_map/convert_element_type | solution.py:122
  686.3 11.8 %copy.447 = f32[1,4,3,32,4,1536]{5,1,4,3,2,0:T(4,128)} copy(f32[1,4,3,32,4,1536]{5,4,2,1,3,0:T(4,128)} %convert_bitcast_fusion) | data formatting | bytes 18874368 | tf_op jit(solution)/shard_map/convert_element_type | solution.py:122
  698.1 12.0 %copy.454 = f32[1,4,3,128,1536]{3,4,2,1,0:T(8,128)} copy(f32[1,4,3,128,1536]{4,1,3,2,0:T(4,128)} %bitcast.266) | data formatting | bytes 18874368 | tf_op jit(solution)/shard_map/convert_element_type | solution.py:122
  710.1 8.8 %fusion.2 = bf16[1,4,3,128,1536]{3,4,2,1,0:T(8,128)(2,1)} fusion(f32[1,4,3,128,1536]{3,4,2,1,0:T(8,128)} %copy.454, f32[1,4,1,128,1536]{3,4,2,1,0:T(8,128)} %bitcast.278, f32[1,4,1,128,1536]{3,4,2,1,0:T(8,128)} %bitcast.277, f32[1,4,1,128,1536]{3,4,2,1,0:T(8,128)S(1)} %bitcast.276, f32[4,3,128,12]{2,3,0,1:T(8,128)S(1)} %get-tuple-element.6, ...), kind=kLoop, calls=%fused_computation.5 | loop fusion | flops 16515072 | bytes 23814144 | tf_op jit(solution)/shard_map/convert_element_type | solution.py:124
  718.9 6.6 copy.456
  (157 shorter events, 151.9 us)
Async XLA Ops:
  6.5 145.7 %all-gather.3.cloned.1.call-start = ((), (), s32[]{:S(2)}) async-start(), calls=%async_computation.6 | async-start | bytes 9732096 | tf_op jit(solution)/shard_map/all_gather | solution.py:58
  7.3 282.0 %all-gather.5.cloned.1.call-start = ((), (), s32[]{:S(2)}) async-start(), calls=%async_computation.7 | async-start | bytes 9732096 | tf_op jit(solution)/shard_map/all_gather | solution.py:57
  16.2 164.0 %all-to-all-start.2 = ((bf16[1,4,3,128,1536]{4,1,2,0,3:T(4,128)(2,1)}), bf16[1,4,3,128,1536]{4,1,2,0,3:T(4,128)(2,1)}, u32[]{:S(2)}, u32[]{:S(2)}) async-start(bf16[1,4,3,128,1536]{4,1,2,0,3:T(4,128)(2,1)} %copy.418), calls=%async_computation.2 | async-start | bytes 9437184 | tf_op jit(solution)/shard_map/all_to_all | solution.py:63
  180.2 144.1 %all-to-all-start = ((bf16[1,4,3,128,1536]{4,1,2,0,3:T(4,128)(2,1)}), bf16[1,4,3,128,1536]{4,1,2,0,3:T(4,128)(2,1)}, u32[]{:S(2)}, u32[]{:S(2)}) async-start(bf16[1,4,3,128,1536]{4,1,2,0,3:T(4,128)(2,1)} %copy.400), calls=%async_computation | async-start | bytes 9437184 | tf_op jit(solution)/shard_map/all_to_all | solution.py:65
  317.2 10.8 %copy-start.29 = (s32[1,4,3,2,2]{1,4,3,2,0:T(2,128)S(1)}, s32[1,4,3,2,2]{1,4,3,2,0:T(2,128)}, u32[]{:S(2)}) copy-start(s32[1,4,3,2,2]{1,4,3,2,0:T(2,128)} %param.9) | copy-start | bytes 580
  324.2 169.1 %all-to-all-start.1 = ((bf16[1,4,3,128,1536]{4,1,2,0,3:T(4,128)(2,1)}), bf16[1,4,3,128,1536]{4,1,2,0,3:T(4,128)(2,1)}, u32[]{:S(2)}, u32[]{:S(2)}) async-start(bf16[1,4,3,128,1536]{4,1,2,0,3:T(4,128)(2,1)} %copy.404), calls=%async_computation.1 | async-start | bytes 9437184 | tf_op jit(solution)/shard_map/all_to_all | solution.py:64
  442.8 5.0 copy-start.31
  519.5 35.3 %all-to-all-start.3 = ((f32[32,1,576]{2,1,0:T(1,128)}), f32[32,1,576]{2,1,0:T(1,128)S(1)}, u32[]{:S(2)}, u32[]{:S(2)}) async-start(f32[32,1,576]{2,1,0:T(1,128)} %reshape.1497), calls=%async_computation.3 | async-start | bytes 163840 | tf_op jit(solution)/shard_map/all_to_all | solution.py:96
  539.3 3.9 copy-start.3
  539.3 3.9 copy-start.17
  545.6 5.4 copy-start.24
  545.6 5.4 copy-start.25
  546.9 13.9 %copy-start.7 = (bf16[1,128,1,4,1536]{4,3,2,0,1:T(4,128)(2,1)S(1)}, bf16[1,128,1,4,1536]{4,3,2,0,1:T(4,128)(2,1)}, u32[]{:S(2)}) copy-start(bf16[1,128,1,4,1536]{4,3,2,0,1:T(4,128)(2,1)} %copy.444) | copy-start | bytes 4718596
  554.8 13.5 %all-to-all-start.5 = ((f32[32,1,576]{2,1,0:T(1,128)}), f32[32,1,576]{2,1,0:T(1,128)S(1)}, u32[]{:S(2)}, u32[]{:S(2)}) async-start(f32[32,1,576]{2,1,0:T(1,128)} %reshape.1495), calls=%async_computation.5 | async-start | bytes 163840 | tf_op jit(solution)/shard_map/all_to_all | solution.py:97
  569.0 109.9 %all-to-all-start.4 = ((bf16[1,128,3,4,1536]{4,3,2,0,1:T(4,128)(2,1)}), bf16[1,128,3,4,1536]{4,3,2,0,1:T(4,128)(2,1)}, u32[]{:S(2)}, u32[]{:S(2)}) async-start(bf16[1,128,3,4,1536]{4,3,2,0,1:T(4,128)(2,1)} %pad_maximum_fusion), calls=%async_computation.4 | async-start | bytes 9437184 | tf_op jit(solution)/shard_map/all_to_all | solution.py:94
  579.4 4.3 copy-start.30
  579.4 4.5 copy-start.32
  579.4 4.6 copy-start.5
  581.0 4.7 copy-start.4
  585.7 4.3 copy-start.6
  587.3 4.3 copy-start.10
  624.4 9.5 %copy-start.27 = (f32[4,128,12]{1,2,0:T(8,128)S(1)}, f32[4,128,12]{1,2,0:T(8,128)}, u32[]{:S(2)}) copy-start(f32[4,128,12]{1,2,0:T(8,128)} %fusion.8) | copy-start | bytes 73732
  624.4 9.5 %copy-start.28 = (f32[4,128,12]{1,2,0:T(8,128)S(1)}, f32[4,128,12]{1,2,0:T(8,128)}, u32[]{:S(2)}) copy-start(f32[4,128,12]{1,2,0:T(8,128)} %fusion.10) | copy-start | bytes 73732
  698.1 12.0 %copy-start.20 = (f32[4,3,128,12]{2,3,0,1:T(8,128)S(1)}, f32[4,3,128,12]{2,3,0,1:T(8,128)}, u32[]{:S(2)}) copy-start(f32[4,3,128,12]{2,3,0,1:T(8,128)} %get-tuple-element.7) | copy-start | bytes 221188
  (17 other events, 31.8 us)
Sparse Core Ops, SparseCore 0:
  10.2 141.9 all-gather.2
  155.2 134.0 all-gather.4
where the time goes:
time: 743 us; the launch traced here: 733 us
  waiting for transfers between devices  287 us (39%)
  local copies, waits for them, and re-layouts  173 us (23%)
  blocking collectives  114 us (15%)
  matrix products  64.8 us (9%)
  starting transfers between devices  45.5 us (6%)
  other arithmetic  34.7 us (5%)
  between operations  14.1 us (2%)
    all_gather x1, waiting for transfers between devices, on_device(): lax.all_gather(value_weight, 'seq', axis=0, tiled=True)  129 us
    all_gather x1, blocking collectives, on_device(): code_table = lax.all_gather(halves, 'seq', axis=1, tiled=True)  114 us
    all_gather x1, waiting for transfers between devices, on_device(): key_sum = add_panel(lax.all_gather(key_weight, 'seq', axis=0, tiled=True))  105 us
    all_to_all x1, waiting for transfers between devices, on_device(): lax.all_to_all(remote_mean, 'seq', split_axis=1, concat_axis=3, tiled=True)  43.3 us
    dot_general x2, matrix products, add_panel(): return jnp.dot(home_rows, weight_panel, preferred_element_type=jnp.float32)  39.8 us
    unnamed x78, local copies, waits for them, and re-layouts  39.1 us
    convert_element_type x2, local copies, waits for them, and re-layouts, on_device(): back_mean.astype(jnp.float32)  23.8 us
    all_to_all x1, starting transfers between devices, on_device(): lax.all_to_all(remote_peak, 'seq', split_axis=1, concat_axis=3, tiled=True)  19.8 us
  transfers between devices with their start and end apart: 8, of which 5 were waited for; matrix products, arithmetic and copies ran while one was open for 26% of the time, Pallas kernels for 0%

commit v1 on v0

v1 whole, which is shorter than its diff:
```python
import functools
import math

import jax
import jax.numpy as jnp
import numpy as np
from jax import lax
from jax.experimental import pallas as pl
from jax.experimental.pallas import tpu as pltpu
from jax.sharding import PartitionSpec as P

HEADS = 12
HDIM = 128
LANES = 128
SCALE = 1.0 / math.sqrt(HDIM)
BF16 = jnp.bfloat16
F32 = jnp.float32


def home_order(lines, res):
    span = res // lines
    out = np.zeros((res, res), np.float32)
    for line in range(lines):
        for dest in range(span // lines):
            for pos in range(lines):
                out[(dest * lines + pos) * lines + line, line * span + dest * lines + pos] = 1.0
    return out


def away_order(lines, res):
    span = res // lines
    out = np.zeros((res, res), np.float32)
    for src in range(span // lines):
        for pos in range(lines):
            for line in range(lines):
                out[pos * span + src * lines + line, (src * lines + pos) * lines + line] = 1.0
    return out


def pick(order, rows):
    return jnp.dot(order, rows, preferred_element_type=F32).astype(BF16)


def order_kernel(x_ref, order_ref, out_ref):
    lines, span, width = x_ref.shape
    out_ref[...] = pick(order_ref[...], x_ref[...].reshape(lines * span, width))


def order_queries(queries, order):
    lines, planes, res, width = queries.shape
    span = res // lines
    return pl.pallas_call(
        order_kernel,
        grid=(planes, lines),
        in_specs=[
            pl.BlockSpec((lines, None, span, width), lambda p, i: (0, p, i, 0)),
            pl.BlockSpec((res, res), lambda p, i: (0, 0)),
        ],
        out_specs=pl.BlockSpec((res, width), lambda p, i: (i, p)),
        out_shape=jax.ShapeDtypeStruct((lines * res, planes * width), BF16),
        cost_estimate=pl.CostEstimate(
            flops=2 * queries.size * res, bytes_accessed=4 * queries.size, transcendentals=0
        ),
        name="order_queries",
    )(queries, order)


def project_kernel(x_ref, w_ref, order_ref, home_ref, sent_ref):
    lines, res, depth = x_ref.shape
    tile = w_ref.shape[1]
    span = res // lines
    out = jnp.dot(x_ref[...].reshape(lines * res, depth), w_ref[...], preferred_element_type=F32)
    out = out.astype(BF16).reshape(lines, res, tile)
    home_ref[...] = out
    for i in range(lines):
        rows = out[:, i * span : (i + 1) * span].reshape(res, tile)
        sent_ref[pl.ds(i * res, res), :] = pick(order_ref[...], rows)


def project(tokens, weight, order, plane):
    lines, planes, res, depth = tokens.shape
    width = weight.shape[1]
    tile = 256
    return pl.pallas_call(
        project_kernel,
        grid=(width // tile,),
        in_specs=[
            pl.BlockSpec((lines, None, res, depth), lambda n: (0, plane, 0, 0)),
            pl.BlockSpec((depth, tile), lambda n: (0, n)),
            pl.BlockSpec((res, res), lambda n: (0, 0)),
        ],
        out_specs=[
            pl.BlockSpec((lines, res, tile), lambda n: (0, 0, n)),
            pl.BlockSpec((lines * res, tile), lambda n: (0, n)),
        ],
        out_shape=[
            jax.ShapeDtypeStruct((lines, res, width), BF16),
            jax.ShapeDtypeStruct((lines * res, width), BF16),
        ],
        cost_estimate=pl.CostEstimate(
            flops=2 * lines * res * depth * width,
            bytes_accessed=2 * (lines * res * (depth + 2 * width) + depth * width),
            transcendentals=0,
        ),
        name=f"project_{plane}",
    )(tokens, weight, order)


def to_away(src_ref, order_ref, dst_ref):
    lines, res, width = dst_ref.shape
    span = res // lines
    for c in range(lines):
        rows = pick(order_ref[...], src_ref[pl.ds(c * res, res), :])
        for pos in range(lines):
            dst_ref[pos, pl.ds(c * span, span), :] = rows[pos * span : (pos + 1) * span]


def attend(q, k, v, bias):
    scores = lax.dot_general(q, k, (((1,), (1,)), ((), ())), preferred_element_type=F32)
    scores = scores * SCALE + bias
    peak = jnp.max(scores, axis=1, keepdims=True)
    weights = jnp.exp(scores - peak)
    total = jnp.sum(weights, axis=1, keepdims=True)
    out = jnp.dot(weights.astype(BF16), v, preferred_element_type=F32)
    return out, peak, total


def far_kernel(moved_kv, q_ref, kv_ref, bias_ref, order_ref, back_ref, out_ref, q_s, kv_s, mean_s):
    lines, res, width = q_s.shape
    span = res // lines
    heads = width // HDIM
    to_away(q_ref, order_ref, q_s)
    if moved_kv:
        to_away(kv_ref, order_ref, kv_s)
    else:
        kv_s = kv_ref
    lane = lax.broadcasted_iota(jnp.int32, (res, LANES), 1)

    def step(i, carry):
        lse = jnp.zeros((res, LANES), F32)
        for h in range(heads):
            at = pl.ds(h * HDIM, HDIM)
            out, peak, total = attend(
                q_s[i, :, at], kv_s[i, :, at], kv_s[i, :, pl.ds(width + h * HDIM, HDIM)], bias_ref[...]
            )
            mean_s[i, :, at] = (out * (1.0 / total)).astype(BF16)
            lse = jnp.where(lane == h, peak + jnp.log(total), lse)
        high = lse.astype(BF16).astype(F32)
        mid = (lse - high).astype(BF16).astype(F32)
        low = (lse - high - mid).astype(BF16).astype(F32)
        parts = high + pltpu.roll(mid, 16, 1) + pltpu.roll(low, 32, 1)
        mean_s[i, :, pl.ds(width, LANES)] = parts.astype(BF16)
        return carry

    lax.fori_loop(0, lines, step, 0)
    for c in range(lines):
        rows = jnp.concatenate([mean_s[pos, pl.ds(c * span, span), :] for pos in range(lines)], axis=0)
        out_ref[pl.ds(c * res, res), :] = pick(back_ref[...], rows)


VMEM_SPEC = pl.BlockSpec(memory_space=pltpu.VMEM)


def attention_cost(lines, res, width):
    return pl.CostEstimate(
        flops=4 * lines * res * res * width,
        bytes_accessed=2 * lines * res * width * 5,
        transcendentals=lines * res * res * (width // HDIM),
    )


def far_attention(moved_q, kv, bias, order, back, plane, lines, res, width):
    moved_kv = kv.ndim == 2
    kv_shape = (lines, res, 2 * width) if moved_kv else (1, 16, LANES)
    return pl.pallas_call(
        functools.partial(far_kernel, moved_kv),
        grid=(1,),
        in_specs=[
            pl.BlockSpec((lines * res, width), lambda n: (0, plane)),
            pl.BlockSpec(kv.shape, lambda n: (0,) * kv.ndim),
            pl.BlockSpec((None, res, res), lambda n: (plane, 0, 0)),
            pl.BlockSpec((res, res), lambda n: (0, 0)),
            pl.BlockSpec((res, res), lambda n: (0, 0)),
        ],
        out_specs=pl.BlockSpec((lines * res, width + LANES), lambda n: (0, 0)),
        out_shape=jax.ShapeDtypeStruct((lines * res, width + LANES), BF16),
        scratch_shapes=[
            pltpu.VMEM((lines, res, width), BF16),
            pltpu.VMEM(kv_shape, BF16),
            pltpu.VMEM((lines, res, width + LANES), BF16),
        ],
        cost_estimate=attention_cost(lines, res, width),
        name=f"far_{plane}",
    )(moved_q, kv, bias, order, back)


def near_kernel(moved_kv, q_ref, kv_ref, bias_ref, far_ref, order_ref, back_ref, done_ref, out_ref, kv_s, far_s):
    lines, res, width = q_ref.shape
    span = res // lines
    heads = width // HDIM
    if moved_kv:
        to_away(kv_ref, order_ref, kv_s)
    else:
        kv_s = kv_ref
    for c in range(lines):
        rows = pick(back_ref[...], far_ref[pl.ds(c * res, res), :])
        for line in range(lines):
            far_s[line, pl.ds(c * span, span), :] = rows[line * span : (line + 1) * span]

    def step(i, carry):
        parts = far_s[i, :, pl.ds(width, LANES)].astype(F32)
        lse = parts + pltpu.roll(parts, LANES - 16, 1) + pltpu.roll(parts, LANES - 32, 1)
        for h in range(heads):
            at = pl.ds(h * HDIM, HDIM)
            out, peak, total = attend(
                q_ref[i, :, at], kv_s[i, :, at], kv_s[i, :, pl.ds(width + h * HDIM, HDIM)], bias_ref[i]
            )
            far_lse = lse[:, h : h + 1]
            top = jnp.maximum(peak, far_lse)
            near_w = jnp.exp(peak - top)
            far_w = jnp.exp(far_lse - top)
            scale = 1.0 / (total * near_w + far_w)
            mixed = out * (near_w * scale) + far_s[i, :, at].astype(F32) * (far_w * scale)
            out_ref[i, :, at] = mixed.astype(BF16)
        return carry

    lax.fori_loop(0, lines, step, 0)


def near_attention(queries, kv, bias, far, order, back, plane, done):
    lines, planes, res, width = queries.shape
    moved_kv = kv.ndim == 2
    kv_shape = (lines, res, 2 * width) if moved_kv else (1, 16, LANES)
    first = done is None
    kernel = functools.partial(near_kernel, moved_kv)
    in_specs = [
        pl.BlockSpec((lines, None, res, width), lambda n: (0, plane, 0, 0)),
        pl.BlockSpec(kv.shape, lambda n: (0,) * kv.ndim),
        pl.BlockSpec((None, lines, res, res), lambda n: (plane, 0, 0, 0)),
        pl.BlockSpec((lines * res, width + LANES), lambda n: (0, 0)),
        pl.BlockSpec((res, res), lambda n: (0, 0)),
        pl.BlockSpec((res, res), lambda n: (0, 0)),
        pl.BlockSpec(memory_space=pl.ANY),
    ]
    args = (queries, kv, bias, far, order, back)
    if first:
        body = lambda *refs: kernel(*refs[:6], None, *refs[6:])
        in_specs = in_specs[:-1]
        alias = {}
    else:
        body = kernel
        args = args + (done,)
        alias = {6: 0}
    return pl.pallas_call(
        body,
        grid=(1,),
        in_specs=in_specs,
        out_specs=pl.BlockSpec((lines, None, res, width), lambda n: (0, plane, 0, 0)),
        out_shape=jax.ShapeDtypeStruct(queries.shape, BF16),
        scratch_shapes=[
            pltpu.VMEM(kv_shape, BF16),
            pltpu.VMEM((lines, res, width + LANES), BF16),
        ],
        input_output_aliases=alias,
        cost_estimate=attention_cost(lines, res, width),
        name=f"near_{plane}",
    )(*args)


def mask_bias(codes, res):
    first_kept = (codes % 2 == 1)[..., None]
    second_kept = (codes >= 2)[..., None]
    kept = jnp.where(jnp.arange(res) < res // 2, first_kept, second_kept)
    return jnp.where(kept, 0.0, -jnp.inf).astype(F32)


def exchange(rows):
    return lax.all_to_all(rows, "seq", split_axis=0, concat_axis=0, tiled=True)


def on_device(count, tokens, queries, key_weight, value_weight, halves):
    scenes, lines, planes, res, depth = tokens.shape
    width = queries.shape[-1]
    tokens = tokens.reshape(lines, planes, res, depth)
    queries = queries.reshape(lines, planes, res, width)
    halves = halves.reshape(lines, planes, 2, 2)
    to_sent = jnp.asarray(home_order(lines, res), BF16)
    to_home = jnp.asarray(home_order(lines, res).T, BF16)
    away = jnp.asarray(away_order(lines, res), BF16)
    from_away = jnp.asarray(away_order(lines, res).T, BF16)

    weight = lax.all_gather(jnp.concatenate([key_weight, value_weight], axis=1), "seq", axis=0, tiled=True)

    dest_half = (np.arange(count) * lines) // (res // 2)
    sent_codes = jnp.where(
        (dest_half == 0)[:, None], halves[:, :, 0, 1].reshape(1, -1), halves[:, :, 1, 1].reshape(1, -1)
    )
    codes = exchange(sent_codes).reshape(res, planes).T
    far_bias = mask_bias(codes, res)
    home_half = jnp.arange(res) // (res // 2)
    near_codes = jnp.where(home_half == 0, halves[:, :, 0:1, 0], halves[:, :, 1:2, 0])
    near_bias = mask_bias(near_codes.transpose(1, 0, 2), res)

    moved_q = exchange(order_queries(queries, to_sent))
    home_2, sent_2 = project(tokens, weight, to_sent, 2)
    moved_2 = exchange(sent_2)
    home_1, sent_1 = project(tokens, weight, to_sent, 1)
    far = functools.partial(far_attention, order=away, back=from_away, lines=lines, res=res, width=width)
    far_0 = exchange(far(moved_q, home_2, far_bias, plane=0))
    moved_1 = exchange(sent_1)
    home_0, sent_0 = project(tokens, weight, to_sent, 0)
    far_1 = exchange(far(moved_q, moved_2, far_bias, plane=1))
    moved_0 = exchange(sent_0)
    far_2 = exchange(far(moved_q, moved_1, far_bias, plane=2))
    out = near_attention(queries, home_1, near_bias, far_0, away, to_home, 0, None)
    out = near_attention(queries, home_0, near_bias, far_1, away, to_home, 1, out)
    out = near_attention(queries, moved_0, near_bias, far_2, away, to_home, 2, out)
    return out.reshape(scenes, lines, planes, res, width)


def solution(mesh):
    in_specs = (
        P("parts", "seq", None, None, None),
        P("parts", "seq", None, None, None),
        P("seq", None),
        P("seq", None),
        P("parts", "seq", None, None, None),
    )
    return jax.shard_map(
        functools.partial(on_device, mesh.shape["seq"]),
        mesh=mesh,
        in_specs=in_specs,
        out_specs=P("parts", "seq", None, None, None),
        check_vma=False,
    )
```

time: 743 us -> 643 us (0.87); the launches traced: 733 us -> 641 us
  Pallas kernels: 0 us -> 178 us
  local copies, waits for them, and re-layouts: 173 us -> 6.44 us
  waiting for transfers between devices: 287 us -> 361 us
  blocking collectives: 114 us -> 43.9 us
  matrix products: 64.8 us -> 0 us
  other arithmetic: 34.7 us -> 6.28 us
  starting transfers between devices: 45.5 us -> 32.9 us
    pallas_call x0 -> x10, Pallas kernels: none -> 178 us  [the longest x3 59.6 us: project(): pl.pallas_call(project_kernel, grid=(width // tile,), in_specs=[pl.BlockS...]
    all_to_all x6 -> x7, waiting for transfers between devices: 51.5 us -> 181 us  [exchange(): return lax.all_to_all(rows, 'seq', split_axis=0, concat_axis=0, tiled=True)]
    all_gather x1 -> x0, blocking collectives: 114 us -> none  [on_device(): code_table = lax.all_gather(halves, 'seq', axis=1, tiled=True)]
    dot_general x14 -> x0, matrix products: 64.8 us -> none  [the longest x2 39.8 us: add_panel(): return jnp.dot(home_rows, weight_panel, preferred_element_type=jnp.float32)]
    all_gather x2 -> x1, waiting for transfers between devices: 234 us -> 180 us  [on_device(): lax.all_gather(jnp.concatenate([key_weight, value_weight], axis=1), 'seq'...]
    slice x23 -> x3, local copies, waits for them, and re-layouts: 54.1 us -> 0.96 us  [the longest x2 0.87 us: on_device(): halves[:, :, 0, 1].reshape(1, -1)]
    all_to_all x0 -> x1, blocking collectives: none -> 43.9 us  [exchange(): return lax.all_to_all(rows, 'seq', split_axis=0, concat_axis=0, tiled=True)]
    unnamed x78 -> x8, local copies, waits for them, and re-layouts: 39.1 us -> 4.53 us
  transfers between devices with their start and end apart: 8 -> 8, of which waited for: 5 -> 6; matrix products, arithmetic and copies ran while one was open for 26% -> 1% of each run, Pallas kernels for 0% -> 22%
where the time goes in v1:
time: 643 us; the launch traced here: 641 us
  waiting for transfers between devices  361 us (56%)
  Pallas kernels  178 us (28%)
  blocking collectives  43.9 us (7%)
  starting transfers between devices  32.9 us (5%)
  between operations  13.5 us (2%)
  local copies, waits for them, and re-layouts  6.44 us (1%)
    all_to_all x7, waiting for transfers between devices, exchange(): return lax.all_to_all(rows, 'seq', split_axis=0, concat_axis=0, tiled=True)  181 us
    all_gather x1, waiting for transfers between devices, on_device(): lax.all_gather(jnp.concatenate([key_weight, value_weight], axis=1), 'seq'...  180 us
    pallas_call x3, Pallas kernels, project(): pl.pallas_call(project_kernel, grid=(width // tile,), in_specs=[pl.BlockS...  59.6 us
    pallas_call x3, Pallas kernels, near_attention(): pl.pallas_call(body, grid=(1,), in_specs=in_specs, out_specs=pl.BlockSpec...  56 us
    pallas_call x3, Pallas kernels, far_attention(): pl.pallas_call(functools.partial(far_kernel, moved_kv), grid=(1,), in_spe...  52.3 us
    all_to_all x1, blocking collectives, exchange(): return lax.all_to_all(rows, 'seq', split_axis=0, concat_axis=0, tiled=True)  43.9 us
    all_to_all x7, starting transfers between devices, exchange(): return lax.all_to_all(rows, 'seq', split_axis=0, concat_axis=0, tiled=True)  32.9 us
  transfers between devices with their start and end apart: 8, of which 6 were waited for; matrix products, arithmetic and copies ran while one was open for 1% of the time, Pallas kernels for 22%

profile of v1, /device:TPU:0, one launch (start us, length us, event | category | flops | bytes accessed | tf_op | source)
XLA Modules:
  0.0 641.5 jit_solution(10601057571388741464)
XLA Ops:
  11.0 7.3 %all-to-all-start.3 = ((s32[32,1,12]{2,1,0:T(1,128)}), s32[32,1,12]{2,1,0:T(1,128)S(1)}, u32[]{:S(2)}, u32[]{:S(2)}) async-start(s32[32,1,12]{2,1,0:T(1,128)} %broadcast_select_fusion), calls=%async_computation.3 | async-start | bytes 32768 | tf_op jit(solution)/shard_map/all_to_all | solution.py:278
  18.3 9.8 %order_queries.1 = bf16[512,4608]{1,0:T(8,128)(2,1)} custom-call(bf16[4,3,128,1536]{3,2,1,0:T(8,128)(2,1)} %bitcast.35, bf16[128,128]{1,0:T(8,128)(2,1)} %constant.60.clone.order_ref), custom_call_target="tpu_custom_call" | custom-call | flops 603979776 | bytes 9437184 | tf_op jit(solution)/shard_map/order_queries/pallas_call | solution.py:52
  28.1 6.0 all-to-all-start.1
  36.5 179.6 %all-gather.2.cloned.1.call-done.w_ref = bf16[3072,3072]{1,0:T(8,128)(2,1)} async-done(((bf16[96,3072]{1,0:T(8,128)(2,1)}), bf16[3072,3072]{1,0:T(8,128)(2,1)}) %all-gather.2.cloned.1.call-update) | async-done | bytes 18874384 | tf_op jit(solution)/shard_map/all_gather | solution.py:292
  216.1 19.9 %project_2.1 = (bf16[4,128,3072]{2,1,0:T(8,128)(2,1)}, bf16[512,3072]{1,0:T(8,128)(2,1)}) custom-call(bf16[4,3,128,3072]{3,2,1,0:T(8,128)(2,1)} %bitcast.52, bf16[3072,3072]{1,0:T(8,128)(2,1)} %all-gather.2.cloned.1.call-done.w_ref, bf16[128,128]{1,0:T(8,128)(2,1)} %constant.60.clone.order_ref), custom_call_target="tpu_custom_call" | custom-call | flops 9663676416 | bytes 28311552 | tf_op jit(solution)/shard_map/project_2/pallas_call | solution.py:84
  235.9 16.9 %far_0.1 = bf16[512,1664]{1,0:T(8,128)(2,1)} custom-call(bf16[512,4608]{1,0:T(8,128)(2,1)} %bitcast.12.q_ref, bf16[4,128,3072]{2,1,0:T(8,128)(2,1)} %get-tuple-element.16.kv_ref, f32[3,128,128]{2,1,0:T(8,128)} %select_select_fusion.1.bias_ref, bf16[128,128]{1,0:T(8,128)(2,1)} %constant.62.clone.order_ref.refs_4_, bf16[128,128]{1,0:T(8,128)(2,1)} %constant.63.clone.back_ref), custom_call_target="tpu_custom_call" | custom-call | flops 402653184 | bytes 7864320 | tf_op jit(solution)/shard_map/far_0/pallas_call | solution.py:175
  252.8 43.9 %all_to_all.83 = bf16[32,16,1664]{2,1,0:T(8,128)(2,1)} all-to-all(bf16[32,16,1664]{2,1,0:T(8,128)(2,1)} %bitcast.46), channel_id=1, replica_groups=mesh['parts'=1,'seq'=32] {'seq'}, dimensions={0} | all-to-all | bytes 3407872 | tf_op jit(solution)/shard_map/all_to_all | solution.py:278
  296.7 3.3 all-to-all-start.5
  300.0 19.9 %project_1.1 = (bf16[4,128,3072]{2,1,0:T(8,128)(2,1)}, bf16[512,3072]{1,0:T(8,128)(2,1)}) custom-call(bf16[4,3,128,3072]{3,2,1,0:T(8,128)(2,1)} %bitcast.53, bf16[3072,3072]{1,0:T(8,128)(2,1)} %all-gather.2.cloned.1.call-done.w_ref, bf16[128,128]{1,0:T(8,128)(2,1)} %constant.60.clone.order_ref), custom_call_target="tpu_custom_call" | custom-call | flops 9663676416 | bytes 28311552 | tf_op jit(solution)/shard_map/project_1/pallas_call | solution.py:84
  319.9 51.4 %all-to-all-done.5 = bf16[32,16,3072]{2,1,0:T(8,128)(2,1)S(1)} async-done(((bf16[32,16,3072]{2,1,0:T(8,128)(2,1)}), bf16[32,16,3072]{2,1,0:T(8,128)(2,1)S(1)}, u32[]{:S(2)}, u32[]{:S(2)}) %all-to-all-start.5) | async-done | bytes 3145760 | tf_op jit(solution)/shard_map/all_to_all | solution.py:278
  373.0 4.0 all-to-all-start.2
  377.0 19.9 %project_0.1 = (bf16[4,128,3072]{2,1,0:T(8,128)(2,1)}, bf16[512,3072]{1,0:T(8,128)(2,1)}) custom-call(bf16[4,3,128,3072]{3,2,1,0:T(8,128)(2,1)} %bitcast.54, bf16[3072,3072]{1,0:T(8,128)(2,1)} %all-gather.2.cloned.1.call-done.w_ref, bf16[128,128]{1,0:T(8,128)(2,1)} %constant.60.clone.order_ref), custom_call_target="tpu_custom_call" | custom-call | flops 9663676416 | bytes 28311552 | tf_op jit(solution)/shard_map/project_0/pallas_call | solution.py:84
  396.9 51.5 %all-to-all-done.2 = bf16[32,16,3072]{2,1,0:T(8,128)(2,1)S(1)} async-done(((bf16[32,16,3072]{2,1,0:T(8,128)(2,1)}), bf16[32,16,3072]{2,1,0:T(8,128)(2,1)S(1)}, u32[]{:S(2)}, u32[]{:S(2)}) %all-to-all-start.2) | async-done | bytes 3145760 | tf_op jit(solution)/shard_map/all_to_all | solution.py:278
  450.0 4.0 all-to-all-start
  454.1 17.7 %far_1.1 = bf16[512,1664]{1,0:T(8,128)(2,1)} custom-call(bf16[512,4608]{1,0:T(8,128)(2,1)} %bitcast.12.q_ref, bf16[512,3072]{1,0:T(8,128)(2,1)} %bitcast.42, f32[3,128,128]{2,1,0:T(8,128)} %select_select_fusion.1.bias_ref, bf16[128,128]{1,0:T(8,128)(2,1)} %constant.62.clone.order_ref.refs_4_, bf16[128,128]{1,0:T(8,128)(2,1)} %constant.63.clone.back_ref), custom_call_target="tpu_custom_call" | custom-call | flops 402653184 | bytes 7864320 | tf_op jit(solution)/shard_map/far_1/pallas_call | solution.py:175
  471.8 53.6 %all-to-all-done = bf16[32,16,3072]{2,1,0:T(8,128)(2,1)S(1)} async-done(((bf16[32,16,3072]{2,1,0:T(8,128)(2,1)}), bf16[32,16,3072]{2,1,0:T(8,128)(2,1)S(1)}, u32[]{:S(2)}, u32[]{:S(2)}) %all-to-all-start) | async-done | bytes 3145760 | tf_op jit(solution)/shard_map/all_to_all | solution.py:278
  525.4 4.3 all-to-all-start.6
  529.7 17.7 %far_2.1 = bf16[512,1664]{1,0:T(8,128)(2,1)} custom-call(bf16[512,4608]{1,0:T(8,128)(2,1)} %bitcast.12.q_ref, bf16[512,3072]{1,0:T(8,128)(2,1)} %bitcast.41, f32[3,128,128]{2,1,0:T(8,128)} %select_select_fusion.1.bias_ref, bf16[128,128]{1,0:T(8,128)(2,1)} %constant.62.clone.order_ref.refs_4_, bf16[128,128]{1,0:T(8,128)(2,1)} %constant.63.clone.back_ref), custom_call_target="tpu_custom_call" | custom-call | flops 402653184 | bytes 7864320 | tf_op jit(solution)/shard_map/far_2/pallas_call | solution.py:175
  547.4 22.6 %all-to-all-done.6 = bf16[32,16,1664]{2,1,0:T(8,128)(2,1)} async-done(((bf16[32,16,1664]{2,1,0:T(8,128)(2,1)}), bf16[32,16,1664]{2,1,0:T(8,128)(2,1)}, u32[]{:S(2)}, u32[]{:S(2)}) %all-to-all-start.6) | async-done | bytes 1703968 | tf_op jit(solution)/shard_map/all_to_all | solution.py:278
  570.0 3.9 all-to-all-start.4
  575.3 18.4 %near_0.1.done_ref = bf16[4,3,128,1536]{3,2,1,0:T(8,128)(2,1)} custom-call(bf16[4,3,128,1536]{3,2,1,0:T(8,128)(2,1)} %bitcast.36, bf16[4,128,3072]{2,1,0:T(8,128)(2,1)} %get-tuple-element.15.refs_1_, f32[3,4,128,128]{3,2,1,0:T(8,128)} %select_select_fusion.refs_2_.bias_ref, bf16[512,1664]{1,0:T(8,128)(2,1)} %bitcast.47, ...), custom_call_target="tpu_custom_call" | custom-call | flops 402653184 | bytes 7864320 | tf_op jit(solution)/shard_map/near_0/pallas_call | solution.py:254
  593.7 18.4 %near_1.1.done_ref = bf16[4,3,128,1536]{3,2,1,0:T(8,128)(2,1)} custom-call(bf16[4,3,128,1536]{3,2,1,0:T(8,128)(2,1)} %bitcast.37, bf16[4,128,3072]{2,1,0:T(8,128)(2,1)} %get-tuple-element.13.kv_ref, f32[3,4,128,128]{3,2,1,0:T(8,128)} %select_select_fusion.refs_2_.bias_ref, bf16[512,1664]{1,0:T(8,128)(2,1)} %bitcast.21.far_ref, ...), custom_call_target="tpu_custom_call", output_to_operand_aliasing={{}: (6, {})} | custom-call | flops 402653184 | bytes 7864320 | tf_op jit(solution)/shard_map/near_1/pallas_call | solution.py:254
  612.1 2.1 all-to-all-done.4
  615.4 19.2 %near_2.1 = bf16[4,3,128,1536]{3,2,1,0:T(8,128)(2,1)} custom-call(bf16[4,3,128,1536]{3,2,1,0:T(8,128)(2,1)} %bitcast.38, bf16[512,3072]{1,0:T(8,128)(2,1)} %bitcast.40, f32[3,4,128,128]{3,2,1,0:T(8,128)} %select_select_fusion.refs_2_.bias_ref, bf16[512,1664]{1,0:T(8,128)(2,1)} %bitcast.44, ...), custom_call_target="tpu_custom_call", output_to_operand_aliasing={{}: (6, {})} | custom-call | flops 402653184 | bytes 7864320 | tf_op jit(solution)/shard_map/near_2/pallas_call | solution.py:254
  (31 shorter events, 12.7 us)
Async XLA Ops:
  6.5 209.5 %all-gather.2.cloned.1.call-start = ((), (), s32[]{:S(2)}) async-start(), calls=%async_computation.8 | async-start | bytes 19464192 | tf_op jit(solution)/shard_map/all_gather | solution.py:292
  11.0 17.2 %all-to-all-start.3 = ((s32[32,1,12]{2,1,0:T(1,128)}), s32[32,1,12]{2,1,0:T(1,128)S(1)}, u32[]{:S(2)}, u32[]{:S(2)}) async-start(s32[32,1,12]{2,1,0:T(1,128)} %broadcast_select_fusion), calls=%async_computation.3 | async-start | bytes 32768 | tf_op jit(solution)/shard_map/all_to_all | solution.py:278
  28.1 207.8 %all-to-all-start.1 = ((bf16[32,16,4608]{2,1,0:T(8,128)(2,1)}), bf16[32,16,4608]{2,1,0:T(8,128)(2,1)}, u32[]{:S(2)}, u32[]{:S(2)}) async-start(bf16[32,16,4608]{2,1,0:T(8,128)(2,1)} %bitcast.39), calls=%async_computation.1 | async-start | bytes 9437184 | tf_op jit(solution)/shard_map/all_to_all | solution.py:278
  296.7 74.7 %all-to-all-start.5 = ((bf16[32,16,3072]{2,1,0:T(8,128)(2,1)}), bf16[32,16,3072]{2,1,0:T(8,128)(2,1)S(1)}, u32[]{:S(2)}, u32[]{:S(2)}) async-start(bf16[32,16,3072]{2,1,0:T(8,128)(2,1)} %bitcast.48), calls=%async_computation.5 | async-start | bytes 6291456 | tf_op jit(solution)/shard_map/all_to_all | solution.py:278
  371.3 1.6 copy-start.2
  373.0 75.4 %all-to-all-start.2 = ((bf16[32,16,3072]{2,1,0:T(8,128)(2,1)}), bf16[32,16,3072]{2,1,0:T(8,128)(2,1)S(1)}, u32[]{:S(2)}, u32[]{:S(2)}) async-start(bf16[32,16,3072]{2,1,0:T(8,128)(2,1)} %bitcast.49), calls=%async_computation.2 | async-start | bytes 6291456 | tf_op jit(solution)/shard_map/all_to_all | solution.py:278
  448.4 1.7 copy-start.1
  450.0 75.4 %all-to-all-start = ((bf16[32,16,3072]{2,1,0:T(8,128)(2,1)}), bf16[32,16,3072]{2,1,0:T(8,128)(2,1)S(1)}, u32[]{:S(2)}, u32[]{:S(2)}) async-start(bf16[32,16,3072]{2,1,0:T(8,128)(2,1)} %bitcast.50), calls=%async_computation | async-start | bytes 6291456 | tf_op jit(solution)/shard_map/all_to_all | solution.py:278
  525.4 22.0 %copy-start = (bf16[32,16,3072]{2,1,0:T(8,128)(2,1)}, bf16[32,16,3072]{2,1,0:T(8,128)(2,1)S(1)}, u32[]{:S(2)}) copy-start(bf16[32,16,3072]{2,1,0:T(8,128)(2,1)S(1)} %all-to-all-done) | copy-start | bytes 9437188
  525.4 44.6 %all-to-all-start.6 = ((bf16[32,16,1664]{2,1,0:T(8,128)(2,1)}), bf16[32,16,1664]{2,1,0:T(8,128)(2,1)}, u32[]{:S(2)}, u32[]{:S(2)}) async-start(bf16[32,16,1664]{2,1,0:T(8,128)(2,1)} %bitcast.45), calls=%async_computation.6 | async-start | bytes 3407872 | tf_op jit(solution)/shard_map/all_to_all | solution.py:278
  570.0 44.2 %all-to-all-start.4 = ((bf16[32,16,1664]{2,1,0:T(8,128)(2,1)}), bf16[32,16,1664]{2,1,0:T(8,128)(2,1)S(1)}, u32[]{:S(2)}, u32[]{:S(2)}) async-start(bf16[32,16,1664]{2,1,0:T(8,128)(2,1)} %bitcast.43), calls=%async_computation.4 | async-start | bytes 3407872 | tf_op jit(solution)/shard_map/all_to_all | solution.py:278
  614.2 1.2 copy-start.3
Sparse Core Ops, SparseCore 0:
  10.2 205.7 all-gather.1

commit v2 on v1

v2 whole, which is shorter than its diff:
```python
import functools
import math

import jax
import jax.numpy as jnp
import numpy as np
from jax import lax
from jax.experimental import pallas as pl
from jax.experimental.pallas import tpu as pltpu
from jax.sharding import PartitionSpec as P

HEADS = 12
HDIM = 128
LANES = 128
PLANES = 3
SCALE = 1.0 / math.sqrt(HDIM)
BF16 = jnp.bfloat16
F32 = jnp.float32


def home_order(lines, res):
    span = res // lines
    out = np.zeros((res, res), np.float32)
    for line in range(lines):
        for dest in range(span // lines):
            for pos in range(lines):
                out[(dest * lines + pos) * lines + line, line * span + dest * lines + pos] = 1.0
    return out


def away_order(lines, res):
    span = res // lines
    out = np.zeros((res, res), np.float32)
    for src in range(span // lines):
        for pos in range(lines):
            for line in range(lines):
                out[pos * span + src * lines + line, (src * lines + pos) * lines + line] = 1.0
    return out


def pick(order, rows):
    return jnp.dot(order, rows, preferred_element_type=F32).astype(BF16)


def order_kernel(tokens_ref, queries_ref, order_ref, out_ref):
    lines, res, width = queries_ref.shape
    span = res // lines
    first = pl.program_id(0) < pl.num_programs(0) - PLANES

    def put(ref):
        for i in range(lines):
            rows = ref[:, pl.ds(i * span, span), :].reshape(res, width)
            out_ref[pl.ds(i * res, res), :] = pick(order_ref[...], rows)

    pl.when(first)(lambda: put(tokens_ref))
    pl.when(jnp.logical_not(first))(lambda: put(queries_ref))


def order_sent(tokens, queries, order):
    lines, planes, res, width = queries.shape
    depth = tokens.shape[-1]
    lead = depth // width
    return pl.pallas_call(
        order_kernel,
        grid=(lead + planes,),
        in_specs=[
            pl.BlockSpec((lines, None, res, width), lambda p: (0, 0, 0, jnp.minimum(p, lead - 1))),
            pl.BlockSpec((lines, None, res, width), lambda p: (0, jnp.maximum(p - lead, 0), 0, 0)),
            pl.BlockSpec((res, res), lambda p: (0, 0)),
        ],
        out_specs=pl.BlockSpec((lines * res, width), lambda p: (0, p)),
        out_shape=jax.ShapeDtypeStruct((lines * res, depth + planes * width), BF16),
        cost_estimate=pl.CostEstimate(
            flops=2 * lines * res * (depth + planes * width) * res,
            bytes_accessed=4 * lines * res * (depth + planes * width),
            transcendentals=0,
        ),
        name="order_sent",
    )(tokens, queries, order)


def project_kernel(x_ref, w_ref, order_ref, *out_refs):
    out = jnp.dot(x_ref[...].reshape(-1, x_ref.shape[-1]), w_ref[...], preferred_element_type=F32)
    out = out.astype(BF16)
    tile = w_ref.shape[1]
    home_ref = out_refs[0]
    home_ref[...] = out.reshape(home_ref.shape)
    if len(out_refs) > 1:
        lines, res, _ = x_ref.shape
        span = res // lines
        by_line = out.reshape(lines, res, tile)
        for i in range(lines):
            rows = by_line[:, i * span : (i + 1) * span].reshape(res, tile)
            out_refs[1][pl.ds(i * res, res), :] = pick(order_ref[...], rows)


def project(tokens, weight, order, plane, sent_width):
    depth, width = weight.shape
    tile = 512
    if tokens.ndim == 4:
        lines, planes, res, _ = tokens.shape
        x_spec = pl.BlockSpec((lines, None, res, depth), lambda n: (0, plane, 0, 0))
        rows = lines * res
        out_specs = [pl.BlockSpec((lines, res, tile), lambda n: (0, 0, n))]
        out_shape = [jax.ShapeDtypeStruct((lines, res, width), BF16)]
    else:
        rows = tokens.shape[0]
        x_spec = pl.BlockSpec((rows, depth), lambda n: (0, 0))
        out_specs = [pl.BlockSpec((rows, tile), lambda n: (0, n))]
        out_shape = [jax.ShapeDtypeStruct((rows, width), BF16)]
    if sent_width:
        out_specs.append(pl.BlockSpec((rows, tile), lambda n: (0, n)))
        out_shape.append(jax.ShapeDtypeStruct((rows, sent_width), BF16))
    return pl.pallas_call(
        project_kernel,
        grid=(width // tile,),
        in_specs=[
            x_spec,
            pl.BlockSpec((depth, tile), lambda n: (0, n)),
            pl.BlockSpec(order.shape, lambda n: (0, 0)),
        ],
        out_specs=out_specs,
        out_shape=out_shape,
        cost_estimate=pl.CostEstimate(
            flops=2 * rows * depth * width,
            bytes_accessed=2 * (rows * (depth + 2 * width) + depth * width),
            transcendentals=0,
        ),
        name=f"project_{plane}",
    )(tokens, weight, order)


def to_away(src_ref, order_ref, dst_ref):
    lines, res, width = dst_ref.shape
    span = res // lines
    for c in range(lines):
        rows = pick(order_ref[...], src_ref[pl.ds(c * res, res), :])
        for pos in range(lines):
            dst_ref[pos, pl.ds(c * span, span), :] = rows[pos * span : (pos + 1) * span]


def attend(q, k, v, bias):
    scores = lax.dot_general(q, k, (((1,), (1,)), ((), ())), preferred_element_type=F32)
    scores = scores * SCALE + bias
    peak = jnp.max(scores, axis=1, keepdims=True)
    weights = jnp.exp(scores - peak)
    total = jnp.sum(weights, axis=1, keepdims=True)
    out = jnp.dot(weights.astype(BF16), v, preferred_element_type=F32)
    return out, peak, total


def far_kernel(moved_kv, column, q_ref, kv_ref, bias_ref, order_ref, back_ref, *rest):
    out_ref, q_s, kv_s, mean_s, sent_s, sem = rest[-6:]
    lines, res, width = q_s.shape
    span = res // lines
    heads = width // HDIM
    to_away(q_ref, order_ref, q_s)
    if moved_kv:
        to_away(kv_ref, order_ref, kv_s)
    else:
        kv_s = kv_ref
    lane = lax.broadcasted_iota(jnp.int32, (res, LANES), 1)

    def step(i, carry):
        lse = jnp.zeros((res, LANES), F32)
        for h in range(heads):
            at = pl.ds(h * HDIM, HDIM)
            out, peak, total = attend(
                q_s[i, :, at], kv_s[i, :, at], kv_s[i, :, pl.ds(width + h * HDIM, HDIM)], bias_ref[...]
            )
            mean_s[i, :, at] = (out * (1.0 / total)).astype(BF16)
            lse = jnp.where(lane == h, peak + jnp.log(total), lse)
        high = lse.astype(BF16).astype(F32)
        mid = (lse - high).astype(BF16).astype(F32)
        low = (lse - high - mid).astype(BF16).astype(F32)
        parts = high + pltpu.roll(mid, 16, 1) + pltpu.roll(low, 32, 1)
        mean_s[i, :, pl.ds(width, LANES)] = parts.astype(BF16)
        return carry

    lax.fori_loop(0, lines, step, 0)
    for c in range(lines):
        rows = jnp.concatenate([mean_s[pos, pl.ds(c * span, span), :] for pos in range(lines)], axis=0)
        sent_s[pl.ds(c * res, res), :] = pick(back_ref[...], rows)
    copy = pltpu.make_async_copy(sent_s, out_ref.at[:, pl.ds(column, width + LANES)], sem)
    copy.start()
    copy.wait()


VMEM_SPEC = pl.BlockSpec(memory_space=pltpu.VMEM)


def attention_cost(lines, res, width):
    return pl.CostEstimate(
        flops=4 * lines * res * res * width,
        bytes_accessed=2 * lines * res * width * 5,
        transcendentals=lines * res * res * (width // HDIM),
    )


def far_attention(moved_q, kv, bias, order, back, plane, lead, lines, res, width, into=None):
    moved_kv = kv.ndim == 2
    kv_shape = (lines, res, 2 * width) if moved_kv else (1, 16, LANES)
    kv_block = kv.shape[:-1] + (2 * width,)
    column = 0 if into is None else into.shape[1] - width - LANES
    shape = (lines * res, column + width + LANES)
    in_specs = [
        pl.BlockSpec((lines * res, width), lambda n: (0, lead + plane)),
        pl.BlockSpec(kv_block, lambda n: (0,) * kv.ndim),
        pl.BlockSpec((None, res, res), lambda n: (plane, 0, 0)),
        pl.BlockSpec((res, res), lambda n: (0, 0)),
        pl.BlockSpec((res, res), lambda n: (0, 0)),
    ]
    args = (moved_q, kv, bias, order, back)
    if into is not None:
        in_specs.append(pl.BlockSpec(memory_space=pl.ANY))
        args = args + (into,)
    return pl.pallas_call(
        functools.partial(far_kernel, moved_kv, column),
        grid=(1,),
        in_specs=in_specs,
        out_specs=pl.BlockSpec(memory_space=pl.ANY),
        out_shape=jax.ShapeDtypeStruct(shape, BF16),
        scratch_shapes=[
            pltpu.VMEM((lines, res, width), BF16),
            pltpu.VMEM(kv_shape, BF16),
            pltpu.VMEM((lines, res, width + LANES), BF16),
            pltpu.VMEM((lines * res, width + LANES), BF16),
            pltpu.SemaphoreType.DMA,
        ],
        input_output_aliases={} if into is None else {5: 0},
        cost_estimate=attention_cost(lines, res, width),
        name=f"far_{plane}",
    )(*args)


def far_sum(parts):
    return parts + pltpu.roll(parts, LANES - 16, 1) + pltpu.roll(parts, LANES - 32, 1)


def near_kernel(column, q_ref, kv_ref, bias_ref, far_ref, back_ref, *rest):
    out_ref, far_s = rest[-2:]
    lines, res, width = q_ref.shape
    span = res // lines
    heads = width // HDIM
    for c in range(lines):
        rows = pick(back_ref[...], far_ref[pl.ds(c * res, res), pl.ds(column, width + LANES)])
        for line in range(lines):
            far_s[line, pl.ds(c * span, span), :] = rows[line * span : (line + 1) * span]

    def step(i, carry):
        lse = far_sum(far_s[i, :, pl.ds(width, LANES)].astype(F32))
        for h in range(heads):
            at = pl.ds(h * HDIM, HDIM)
            out, peak, total = attend(
                q_ref[i, :, at], kv_ref[i, :, at], kv_ref[i, :, pl.ds(width + h * HDIM, HDIM)], bias_ref[i]
            )
            far_lse = lse[:, h : h + 1]
            top = jnp.maximum(peak, far_lse)
            near_w = jnp.exp(peak - top)
            far_w = jnp.exp(far_lse - top)
            scale = 1.0 / (total * near_w + far_w)
            mixed = out * (near_w * scale) + far_s[i, :, at].astype(F32) * (far_w * scale)
            out_ref[i, :, at] = mixed.astype(BF16)
        return carry

    lax.fori_loop(0, lines, step, 0)


def near_attention(queries, kv, bias, far, back, plane, done):
    lines, planes, res, width = queries.shape
    in_specs = [
        pl.BlockSpec((lines, None, res, width), lambda n: (0, plane, 0, 0)),
        pl.BlockSpec(kv.shape, lambda n: (0,) * kv.ndim),
        pl.BlockSpec((None, lines, res, res), lambda n: (plane, 0, 0, 0)),
        pl.BlockSpec(far.shape, lambda n: (0, 0)),
        pl.BlockSpec((res, res), lambda n: (0, 0)),
    ]
    args = (queries, kv, bias, far, back)
    if done is not None:
        in_specs.append(pl.BlockSpec(memory_space=pl.ANY))
        args = args + (done,)
    return pl.pallas_call(
        functools.partial(near_kernel, far.shape[1] - width - LANES),
        grid=(1,),
        in_specs=in_specs,
        out_specs=pl.BlockSpec((lines, None, res, width), lambda n: (0, plane, 0, 0)),
        out_shape=jax.ShapeDtypeStruct(queries.shape, BF16),
        scratch_shapes=[pltpu.VMEM((lines, res, width + LANES), BF16)],
        input_output_aliases={} if done is None else {5: 0},
        cost_estimate=attention_cost(lines, res, width),
        name=f"near_{plane}",
    )(*args)


def part_kernel(q_ref, kv_ref, bias_ref, order_ref, mean_ref, lse_ref, kv_s):
    lines, res, width = q_ref.shape
    heads = width // HDIM
    to_away(kv_ref, order_ref, kv_s)
    lane = lax.broadcasted_iota(jnp.int32, (res, LANES), 1)

    def step(i, carry):
        lse = jnp.zeros((res, LANES), F32)
        for h in range(heads):
            at = pl.ds(h * HDIM, HDIM)
            out, peak, total = attend(
                q_ref[i, :, at], kv_s[i, :, at], kv_s[i, :, pl.ds(width + h * HDIM, HDIM)], bias_ref[i]
            )
            mean_ref[i, :, at] = out * (1.0 / total)
            lse = jnp.where(lane == h, peak + jnp.log(total), lse)
        lse_ref[i] = lse
        return carry

    lax.fori_loop(0, lines, step, 0)


def near_part(queries, kv, bias, order, plane):
    lines, planes, res, width = queries.shape
    return pl.pallas_call(
        part_kernel,
        grid=(1,),
        in_specs=[
            pl.BlockSpec((lines, None, res, width), lambda n: (0, plane, 0, 0)),
            pl.BlockSpec(kv.shape, lambda n: (0, 0)),
            pl.BlockSpec((None, lines, res, res), lambda n: (plane, 0, 0, 0)),
            pl.BlockSpec((res, res), lambda n: (0, 0)),
        ],
        out_specs=[
            pl.BlockSpec((lines, res, width), lambda n: (0, 0, 0)),
            pl.BlockSpec((lines, res, LANES), lambda n: (0, 0, 0)),
        ],
        out_shape=[
            jax.ShapeDtypeStruct((lines, res, width), F32),
            jax.ShapeDtypeStruct((lines, res, LANES), F32),
        ],
        scratch_shapes=[pltpu.VMEM((lines, res, 2 * width), BF16)],
        cost_estimate=attention_cost(lines, res, width),
        name=f"near_part_{plane}",
    )(queries, kv, bias, order)


def merge_kernel(far_ref, mean_ref, lse_ref, back_ref, done_ref, out_ref):
    lines, span, width = mean_ref.shape
    res = lines * span
    far = pick(back_ref[...], far_ref[...])
    far_lse = far_sum(far[:, width:].astype(F32))
    near_lse = lse_ref[...].reshape(res, LANES)
    top = jnp.maximum(near_lse, far_lse)
    near_w = jnp.exp(near_lse - top)
    far_w = jnp.exp(far_lse - top)
    scale = 1.0 / (near_w + far_w)
    near_w = near_w * scale
    far_w = far_w * scale
    for h in range(width // HDIM):
        at = pl.ds(h * HDIM, HDIM)
        near = mean_ref[:, :, at].reshape(res, HDIM)
        far_h = far[:, h * HDIM : (h + 1) * HDIM].astype(F32)
        mixed = near * near_w[:, h : h + 1] + far_h * far_w[:, h : h + 1]
        out_ref[:, :, at] = mixed.astype(BF16).reshape(lines, span, HDIM)


def merge_parts(far, mean, lse, back, plane, done):
    lines, planes, res, width = done.shape
    span = res // lines
    return pl.pallas_call(
        merge_kernel,
        grid=(lines,),
        in_specs=[
            pl.BlockSpec((res, width + LANES), lambda c: (c, 0)),
            pl.BlockSpec((lines, span, width), lambda c: (0, c, 0)),
            pl.BlockSpec((lines, span, LANES), lambda c: (0, c, 0)),
            pl.BlockSpec((res, res), lambda c: (0, 0)),
            pl.BlockSpec(memory_space=pl.ANY),
        ],
        out_specs=pl.BlockSpec((lines, None, span, width), lambda c: (0, plane, c, 0)),
        out_shape=jax.ShapeDtypeStruct(done.shape, BF16),
        input_output_aliases={4: 0},
        cost_estimate=pl.CostEstimate(
            flops=2 * lines * res * res * width, bytes_accessed=10 * lines * res * width, transcendentals=0
        ),
        name=f"merge_{plane}",
    )(far, mean, lse, back, done)


def mask_bias(codes, res):
    first_kept = (codes % 2 == 1)[..., None]
    second_kept = (codes >= 2)[..., None]
    kept = jnp.where(jnp.arange(res) < res // 2, first_kept, second_kept)
    return jnp.where(kept, 0.0, -jnp.inf).astype(F32)


def exchange(rows):
    return lax.all_to_all(rows, "seq", split_axis=0, concat_axis=0, tiled=True)


def on_device(count, tokens, queries, key_weight, value_weight, halves):
    scenes, lines, planes, res, depth = tokens.shape
    width = queries.shape[-1]
    tokens = tokens.reshape(lines, planes, res, depth)
    queries = queries.reshape(lines, planes, res, width)
    halves = halves.reshape(lines, planes, 2, 2)
    to_sent = jnp.asarray(home_order(lines, res), BF16)
    to_home = jnp.asarray(home_order(lines, res).T, BF16)
    away = jnp.asarray(away_order(lines, res), BF16)
    from_away = jnp.asarray(away_order(lines, res).T, BF16)

    weight = lax.all_gather(jnp.concatenate([key_weight, value_weight], axis=1), "seq", axis=0, tiled=True)

    dest_half = (np.arange(count) * lines) // (res // 2)
    sent_codes = jnp.where(
        (dest_half == 0)[:, None], halves[:, :, 0, 1].reshape(1, -1), halves[:, :, 1, 1].reshape(1, -1)
    )
    codes = exchange(sent_codes).reshape(res, planes).T
    far_bias = mask_bias(codes, res)
    home_half = jnp.arange(res) // (res // 2)
    near_codes = jnp.where(home_half == 0, halves[:, :, 0:1, 0], halves[:, :, 1:2, 0])
    near_bias = mask_bias(near_codes.transpose(1, 0, 2), res)

    moved = exchange(order_sent(tokens, queries, to_sent))
    far = functools.partial(
        far_attention, moved, bias=far_bias, order=away, back=from_away,
        lead=depth // width, lines=lines, res=res, width=width,
    )
    mean_width = width + LANES
    home_2, sent_2 = project(tokens, weight, to_sent, 2, 2 * width)
    moved_2 = exchange(sent_2)
    home_1, sent_1 = project(tokens, weight, to_sent, 1, 2 * width + mean_width)
    (moved_0,) = project(moved, weight, to_sent, 0, 0)
    sent_1, moved_0 = lax.optimization_barrier((sent_1, moved_0))
    moved_1 = exchange(far(kv=home_2, plane=0, into=sent_1))
    (home_0,) = project(tokens, weight, to_sent, 0, 0)
    mean_2, lse_2 = near_part(queries, moved_0, near_bias, away, 2)
    sent, home_0, mean_2, lse_2 = lax.optimization_barrier((far(kv=moved_2, plane=1), home_0, mean_2, lse_2))
    far_1 = exchange(sent)
    out = near_attention(queries, home_1, near_bias, moved_1, to_home, 0, None)
    sent, out = lax.optimization_barrier((far(kv=moved_1, plane=2), out))
    far_2 = exchange(sent)
    out = near_attention(queries, home_0, near_bias, far_1, to_home, 1, out)
    out = merge_parts(far_2, mean_2, lse_2, to_home, 2, out)
    return out.reshape(scenes, lines, planes, res, width)


def solution(mesh):
    in_specs = (
        P("parts", "seq", None, None, None),
        P("parts", "seq", None, None, None),
        P("seq", None),
        P("seq", None),
        P("parts", "seq", None, None, None),
    )
    return jax.shard_map(
        functools.partial(on_device, mesh.shape["seq"]),
        mesh=mesh,
        in_specs=in_specs,
        out_specs=P("parts", "seq", None, None, None),
        check_vma=False,
    )
```

time: 643 us -> 576 us (0.90)
  blocking collectives: 43.9 us -> 0 us
  waiting for transfers between devices: 361 us -> 337 us
    all_to_all x7 -> x6, waiting for transfers between devices: 181 us -> 115 us  [exchange(): return lax.all_to_all(rows, 'seq', split_axis=0, concat_axis=0, tiled=True)]
    all_to_all x1 -> x0, blocking collectives: 43.9 us -> none  [exchange(): return lax.all_to_all(rows, 'seq', split_axis=0, concat_axis=0, tiled=True)]
    all_gather x1, waiting for transfers between devices: 180 us -> 221 us  [on_device(): lax.all_gather(jnp.concatenate([key_weight, value_weight], axis=1), 'seq'...]
    pallas_call x10 -> x12, Pallas kernels: 178 us -> 184 us  [the longest x4 62.7 us: project(): pl.pallas_call(project_kernel, grid=(width // tile,), in_specs=[x_spec, p...]
    all_to_all x7 -> x6, starting transfers between devices: 32.9 us -> 29 us  [exchange(): return lax.all_to_all(rows, 'seq', split_axis=0, concat_axis=0, tiled=True)]
  transfers between devices with their start and end apart: 8 -> 7, of which waited for: 6 -> 6; matrix products, arithmetic and copies ran while one was open for 1% -> 1% of each run, Pallas kernels for 22% -> 31%
where the time goes in v2:
time: 576 us; the launch traced here: 574 us
  waiting for transfers between devices  337 us (59%)
  Pallas kernels  184 us (32%)
  starting transfers between devices  29 us (5%)
  between operations  13.5 us (2%)
  other arithmetic  6.2 us (1%)
    all_gather x1, waiting for transfers between devices, on_device(): lax.all_gather(jnp.concatenate([key_weight, value_weight], axis=1), 'seq'...  221 us
    all_to_all x6, waiting for transfers between devices, exchange(): return lax.all_to_all(rows, 'seq', split_axis=0, concat_axis=0, tiled=True)  115 us
    pallas_call x4, Pallas kernels, project(): pl.pallas_call(project_kernel, grid=(width // tile,), in_specs=[x_spec, p...  62.7 us
    pallas_call x3, Pallas kernels, far_attention(): pl.pallas_call(functools.partial(far_kernel, moved_kv, column), grid=(1,)...  52.4 us
    pallas_call x2, Pallas kernels, near_attention(): pl.pallas_call(functools.partial(near_kernel, far.shape[1] - width - LANE...  37.7 us
    all_to_all x6, starting transfers between devices, exchange(): return lax.all_to_all(rows, 'seq', split_axis=0, concat_axis=0, tiled=True)  29 us
    pallas_call x1, Pallas kernels, near_part(): pl.pallas_call(part_kernel, grid=(1,), in_specs=[pl.BlockSpec((lines, Non...  17 us
  transfers between devices with their start and end apart: 7, of which 6 were waited for; matrix products, arithmetic and copies ran while one was open for 1% of the time, Pallas kernels for 31%

profile of v2, /device:TPU:0, one launch (start us, length us, event | category | flops | bytes accessed | tf_op | source)
XLA Modules:
  0.0 574.4 jit_solution(8188536038202082647)
XLA Ops:
  11.0 7.3 %all-to-all-start.1 = ((s32[32,1,12]{2,1,0:T(1,128)}), s32[32,1,12]{2,1,0:T(1,128)S(1)}, u32[]{:S(2)}, u32[]{:S(2)}) async-start(s32[32,1,12]{2,1,0:T(1,128)} %broadcast_select_fusion), calls=%async_computation.1 | async-start | bytes 32768 | tf_op jit(solution)/shard_map/all_to_all | solution.py:392
  18.3 8.2 %order_sent.1 = bf16[512,7680]{1,0:T(8,128)(2,1)} custom-call(bf16[4,3,128,3072]{3,2,1,0:T(8,128)(2,1)} %bitcast.38, bf16[4,3,128,1536]{3,2,1,0:T(8,128)(2,1)} %bitcast.31, bf16[128,128]{1,0:T(8,128)(2,1)} %constant.60.clone.order_ref), custom_call_target="tpu_custom_call" | custom-call | flops 1006632960 | bytes 15728640 | tf_op jit(solution)/shard_map/order_sent/pallas_call | solution.py:63
  26.5 6.0 %all-to-all-start = ((bf16[32,16,7680]{2,1,0:T(8,128)(2,1)}), bf16[32,16,7680]{2,1,0:T(8,128)(2,1)}, u32[]{:S(2)}, u32[]{:S(2)}) async-start(bf16[32,16,7680]{2,1,0:T(8,128)(2,1)} %bitcast.35), calls=%async_computation | async-start | bytes 15728640 | tf_op jit(solution)/shard_map/all_to_all | solution.py:392
  32.4 221.5 %all-gather.2.cloned.1.call-done.w_ref = bf16[3072,3072]{1,0:T(8,128)(2,1)} async-done(((bf16[96,3072]{1,0:T(8,128)(2,1)}), bf16[3072,3072]{1,0:T(8,128)(2,1)}) %all-gather.2.cloned.1.call-update) | async-done | bytes 18874384 | tf_op jit(solution)/shard_map/all_gather | solution.py:406
  253.9 16.1 %project_2.1 = (bf16[4,128,3072]{2,1,0:T(8,128)(2,1)}, bf16[512,3072]{1,0:T(8,128)(2,1)}) custom-call(bf16[4,3,128,3072]{3,2,1,0:T(8,128)(2,1)} %bitcast.39, bf16[3072,3072]{1,0:T(8,128)(2,1)} %all-gather.2.cloned.1.call-done.w_ref, bf16[128,128]{1,0:T(8,128)(2,1)} %constant.60.clone.order_ref), custom_call_target="tpu_custom_call" | custom-call | flops 9663676416 | bytes 28311552 | tf_op jit(solution)/shard_map/project_2/pallas_call | solution.py:114
  270.0 13.1 %all-to-all-done = bf16[32,16,7680]{2,1,0:T(8,128)(2,1)} async-done(((bf16[32,16,7680]{2,1,0:T(8,128)(2,1)}), bf16[32,16,7680]{2,1,0:T(8,128)(2,1)}, u32[]{:S(2)}, u32[]{:S(2)}) %all-to-all-start) | async-done | bytes 7864352 | tf_op jit(solution)/shard_map/all_to_all | solution.py:392
  283.1 3.3 all-to-all-start.4
  288.7 16.1 %project_1.1 = (bf16[4,128,3072]{2,1,0:T(8,128)(2,1)}, bf16[512,4736]{1,0:T(8,128)(2,1)}) custom-call(bf16[4,3,128,3072]{3,2,1,0:T(8,128)(2,1)} %bitcast.40, bf16[3072,3072]{1,0:T(8,128)(2,1)} %all-gather.2.cloned.1.call-done.w_ref, bf16[128,128]{1,0:T(8,128)(2,1)} %constant.60.clone.order_ref), custom_call_target="tpu_custom_call" | custom-call | flops 9663676416 | bytes 28311552 | tf_op jit(solution)/shard_map/project_1/pallas_call | solution.py:114
  304.7 15.2 %project_0.2.kv_ref = bf16[512,3072]{1,0:T(8,128)(2,1)} custom-call(bf16[512,7680]{1,0:T(8,128)(2,1)} %bitcast.3.x_ref.q_ref, bf16[3072,3072]{1,0:T(8,128)(2,1)} %all-gather.2.cloned.1.call-done.w_ref, bf16[128,128]{1,0:T(8,128)(2,1)} %constant.60.clone.order_ref), custom_call_target="tpu_custom_call" | custom-call | flops 9663676416 | bytes 28311552 | tf_op jit(solution)/shard_map/project_0/pallas_call | solution.py:114
  320.0 16.9 %far_0.1 = bf16[512,4736]{1,0:T(8,128)(2,1)} custom-call(bf16[512,7680]{1,0:T(8,128)(2,1)} %bitcast.3.x_ref.q_ref, bf16[4,128,3072]{2,1,0:T(8,128)(2,1)} %get-tuple-element.19.kv_ref, f32[3,128,128]{2,1,0:T(8,128)} %select_select_fusion.1.bias_ref, bf16[128,128]{1,0:T(8,128)(2,1)} %constant.62.clone.order_ref, ...), custom_call_target="tpu_custom_call", output_to_operand_aliasing={{}: (5, {})} | custom-call | flops 402653184 | bytes 7864320 | tf_op jit(solution)/shard_map/far_0/pallas_call | solution.py:217
  336.9 20.8 %all-to-all-done.4 = bf16[32,16,3072]{2,1,0:T(8,128)(2,1)S(1)} async-done(((bf16[32,16,3072]{2,1,0:T(8,128)(2,1)}), bf16[32,16,3072]{2,1,0:T(8,128)(2,1)S(1)}, u32[]{:S(2)}, u32[]{:S(2)}) %all-to-all-start.4) | async-done | bytes 3145760 | tf_op jit(solution)/shard_map/all_to_all | solution.py:392
  359.4 4.3 all-to-all-start.2
  365.1 17.0 %near_part_2.1 = (f32[4,128,1536]{2,1,0:T(8,128)}, f32[4,128,128]{2,1,0:T(8,128)}) custom-call(bf16[4,3,128,1536]{3,2,1,0:T(8,128)(2,1)} %bitcast.32, bf16[512,3072]{1,0:T(8,128)(2,1)} %project_0.2.kv_ref, f32[3,4,128,128]{3,2,1,0:T(8,128)} %select_select_fusion.bias_ref, bf16[128,128]{1,0:T(8,128)(2,1)} %constant.62.clone.order_ref), custom_call_target="tpu_custom_call" | custom-call | flops 402653184 | bytes 7864320 | tf_op jit(solution)/shard_map/near_part_2/pallas_call | solution.py:318
  382.1 15.3 %project_0.3.kv_ref = bf16[4,128,3072]{2,1,0:T(8,128)(2,1)} custom-call(bf16[4,3,128,3072]{3,2,1,0:T(8,128)(2,1)} %bitcast.41, bf16[3072,3072]{1,0:T(8,128)(2,1)} %all-gather.2.cloned.1.call-done.w_ref, bf16[128,128]{1,0:T(8,128)(2,1)} %constant.60.clone.order_ref), custom_call_target="tpu_custom_call" | custom-call | flops 9663676416 | bytes 28311552 | tf_op jit(solution)/shard_map/project_0/pallas_call | solution.py:114
  397.4 17.8 %far_1.1 = bf16[512,1664]{1,0:T(8,128)(2,1)} custom-call(bf16[512,7680]{1,0:T(8,128)(2,1)} %bitcast.3.x_ref.q_ref, bf16[512,3072]{1,0:T(8,128)(2,1)} %bitcast.37, f32[3,128,128]{2,1,0:T(8,128)} %select_select_fusion.1.bias_ref, bf16[128,128]{1,0:T(8,128)(2,1)} %constant.62.clone.order_ref, bf16[128,128]{1,0:T(8,128)(2,1)} %constant.63.clone.back_ref), custom_call_target="tpu_custom_call" | custom-call | flops 402653184 | bytes 7864320 | tf_op jit(solution)/shard_map/far_1/pallas_call | solution.py:217
  415.2 56.4 %all-to-all-done.2 = bf16[32,16,4736]{2,1,0:T(8,128)(2,1)} async-done(((bf16[32,16,4736]{2,1,0:T(8,128)(2,1)}), bf16[32,16,4736]{2,1,0:T(8,128)(2,1)}, u32[]{:S(2)}, u32[]{:S(2)}) %all-to-all-start.2) | async-done | bytes 4849696 | tf_op jit(solution)/shard_map/all_to_all | solution.py:392
  471.5 3.8 all-to-all-start.5
  475.4 17.7 %far_2.1 = bf16[512,1664]{1,0:T(8,128)(2,1)} custom-call(bf16[512,7680]{1,0:T(8,128)(2,1)} %bitcast.3.x_ref.q_ref, bf16[512,4736]{1,0:T(8,128)(2,1)} %bitcast.7.kv_ref.far_ref, f32[3,128,128]{2,1,0:T(8,128)} %select_select_fusion.1.bias_ref, bf16[128,128]{1,0:T(8,128)(2,1)} %constant.62.clone.order_ref, bf16[128,128]{1,0:T(8,128)(2,1)} %constant.63.clone.back_ref), custom_call_target="tpu_custom_call" | custom-call | flops 402653184 | bytes 7864320 | tf_op jit(solution)/shard_map/far_2/pallas_call | solution.py:217
  493.1 19.3 %near_0.1.rest_0_ = bf16[4,3,128,1536]{3,2,1,0:T(8,128)(2,1)} custom-call(bf16[4,3,128,1536]{3,2,1,0:T(8,128)(2,1)} %bitcast.33, bf16[4,128,3072]{2,1,0:T(8,128)(2,1)} %get-tuple-element.22.kv_ref, f32[3,4,128,128]{3,2,1,0:T(8,128)} %select_select_fusion.bias_ref, bf16[512,4736]{1,0:T(8,128)(2,1)} %bitcast.7.kv_ref.far_ref, ...), custom_call_target="tpu_custom_call" | custom-call | flops 402653184 | bytes 7864320 | tf_op jit(solution)/shard_map/near_0/pallas_call | solution.py:282
  512.4 3.3 all-to-all-done.5
  515.7 4.2 all-to-all-start.3
  520.0 18.4 %near_1.1.done_ref = bf16[4,3,128,1536]{3,2,1,0:T(8,128)(2,1)} custom-call(bf16[4,3,128,1536]{3,2,1,0:T(8,128)(2,1)} %bitcast.34, bf16[4,128,3072]{2,1,0:T(8,128)(2,1)} %project_0.3.kv_ref, f32[3,4,128,128]{3,2,1,0:T(8,128)} %select_select_fusion.bias_ref, bf16[512,1664]{1,0:T(8,128)(2,1)} %bitcast.42, ...), custom_call_target="tpu_custom_call", output_to_operand_aliasing={{}: (5, {})} | custom-call | flops 402653184 | bytes 7864320 | tf_op jit(solution)/shard_map/near_1/pallas_call | solution.py:282
  538.4 21.9 %all-to-all-done.3 = bf16[32,16,1664]{2,1,0:T(8,128)(2,1)S(1)} async-done(((bf16[32,16,1664]{2,1,0:T(8,128)(2,1)}), bf16[32,16,1664]{2,1,0:T(8,128)(2,1)S(1)}, u32[]{:S(2)}, u32[]{:S(2)}) %all-to-all-start.3) | async-done | bytes 1703968 | tf_op jit(solution)/shard_map/all_to_all | solution.py:392
  561.5 6.1 %merge_2.1 = bf16[4,3,128,1536]{3,2,1,0:T(8,128)(2,1)} custom-call(bf16[512,1664]{1,0:T(8,128)(2,1)} %bitcast.44, f32[4,128,1536]{2,1,0:T(8,128)} %get-tuple-element.28.mean_ref, f32[4,128,128]{2,1,0:T(8,128)} %get-tuple-element.29.lse_ref, bf16[128,128]{1,0:T(8,128)(2,1)} %constant.61.clone.back_ref, ...), custom_call_target="tpu_custom_call", output_to_operand_aliasing={{}: (4, {})} | custom-call | flops 201326592 | bytes 7864320 | tf_op jit(solution)/shard_map/merge_2/pallas_call | solution.py:364
  (28 shorter events, 11.0 us)
Async XLA Ops:
  6.5 247.4 %all-gather.2.cloned.1.call-start = ((), (), s32[]{:S(2)}) async-start(), calls=%async_computation.6 | async-start | bytes 19464192 | tf_op jit(solution)/shard_map/all_gather | solution.py:406
  11.0 15.5 %all-to-all-start.1 = ((s32[32,1,12]{2,1,0:T(1,128)}), s32[32,1,12]{2,1,0:T(1,128)S(1)}, u32[]{:S(2)}, u32[]{:S(2)}) async-start(s32[32,1,12]{2,1,0:T(1,128)} %broadcast_select_fusion), calls=%async_computation.1 | async-start | bytes 32768 | tf_op jit(solution)/shard_map/all_to_all | solution.py:392
  26.5 256.6 %all-to-all-start = ((bf16[32,16,7680]{2,1,0:T(8,128)(2,1)}), bf16[32,16,7680]{2,1,0:T(8,128)(2,1)}, u32[]{:S(2)}, u32[]{:S(2)}) async-start(bf16[32,16,7680]{2,1,0:T(8,128)(2,1)} %bitcast.35), calls=%async_computation | async-start | bytes 15728640 | tf_op jit(solution)/shard_map/all_to_all | solution.py:392
  283.1 74.7 %all-to-all-start.4 = ((bf16[32,16,3072]{2,1,0:T(8,128)(2,1)}), bf16[32,16,3072]{2,1,0:T(8,128)(2,1)S(1)}, u32[]{:S(2)}, u32[]{:S(2)}) async-start(bf16[32,16,3072]{2,1,0:T(8,128)(2,1)} %bitcast.45), calls=%async_computation.4 | async-start | bytes 6291456 | tf_op jit(solution)/shard_map/all_to_all | solution.py:392
  357.7 1.7 copy-start
  359.4 112.2 %all-to-all-start.2 = ((bf16[32,16,4736]{2,1,0:T(8,128)(2,1)}), bf16[32,16,4736]{2,1,0:T(8,128)(2,1)}, u32[]{:S(2)}, u32[]{:S(2)}) async-start(bf16[32,16,4736]{2,1,0:T(8,128)(2,1)} %bitcast.36), calls=%async_computation.2 | async-start | bytes 9699328 | tf_op jit(solution)/shard_map/all_to_all | solution.py:392
  471.5 44.2 %all-to-all-start.5 = ((bf16[32,16,1664]{2,1,0:T(8,128)(2,1)}), bf16[32,16,1664]{2,1,0:T(8,128)(2,1)S(1)}, u32[]{:S(2)}, u32[]{:S(2)}) async-start(bf16[32,16,1664]{2,1,0:T(8,128)(2,1)} %bitcast.43), calls=%async_computation.5 | async-start | bytes 3407872 | tf_op jit(solution)/shard_map/all_to_all | solution.py:392
  515.7 4.3 copy-start.1
  515.7 44.5 %all-to-all-start.3 = ((bf16[32,16,1664]{2,1,0:T(8,128)(2,1)}), bf16[32,16,1664]{2,1,0:T(8,128)(2,1)S(1)}, u32[]{:S(2)}, u32[]{:S(2)}) async-start(bf16[32,16,1664]{2,1,0:T(8,128)(2,1)} %bitcast.14), calls=%async_computation.3 | async-start | bytes 3407872 | tf_op jit(solution)/shard_map/all_to_all | solution.py:392
  560.2 1.2 copy-start.2
Sparse Core Ops, SparseCore 0:
  10.2 243.6 all-gather.1

commit v3 on v2

--- a/solution.py
+++ b/solution.py
@@ -392,6 +392,19 @@
     return lax.all_to_all(rows, "seq", split_axis=0, concat_axis=0, tiled=True)
 
 
+def gather_weight(shard, count, sent, codes):
+    outer = 1
+    while outer * outer < count // 2:
+        outer *= 2
+    inner = count // outer
+    across = [[o * inner + i for o in range(outer)] for i in range(inner)]
+    within = [[o * inner + i for i in range(inner)] for o in range(outer)]
+    blocks = lax.all_gather(shard[None], "seq", axis=0, tiled=True, axis_index_groups=across)
+    blocks, sent, codes = lax.optimization_barrier((blocks, sent, codes))
+    blocks = lax.all_gather(blocks, "seq", axis=1, tiled=True, axis_index_groups=within)
+    return blocks.reshape(-1, shard.shape[-1]), sent, codes
+
+
 def on_device(count, tokens, queries, key_weight, value_weight, halves):
     scenes, lines, planes, res, depth = tokens.shape
     width = queries.shape[-1]
@@ -403,19 +416,20 @@
     away = jnp.asarray(away_order(lines, res), BF16)
     from_away = jnp.asarray(away_order(lines, res).T, BF16)
 
-    weight = lax.all_gather(jnp.concatenate([key_weight, value_weight], axis=1), "seq", axis=0, tiled=True)
-
     dest_half = (np.arange(count) * lines) // (res // 2)
     sent_codes = jnp.where(
         (dest_half == 0)[:, None], halves[:, :, 0, 1].reshape(1, -1), halves[:, :, 1, 1].reshape(1, -1)
     )
-    codes = exchange(sent_codes).reshape(res, planes).T
+    codes = exchange(sent_codes)
+    sent = order_sent(tokens, queries, to_sent)
+    weight, sent, codes = gather_weight(jnp.concatenate([key_weight, value_weight], axis=1), count, sent, codes)
+    codes = codes.reshape(res, planes).T
     far_bias = mask_bias(codes, res)
     home_half = jnp.arange(res) // (res // 2)
     near_codes = jnp.where(home_half == 0, halves[:, :, 0:1, 0], halves[:, :, 1:2, 0])
     near_bias = mask_bias(near_codes.transpose(1, 0, 2), res)
 
-    moved = exchange(order_sent(tokens, queries, to_sent))
+    moved = exchange(sent)
     far = functools.partial(
         far_attention, moved, bias=far_bias, order=away, back=from_away,
         lead=depth // width, lines=lines, res=res, width=width,

time: 576 us -> 554 us (0.962)
  waiting for transfers between devices: 337 us -> 315 us
    all_to_all x6, waiting for transfers between devices: 115 us -> 104 us  [exchange(): return lax.all_to_all(rows, 'seq', split_axis=0, concat_axis=0, tiled=True)]
    all_gather x1 -> x2, waiting for transfers between devices: 221 us -> 212 us  [the longest x1 177 us: gather_weight(): lax.all_gather(blocks, 'seq', axis=1, tiled=True, axis_index_groups=within)]
  transfers between devices with their start and end apart: 7 -> 8, of which waited for: 6 -> 6; matrix products, arithmetic and copies ran while one was open for 1% -> 1% of each run, Pallas kernels for 31% -> 32%
where the time goes in v3:
time: 554 us; the launch traced here: 552 us
  waiting for transfers between devices  315 us (57%)
  Pallas kernels  184 us (33%)
  starting transfers between devices  29.7 us (5%)
  between operations  13.5 us (2%)
  other arithmetic  5.64 us (1%)
    all_gather x1, waiting for transfers between devices, gather_weight(): lax.all_gather(blocks, 'seq', axis=1, tiled=True, axis_index_groups=within)  177 us
    all_to_all x6, waiting for transfers between devices, exchange(): return lax.all_to_all(rows, 'seq', split_axis=0, concat_axis=0, tiled=True)  104 us
    pallas_call x4, Pallas kernels, project(): pl.pallas_call(project_kernel, grid=(width // tile,), in_specs=[x_spec, p...  62.5 us
    pallas_call x3, Pallas kernels, far_attention(): pl.pallas_call(functools.partial(far_kernel, moved_kv, column), grid=(1,)...  52.3 us
    pallas_call x2, Pallas kernels, near_attention(): pl.pallas_call(functools.partial(near_kernel, far.shape[1] - width - LANE...  37.7 us
    all_gather x1, waiting for transfers between devices, gather_weight(): lax.all_gather(shard[None], 'seq', axis=0, tiled=True, axis_index_groups=...  35.1 us
    all_to_all x6, starting transfers between devices, exchange(): return lax.all_to_all(rows, 'seq', split_axis=0, concat_axis=0, tiled=True)  29.6 us
    pallas_call x1, Pallas kernels, near_part(): pl.pallas_call(part_kernel, grid=(1,), in_specs=[pl.BlockSpec((lines, Non...  17 us
  transfers between devices with their start and end apart: 8, of which 6 were waited for; matrix products, arithmetic and copies ran while one was open for 1% of the time, Pallas kernels for 32%

profile of v3, /device:TPU:0, one launch (start us, length us, event | category | flops | bytes accessed | tf_op | source)
XLA Modules:
  0.0 552.5 jit_solution(14111654766860570828)
XLA Ops:
  11.0 7.3 %all-to-all-start = ((s32[32,1,12]{2,1,0:T(1,128)}), s32[32,1,12]{2,1,0:T(1,128)S(1)}, u32[]{:S(2)}, u32[]{:S(2)}) async-start(s32[32,1,12]{2,1,0:T(1,128)} %broadcast_select_fusion), calls=%async_computation | async-start | bytes 32768 | tf_op jit(solution)/shard_map/all_to_all | solution.py:392
  18.3 8.3 %order_sent.1 = bf16[512,7680]{1,0:T(8,128)(2,1)} custom-call(bf16[4,3,128,3072]{3,2,1,0:T(8,128)(2,1)} %bitcast.41, bf16[4,3,128,1536]{3,2,1,0:T(8,128)(2,1)} %bitcast.34, bf16[128,128]{1,0:T(8,128)(2,1)} %constant.60.clone.order_ref), custom_call_target="tpu_custom_call" | custom-call | flops 1006632960 | bytes 15728640 | tf_op jit(solution)/shard_map/order_sent/pallas_call | solution.py:63
  26.6 35.1 %all-gather.6.cloned.1.call-done = bf16[384,3072]{1,0:T(8,128)(2,1)} async-done(((bf16[96,3072]{1,0:T(8,128)(2,1)}), bf16[384,3072]{1,0:T(8,128)(2,1)}) %all-gather.6.cloned.1.call-update) | async-done | bytes 2359312 | tf_op jit(solution)/shard_map/all_gather | solution.py:402
  61.8 3.7 all-to-all-start.1
  65.4 176.7 %all-gather.4.cloned.1.call-done = bf16[4,768,3072]{2,1,0:T(8,128)(2,1)} async-done(((bf16[4,96,3072]{2,1,0:T(8,128)(2,1)}), bf16[4,768,3072]{2,1,0:T(8,128)(2,1)}) %all-gather.4.cloned.1.call-update) | async-done | bytes 18874384 | tf_op jit(solution)/shard_map/all_gather | solution.py:404
  242.1 16.1 %project_2.1 = (bf16[4,128,3072]{2,1,0:T(8,128)(2,1)}, bf16[512,3072]{1,0:T(8,128)(2,1)}) custom-call(bf16[4,3,128,3072]{3,2,1,0:T(8,128)(2,1)} %bitcast.42, bf16[3072,3072]{1,0:T(8,128)(2,1)} %bitcast.52, bf16[128,128]{1,0:T(8,128)(2,1)} %constant.60.clone.order_ref), custom_call_target="tpu_custom_call" | custom-call | flops 9663676416 | bytes 28311552 | tf_op jit(solution)/shard_map/project_2/pallas_call | solution.py:114
  258.2 6.2 %all-to-all-start.4 = ((bf16[32,16,3072]{2,1,0:T(8,128)(2,1)}), bf16[32,16,3072]{2,1,0:T(8,128)(2,1)S(1)}, u32[]{:S(2)}, u32[]{:S(2)}) async-start(bf16[32,16,3072]{2,1,0:T(8,128)(2,1)} %bitcast.48), calls=%async_computation.4 | async-start | bytes 6291456 | tf_op jit(solution)/shard_map/all_to_all | solution.py:392
  265.6 16.1 %project_1.1 = (bf16[4,128,3072]{2,1,0:T(8,128)(2,1)}, bf16[512,4736]{1,0:T(8,128)(2,1)}) custom-call(bf16[4,3,128,3072]{3,2,1,0:T(8,128)(2,1)} %bitcast.43, bf16[3072,3072]{1,0:T(8,128)(2,1)} %bitcast.53, bf16[128,128]{1,0:T(8,128)(2,1)} %constant.60.clone.order_ref), custom_call_target="tpu_custom_call" | custom-call | flops 9663676416 | bytes 28311552 | tf_op jit(solution)/shard_map/project_1/pallas_call | solution.py:114
  281.7 15.2 %project_0.2.kv_ref = bf16[512,3072]{1,0:T(8,128)(2,1)} custom-call(bf16[512,7680]{1,0:T(8,128)(2,1)} %bitcast.6.x_ref.q_ref, bf16[3072,3072]{1,0:T(8,128)(2,1)} %bitcast.54, bf16[128,128]{1,0:T(8,128)(2,1)} %constant.60.clone.order_ref), custom_call_target="tpu_custom_call" | custom-call | flops 9663676416 | bytes 28311552 | tf_op jit(solution)/shard_map/project_0/pallas_call | solution.py:114
  296.9 16.9 %far_0.1 = bf16[512,4736]{1,0:T(8,128)(2,1)} custom-call(bf16[512,7680]{1,0:T(8,128)(2,1)} %bitcast.6.x_ref.q_ref, bf16[4,128,3072]{2,1,0:T(8,128)(2,1)} %get-tuple-element.24.kv_ref, f32[3,128,128]{2,1,0:T(8,128)} %select_select_fusion.1.bias_ref, bf16[128,128]{1,0:T(8,128)(2,1)} %constant.62.clone.order_ref, ...), custom_call_target="tpu_custom_call", output_to_operand_aliasing={{}: (5, {})} | custom-call | flops 402653184 | bytes 7864320 | tf_op jit(solution)/shard_map/far_0/pallas_call | solution.py:217
  313.8 22.0 %all-to-all-done.4 = bf16[32,16,3072]{2,1,0:T(8,128)(2,1)S(1)} async-done(((bf16[32,16,3072]{2,1,0:T(8,128)(2,1)}), bf16[32,16,3072]{2,1,0:T(8,128)(2,1)S(1)}, u32[]{:S(2)}, u32[]{:S(2)}) %all-to-all-start.4) | async-done | bytes 3145760 | tf_op jit(solution)/shard_map/all_to_all | solution.py:392
  337.4 4.3 all-to-all-start.2
  343.2 17.0 %near_part_2.1 = (f32[4,128,1536]{2,1,0:T(8,128)}, f32[4,128,128]{2,1,0:T(8,128)}) custom-call(bf16[4,3,128,1536]{3,2,1,0:T(8,128)(2,1)} %bitcast.35, bf16[512,3072]{1,0:T(8,128)(2,1)} %project_0.2.kv_ref, f32[3,4,128,128]{3,2,1,0:T(8,128)} %select_select_fusion.bias_ref, bf16[128,128]{1,0:T(8,128)(2,1)} %constant.62.clone.order_ref), custom_call_target="tpu_custom_call" | custom-call | flops 402653184 | bytes 7864320 | tf_op jit(solution)/shard_map/near_part_2/pallas_call | solution.py:318
  360.2 15.2 %project_0.3.kv_ref = bf16[4,128,3072]{2,1,0:T(8,128)(2,1)} custom-call(bf16[4,3,128,3072]{3,2,1,0:T(8,128)(2,1)} %bitcast.44, bf16[3072,3072]{1,0:T(8,128)(2,1)} %bitcast.55, bf16[128,128]{1,0:T(8,128)(2,1)} %constant.60.clone.order_ref), custom_call_target="tpu_custom_call" | custom-call | flops 9663676416 | bytes 28311552 | tf_op jit(solution)/shard_map/project_0/pallas_call | solution.py:114
  375.4 17.7 %far_1.1 = bf16[512,1664]{1,0:T(8,128)(2,1)} custom-call(bf16[512,7680]{1,0:T(8,128)(2,1)} %bitcast.6.x_ref.q_ref, bf16[512,3072]{1,0:T(8,128)(2,1)} %bitcast.40, f32[3,128,128]{2,1,0:T(8,128)} %select_select_fusion.1.bias_ref, bf16[128,128]{1,0:T(8,128)(2,1)} %constant.62.clone.order_ref, bf16[128,128]{1,0:T(8,128)(2,1)} %constant.63.clone.back_ref), custom_call_target="tpu_custom_call" | custom-call | flops 402653184 | bytes 7864320 | tf_op jit(solution)/shard_map/far_1/pallas_call | solution.py:217
  393.2 56.4 %all-to-all-done.2 = bf16[32,16,4736]{2,1,0:T(8,128)(2,1)} async-done(((bf16[32,16,4736]{2,1,0:T(8,128)(2,1)}), bf16[32,16,4736]{2,1,0:T(8,128)(2,1)}, u32[]{:S(2)}, u32[]{:S(2)}) %all-to-all-start.2) | async-done | bytes 4849696 | tf_op jit(solution)/shard_map/all_to_all | solution.py:392
  449.6 3.8 all-to-all-start.5
  453.4 17.7 %far_2.1 = bf16[512,1664]{1,0:T(8,128)(2,1)} custom-call(bf16[512,7680]{1,0:T(8,128)(2,1)} %bitcast.6.x_ref.q_ref, bf16[512,4736]{1,0:T(8,128)(2,1)} %bitcast.10.kv_ref.far_ref, f32[3,128,128]{2,1,0:T(8,128)} %select_select_fusion.1.bias_ref, bf16[128,128]{1,0:T(8,128)(2,1)} %constant.62.clone.order_ref, bf16[128,128]{1,0:T(8,128)(2,1)} %constant.63.clone.back_ref), custom_call_target="tpu_custom_call" | custom-call | flops 402653184 | bytes 7864320 | tf_op jit(solution)/shard_map/far_2/pallas_call | solution.py:217
  471.1 19.3 %near_0.1.rest_0_ = bf16[4,3,128,1536]{3,2,1,0:T(8,128)(2,1)} custom-call(bf16[4,3,128,1536]{3,2,1,0:T(8,128)(2,1)} %bitcast.36, bf16[4,128,3072]{2,1,0:T(8,128)(2,1)} %get-tuple-element.28.kv_ref, f32[3,4,128,128]{3,2,1,0:T(8,128)} %select_select_fusion.bias_ref, bf16[512,4736]{1,0:T(8,128)(2,1)} %bitcast.10.kv_ref.far_ref, ...), custom_call_target="tpu_custom_call" | custom-call | flops 402653184 | bytes 7864320 | tf_op jit(solution)/shard_map/near_0/pallas_call | solution.py:282
  490.5 3.3 all-to-all-done.5
  493.7 4.2 all-to-all-start.3
  498.0 18.4 %near_1.1.done_ref = bf16[4,3,128,1536]{3,2,1,0:T(8,128)(2,1)} custom-call(bf16[4,3,128,1536]{3,2,1,0:T(8,128)(2,1)} %bitcast.37, bf16[4,128,3072]{2,1,0:T(8,128)(2,1)} %project_0.3.kv_ref, f32[3,4,128,128]{3,2,1,0:T(8,128)} %select_select_fusion.bias_ref, bf16[512,1664]{1,0:T(8,128)(2,1)} %bitcast.45, ...), custom_call_target="tpu_custom_call", output_to_operand_aliasing={{}: (5, {})} | custom-call | flops 402653184 | bytes 7864320 | tf_op jit(solution)/shard_map/near_1/pallas_call | solution.py:282
  516.4 21.9 %all-to-all-done.3 = bf16[32,16,1664]{2,1,0:T(8,128)(2,1)S(1)} async-done(((bf16[32,16,1664]{2,1,0:T(8,128)(2,1)}), bf16[32,16,1664]{2,1,0:T(8,128)(2,1)S(1)}, u32[]{:S(2)}, u32[]{:S(2)}) %all-to-all-start.3) | async-done | bytes 1703968 | tf_op jit(solution)/shard_map/all_to_all | solution.py:392
  539.5 6.1 %merge_2.1 = bf16[4,3,128,1536]{3,2,1,0:T(8,128)(2,1)} custom-call(bf16[512,1664]{1,0:T(8,128)(2,1)} %bitcast.47, f32[4,128,1536]{2,1,0:T(8,128)} %get-tuple-element.34.mean_ref, f32[4,128,128]{2,1,0:T(8,128)} %get-tuple-element.35.lse_ref, bf16[128,128]{1,0:T(8,128)(2,1)} %constant.61.clone.back_ref, ...), custom_call_target="tpu_custom_call", output_to_operand_aliasing={{}: (4, {})} | custom-call | flops 201326592 | bytes 7864320 | tf_op jit(solution)/shard_map/merge_2/pallas_call | solution.py:364
  (29 shorter events, 10.0 us)
Async XLA Ops:
  6.5 55.2 %all-gather.6.cloned.1.call-start = ((), (), s32[]{:S(2)}) async-start(), calls=%async_computation.7 | async-start | bytes 2949120 | tf_op jit(solution)/shard_map/all_gather | solution.py:402
  11.0 15.6 %all-to-all-start = ((s32[32,1,12]{2,1,0:T(1,128)}), s32[32,1,12]{2,1,0:T(1,128)S(1)}, u32[]{:S(2)}, u32[]{:S(2)}) async-start(s32[32,1,12]{2,1,0:T(1,128)} %broadcast_select_fusion), calls=%async_computation | async-start | bytes 32768 | tf_op jit(solution)/shard_map/all_to_all | solution.py:392
  18.3 223.8 %all-gather.4.cloned.1.call-start = ((), (), s32[]{:S(2)}) async-start(), calls=%async_computation.6 | async-start | bytes 21233664 | tf_op jit(solution)/shard_map/all_gather | solution.py:404
  61.8 196.4 %all-to-all-start.1 = ((bf16[32,16,7680]{2,1,0:T(8,128)(2,1)}), bf16[32,16,7680]{2,1,0:T(8,128)(2,1)}, u32[]{:S(2)}, u32[]{:S(2)}) async-start(bf16[32,16,7680]{2,1,0:T(8,128)(2,1)} %bitcast.38), calls=%async_computation.1 | async-start | bytes 15728640 | tf_op jit(solution)/shard_map/all_to_all | solution.py:392
  258.2 77.6 %all-to-all-start.4 = ((bf16[32,16,3072]{2,1,0:T(8,128)(2,1)}), bf16[32,16,3072]{2,1,0:T(8,128)(2,1)S(1)}, u32[]{:S(2)}, u32[]{:S(2)}) async-start(bf16[32,16,3072]{2,1,0:T(8,128)(2,1)} %bitcast.48), calls=%async_computation.4 | async-start | bytes 6291456 | tf_op jit(solution)/shard_map/all_to_all | solution.py:392
  335.8 1.7 copy-start
  337.4 112.2 %all-to-all-start.2 = ((bf16[32,16,4736]{2,1,0:T(8,128)(2,1)}), bf16[32,16,4736]{2,1,0:T(8,128)(2,1)}, u32[]{:S(2)}, u32[]{:S(2)}) async-start(bf16[32,16,4736]{2,1,0:T(8,128)(2,1)} %bitcast.39), calls=%async_computation.2 | async-start | bytes 9699328 | tf_op jit(solution)/shard_map/all_to_all | solution.py:392
  449.6 44.2 %all-to-all-start.5 = ((bf16[32,16,1664]{2,1,0:T(8,128)(2,1)}), bf16[32,16,1664]{2,1,0:T(8,128)(2,1)S(1)}, u32[]{:S(2)}, u32[]{:S(2)}) async-start(bf16[32,16,1664]{2,1,0:T(8,128)(2,1)} %bitcast.46), calls=%async_computation.5 | async-start | bytes 3407872 | tf_op jit(solution)/shard_map/all_to_all | solution.py:392
  493.7 4.3 copy-start.1
  493.7 44.5 %all-to-all-start.3 = ((bf16[32,16,1664]{2,1,0:T(8,128)(2,1)}), bf16[32,16,1664]{2,1,0:T(8,128)(2,1)S(1)}, u32[]{:S(2)}, u32[]{:S(2)}) async-start(bf16[32,16,1664]{2,1,0:T(8,128)(2,1)} %bitcast.17), calls=%async_computation.3 | async-start | bytes 3407872 | tf_op jit(solution)/shard_map/all_to_all | solution.py:392
  538.3 1.2 copy-start.2
Sparse Core Ops, SparseCore 0:
  8.9 52.7 all-gather.5
  63.6 178.4 all-gather.3

commit v4 on v3

--- a/solution.py
+++ b/solution.py
@@ -12,7 +12,6 @@
 HEADS = 12
 HDIM = 128
 LANES = 128
-PLANES = 3
 SCALE = 1.0 / math.sqrt(HDIM)
 BF16 = jnp.bfloat16
 F32 = jnp.float32
@@ -42,10 +41,10 @@
     return jnp.dot(order, rows, preferred_element_type=F32).astype(BF16)
 
 
-def order_kernel(tokens_ref, queries_ref, order_ref, out_ref):
+def order_kernel(lead, tokens_ref, queries_ref, order_ref, out_ref):
     lines, res, width = queries_ref.shape
     span = res // lines
-    first = pl.program_id(0) < pl.num_programs(0) - PLANES
+    first = pl.program_id(0) < lead
 
     def put(ref):
         for i in range(lines):
@@ -56,24 +55,29 @@
     pl.when(jnp.logical_not(first))(lambda: put(queries_ref))
 
 
-def order_sent(tokens, queries, order):
+def order_sent(tokens, queries, order, token_planes):
     lines, planes, res, width = queries.shape
     depth = tokens.shape[-1]
-    lead = depth // width
+    parts = depth // width
+    lead = token_planes * parts
+    columns = (lead + planes) * width
+
+    def token_block(p):
+        p = jnp.minimum(p, lead - 1)
+        return 0, p // parts, 0, p % parts
+
     return pl.pallas_call(
-        order_kernel,
+        functools.partial(order_kernel, lead),
         grid=(lead + planes,),
         in_specs=[
-            pl.BlockSpec((lines, None, res, width), lambda p: (0, 0, 0, jnp.minimum(p, lead - 1))),
+            pl.BlockSpec((lines, None, res, width), token_block),
             pl.BlockSpec((lines, None, res, width), lambda p: (0, jnp.maximum(p - lead, 0), 0, 0)),
             pl.BlockSpec((res, res), lambda p: (0, 0)),
         ],
         out_specs=pl.BlockSpec((lines * res, width), lambda p: (0, p)),
-        out_shape=jax.ShapeDtypeStruct((lines * res, depth + planes * width), BF16),
+        out_shape=jax.ShapeDtypeStruct((lines * res, columns), BF16),
         cost_estimate=pl.CostEstimate(
-            flops=2 * lines * res * (depth + planes * width) * res,
-            bytes_accessed=4 * lines * res * (depth + planes * width),
-            transcendentals=0,
+            flops=2 * lines * res * columns * res, bytes_accessed=4 * lines * res * columns, transcendentals=0
         ),
         name="order_sent",
     )(tokens, queries, order)
@@ -105,7 +109,7 @@
         out_shape = [jax.ShapeDtypeStruct((lines, res, width), BF16)]
     else:
         rows = tokens.shape[0]
-        x_spec = pl.BlockSpec((rows, depth), lambda n: (0, 0))
+        x_spec = pl.BlockSpec((rows, depth), lambda n: (0, plane))
         out_specs = [pl.BlockSpec((rows, tile), lambda n: (0, n))]
         out_shape = [jax.ShapeDtypeStruct((rows, width), BF16)]
     if sent_width:
@@ -197,12 +201,12 @@
     )
 
 
-def far_attention(moved_q, kv, bias, order, back, plane, lead, lines, res, width, into=None):
+def far_attention(moved_q, kv, bias, order, back, plane, lead, lines, res, width, slot=0, slots=1, into=None):
     moved_kv = kv.ndim == 2
     kv_shape = (lines, res, 2 * width) if moved_kv else (1, 16, LANES)
     kv_block = kv.shape[:-1] + (2 * width,)
-    column = 0 if into is None else into.shape[1] - width - LANES
-    shape = (lines * res, column + width + LANES)
+    column = slot * (width + LANES)
+    shape = (lines * res, slots * (width + LANES))
     in_specs = [
         pl.BlockSpec((lines * res, width), lambda n: (0, lead + plane)),
         pl.BlockSpec(kv_block, lambda n: (0,) * kv.ndim),
@@ -237,65 +241,13 @@
     return parts + pltpu.roll(parts, LANES - 16, 1) + pltpu.roll(parts, LANES - 32, 1)
 
 
-def near_kernel(column, q_ref, kv_ref, bias_ref, far_ref, back_ref, *rest):
-    out_ref, far_s = rest[-2:]
-    lines, res, width = q_ref.shape
-    span = res // lines
-    heads = width // HDIM
-    for c in range(lines):
-        rows = pick(back_ref[...], far_ref[pl.ds(c * res, res), pl.ds(column, width + LANES)])
-        for line in range(lines):
-            far_s[line, pl.ds(c * span, span), :] = rows[line * span : (line + 1) * span]
-
-    def step(i, carry):
-        lse = far_sum(far_s[i, :, pl.ds(width, LANES)].astype(F32))
-        for h in range(heads):
-            at = pl.ds(h * HDIM, HDIM)
-            out, peak, total = attend(
-                q_ref[i, :, at], kv_ref[i, :, at], kv_ref[i, :, pl.ds(width + h * HDIM, HDIM)], bias_ref[i]
-            )
-            far_lse = lse[:, h : h + 1]
-            top = jnp.maximum(peak, far_lse)
-            near_w = jnp.exp(peak - top)
-            far_w = jnp.exp(far_lse - top)
-            scale = 1.0 / (total * near_w + far_w)
-            mixed = out * (near_w * scale) + far_s[i, :, at].astype(F32) * (far_w * scale)
-            out_ref[i, :, at] = mixed.astype(BF16)
-        return carry
-
-    lax.fori_loop(0, lines, step, 0)
-
-
-def near_attention(queries, kv, bias, far, back, plane, done):
-    lines, planes, res, width = queries.shape
-    in_specs = [
-        pl.BlockSpec((lines, None, res, width), lambda n: (0, plane, 0, 0)),
-        pl.BlockSpec(kv.shape, lambda n: (0,) * kv.ndim),
-        pl.BlockSpec((None, lines, res, res), lambda n: (plane, 0, 0, 0)),
-        pl.BlockSpec(far.shape, lambda n: (0, 0)),
-        pl.BlockSpec((res, res), lambda n: (0, 0)),
-    ]
-    args = (queries, kv, bias, far, back)
-    if done is not None:
-        in_specs.append(pl.BlockSpec(memory_space=pl.ANY))
-        args = args + (done,)
-    return pl.pallas_call(
-        functools.partial(near_kernel, far.shape[1] - width - LANES),
-        grid=(1,),
-        in_specs=in_specs,
-        out_specs=pl.BlockSpec((lines, None, res, width), lambda n: (0, plane, 0, 0)),
-        out_shape=jax.ShapeDtypeStruct(queries.shape, BF16),
-        scratch_shapes=[pltpu.VMEM((lines, res, width + LANES), BF16)],
-        input_output_aliases={} if done is None else {5: 0},
-        cost_estimate=attention_cost(lines, res, width),
-        name=f"near_{plane}",
-    )(*args)
-
-
 def part_kernel(q_ref, kv_ref, bias_ref, order_ref, mean_ref, lse_ref, kv_s):
     lines, res, width = q_ref.shape
     heads = width // HDIM
-    to_away(kv_ref, order_ref, kv_s)
+    if len(kv_ref.shape) == 2:
+        to_away(kv_ref, order_ref, kv_s)
+    else:
+        kv_s = kv_ref
     lane = lax.broadcasted_iota(jnp.int32, (res, LANES), 1)
 
     def step(i, carry):
@@ -320,7 +272,7 @@
         grid=(1,),
         in_specs=[
             pl.BlockSpec((lines, None, res, width), lambda n: (0, plane, 0, 0)),
-            pl.BlockSpec(kv.shape, lambda n: (0, 0)),
+            pl.BlockSpec(kv.shape, lambda n: (0,) * kv.ndim),
             pl.BlockSpec((None, lines, res, res), lambda n: (plane, 0, 0, 0)),
             pl.BlockSpec((res, res), lambda n: (0, 0)),
         ],
@@ -332,13 +284,14 @@
             jax.ShapeDtypeStruct((lines, res, width), F32),
             jax.ShapeDtypeStruct((lines, res, LANES), F32),
         ],
-        scratch_shapes=[pltpu.VMEM((lines, res, 2 * width), BF16)],
+        scratch_shapes=[pltpu.VMEM((lines, res, 2 * width) if kv.ndim == 2 else (1, 16, LANES), BF16)],
         cost_estimate=attention_cost(lines, res, width),
         name=f"near_part_{plane}",
     )(queries, kv, bias, order)
 
 
-def merge_kernel(far_ref, mean_ref, lse_ref, back_ref, done_ref, out_ref):
+def merge_kernel(far_ref, mean_ref, lse_ref, back_ref, *rest):
+    out_ref = rest[-1]
     lines, span, width = mean_ref.shape
     res = lines * span
     far = pick(back_ref[...], far_ref[...])
@@ -358,27 +311,32 @@
         out_ref[:, :, at] = mixed.astype(BF16).reshape(lines, span, HDIM)
 
 
-def merge_parts(far, mean, lse, back, plane, done):
-    lines, planes, res, width = done.shape
-    span = res // lines
+def merge_parts(far, slot, near, back, plane, planes, done):
+    mean, lse = near
+    lines, res, width = mean.shape
+    span = res // lines
+    in_specs = [
+        pl.BlockSpec((res, width + LANES), lambda c: (c, slot)),
+        pl.BlockSpec((lines, span, width), lambda c: (0, c, 0)),
+        pl.BlockSpec((lines, span, LANES), lambda c: (0, c, 0)),
+        pl.BlockSpec((res, res), lambda c: (0, 0)),
+    ]
+    args = (far, mean, lse, back)
+    if done is not None:
+        in_specs.append(pl.BlockSpec(memory_space=pl.ANY))
+        args = args + (done,)
     return pl.pallas_call(
         merge_kernel,
         grid=(lines,),
-        in_specs=[
-            pl.BlockSpec((res, width + LANES), lambda c: (c, 0)),
-            pl.BlockSpec((lines, span, width), lambda c: (0, c, 0)),
-            pl.BlockSpec((lines, span, LANES), lambda c: (0, c, 0)),
-            pl.BlockSpec((res, res), lambda c: (0, 0)),
-            pl.BlockSpec(memory_space=pl.ANY),
-        ],
+        in_specs=in_specs,
         out_specs=pl.BlockSpec((lines, None, span, width), lambda c: (0, plane, c, 0)),
-        out_shape=jax.ShapeDtypeStruct(done.shape, BF16),
-        input_output_aliases={4: 0},
+        out_shape=jax.ShapeDtypeStruct((lines, planes, res, width), BF16),
+        input_output_aliases={} if done is None else {4: 0},
         cost_estimate=pl.CostEstimate(
             flops=2 * lines * res * res * width, bytes_accessed=10 * lines * res * width, transcendentals=0
         ),
         name=f"merge_{plane}",
-    )(far, mean, lse, back, done)
+    )(*args)
 
 
 def mask_bias(codes, res):
@@ -421,7 +379,8 @@
         (dest_half == 0)[:, None], halves[:, :, 0, 1].reshape(1, -1), halves[:, :, 1, 1].reshape(1, -1)
     )
     codes = exchange(sent_codes)
-    sent = order_sent(tokens, queries, to_sent)
+    token_planes = 2
+    sent = order_sent(tokens, queries, to_sent, token_planes)
     weight, sent, codes = gather_weight(jnp.concatenate([key_weight, value_weight], axis=1), count, sent, codes)
     codes = codes.reshape(res, planes).T
     far_bias = mask_bias(codes, res)
@@ -432,24 +391,29 @@
     moved = exchange(sent)
     far = functools.partial(
         far_attention, moved, bias=far_bias, order=away, back=from_away,
-        lead=depth // width, lines=lines, res=res, width=width,
+        lead=token_planes * depth // width, lines=lines, res=res, width=width,
     )
-    mean_width = width + LANES
+    near = functools.partial(near_part, queries, bias=near_bias, order=away)
+    merge = functools.partial(merge_parts, back=to_home, planes=planes)
     home_2, sent_2 = project(tokens, weight, to_sent, 2, 2 * width)
+    (home_0,) = project(tokens, weight, to_sent, 0, 0)
+    sent_2, home_0 = lax.optimization_barrier((sent_2, home_0))
     moved_2 = exchange(sent_2)
-    home_1, sent_1 = project(tokens, weight, to_sent, 1, 2 * width + mean_width)
+    (moved_1,) = project(moved, weight, to_sent, 1, 0)
+    (home_1,) = project(tokens, weight, to_sent, 1, 0)
+    sent = far(kv=home_2, plane=0, slots=2)
+    sent = far(kv=moved_1, plane=2, slot=1, slots=2, into=sent)
+    sent, home_1 = lax.optimization_barrier((sent, home_1))
+    far_02 = exchange(sent)
     (moved_0,) = project(moved, weight, to_sent, 0, 0)
-    sent_1, moved_0 = lax.optimization_barrier((sent_1, moved_0))
-    moved_1 = exchange(far(kv=home_2, plane=0, into=sent_1))
-    (home_0,) = project(tokens, weight, to_sent, 0, 0)
-    mean_2, lse_2 = near_part(queries, moved_0, near_bias, away, 2)
-    sent, home_0, mean_2, lse_2 = lax.optimization_barrier((far(kv=moved_2, plane=1), home_0, mean_2, lse_2))
+    near_2 = near(kv=moved_0, plane=2)
+    near_1 = near(kv=home_0, plane=1)
+    sent, near_1, near_2 = lax.optimization_barrier((far(kv=moved_2, plane=1), near_1, near_2))
     far_1 = exchange(sent)
-    out = near_attention(queries, home_1, near_bias, moved_1, to_home, 0, None)
-    sent, out = lax.optimization_barrier((far(kv=moved_1, plane=2), out))
-    far_2 = exchange(sent)
-    out = near_attention(queries, home_0, near_bias, far_1, to_home, 1, out)
-    out = merge_parts(far_2, mean_2, lse_2, to_home, 2, out)
+    near_0 = near(kv=home_1, plane=0)
+    out = merge(far_02, 0, near_0, plane=0, done=None)
+    out = merge(far_02, 1, near_2, plane=2, done=out)
+    out = merge(far_1, 0, near_1, plane=1, done=out)
     return out.reshape(scenes, lines, planes, res, width)
 
 

time: 554 us -> 539 us (0.973)
  waiting for transfers between devices: 315 us -> 273 us
  Pallas kernels: 184 us -> 208 us
    all_to_all x6 -> x5, waiting for transfers between devices: 104 us -> 29.9 us  [exchange(): return lax.all_to_all(rows, 'seq', split_axis=0, concat_axis=0, tiled=True)]
    all_gather x1, waiting for transfers between devices: 177 us -> 211 us  [gather_weight(): lax.all_gather(blocks, 'seq', axis=1, tiled=True, axis_index_groups=within)]
    pallas_call x1 -> x3, Pallas kernels: 17 us -> 49.3 us  [near_part(): pl.pallas_call(part_kernel, grid=(1,), in_specs=[pl.BlockSpec((lines, Non...]
    pallas_call x4, Pallas kernels: 52.1 us -> 29.8 us  [the longest x3 18.4 us: merge_parts(): pl.pallas_call(merge_kernel, grid=(lines,), in_specs=in_specs, out_specs=...]
    pallas_call x4 -> x5, Pallas kernels: 62.5 us -> 76.8 us  [project(): pl.pallas_call(project_kernel, grid=(width // tile,), in_specs=[x_spec, p...]
    all_to_all x6 -> x5, starting transfers between devices: 29.6 us -> 34 us  [exchange(): return lax.all_to_all(rows, 'seq', split_axis=0, concat_axis=0, tiled=True)]
  transfers between devices with their start and end apart: 8 -> 7, of which waited for: 6 -> 6; matrix products, arithmetic and copies ran while one was open for 1% -> 1% of each run, Pallas kernels for 32% -> 38%
where the time goes in v4:
time: 539 us; the launch traced here: 538 us
  waiting for transfers between devices  273 us (51%)
  Pallas kernels  208 us (39%)
  starting transfers between devices  34.1 us (6%)
  between operations  13.5 us (3%)
  other arithmetic  5.62 us (1%)
    all_gather x1, waiting for transfers between devices, gather_weight(): lax.all_gather(blocks, 'seq', axis=1, tiled=True, axis_index_groups=within)  211 us
    pallas_call x5, Pallas kernels, project(): pl.pallas_call(project_kernel, grid=(width // tile,), in_specs=[x_spec, p...  76.8 us
    pallas_call x3, Pallas kernels, far_attention(): pl.pallas_call(functools.partial(far_kernel, moved_kv, column), grid=(1,)...  52.3 us
    pallas_call x3, Pallas kernels, near_part(): pl.pallas_call(part_kernel, grid=(1,), in_specs=[pl.BlockSpec((lines, Non...  49.3 us
    all_to_all x5, starting transfers between devices, exchange(): return lax.all_to_all(rows, 'seq', split_axis=0, concat_axis=0, tiled=True)  34 us
    all_gather x1, waiting for transfers between devices, gather_weight(): lax.all_gather(shard[None], 'seq', axis=0, tiled=True, axis_index_groups=...  31.9 us
    all_to_all x5, waiting for transfers between devices, exchange(): return lax.all_to_all(rows, 'seq', split_axis=0, concat_axis=0, tiled=True)  29.9 us
    pallas_call x3, Pallas kernels, merge_parts(): pl.pallas_call(merge_kernel, grid=(lines,), in_specs=in_specs, out_specs=...  18.4 us
  transfers between devices with their start and end apart: 7, of which 6 were waited for; matrix products, arithmetic and copies ran while one was open for 1% of the time, Pallas kernels for 38%

profile of v4, /device:TPU:0, one launch (start us, length us, event | category | flops | bytes accessed | tf_op | source)
XLA Modules:
  0.0 537.8 jit_solution(3258906519234167074)
XLA Ops:
  11.0 7.3 %all-to-all-start = ((s32[32,1,12]{2,1,0:T(1,128)}), s32[32,1,12]{2,1,0:T(1,128)S(1)}, u32[]{:S(2)}, u32[]{:S(2)}) async-start(s32[32,1,12]{2,1,0:T(1,128)} %broadcast_select_fusion), calls=%async_computation | async-start | bytes 32768 | tf_op jit(solution)/shard_map/all_to_all | solution.py:350
  18.3 11.4 %order_sent.1 = bf16[512,10752]{1,0:T(8,128)(2,1)} custom-call(bf16[4,3,128,3072]{3,2,1,0:T(8,128)(2,1)} %bitcast.40, bf16[4,3,128,1536]{3,2,1,0:T(8,128)(2,1)} %bitcast.32, bf16[128,128]{1,0:T(8,128)(2,1)} %constant.60.clone.order_ref), custom_call_target="tpu_custom_call" | custom-call | flops 1409286144 | bytes 22020096 | tf_op jit(solution)/shard_map/order_sent/pallas_call | solution.py:69
  29.8 31.9 %all-gather.6.cloned.1.call-done = bf16[384,3072]{1,0:T(8,128)(2,1)} async-done(((bf16[96,3072]{1,0:T(8,128)(2,1)}), bf16[384,3072]{1,0:T(8,128)(2,1)}) %all-gather.6.cloned.1.call-update) | async-done | bytes 2359312 | tf_op jit(solution)/shard_map/all_gather | solution.py:360
  65.5 211.5 %all-gather.4.cloned.1.call-done = bf16[4,768,3072]{2,1,0:T(8,128)(2,1)} async-done(((bf16[4,96,3072]{2,1,0:T(8,128)(2,1)}), bf16[4,768,3072]{2,1,0:T(8,128)(2,1)}) %all-gather.4.cloned.1.call-update) | async-done | bytes 18874384 | tf_op jit(solution)/shard_map/all_gather | solution.py:362
  277.0 16.0 %project_2.1 = (bf16[4,128,3072]{2,1,0:T(8,128)(2,1)}, bf16[512,3072]{1,0:T(8,128)(2,1)}) custom-call(bf16[4,3,128,3072]{3,2,1,0:T(8,128)(2,1)} %bitcast.41, bf16[3072,3072]{1,0:T(8,128)(2,1)} %bitcast.49, bf16[128,128]{1,0:T(8,128)(2,1)} %constant.60.clone.order_ref), custom_call_target="tpu_custom_call" | custom-call | flops 9663676416 | bytes 28311552 | tf_op jit(solution)/shard_map/project_2/pallas_call | solution.py:118
  293.0 15.2 %project_0.2.kv_ref = bf16[4,128,3072]{2,1,0:T(8,128)(2,1)} custom-call(bf16[4,3,128,3072]{3,2,1,0:T(8,128)(2,1)} %bitcast.42, bf16[3072,3072]{1,0:T(8,128)(2,1)} %bitcast.50, bf16[128,128]{1,0:T(8,128)(2,1)} %constant.60.clone.order_ref), custom_call_target="tpu_custom_call" | custom-call | flops 9663676416 | bytes 28311552 | tf_op jit(solution)/shard_map/project_0/pallas_call | solution.py:118
  311.7 14.7 %all-to-all-start.2 = ((bf16[32,16,3072]{2,1,0:T(8,128)(2,1)}), bf16[32,16,3072]{2,1,0:T(8,128)(2,1)S(1)}, u32[]{:S(2)}, u32[]{:S(2)}) async-start(bf16[32,16,3072]{2,1,0:T(8,128)(2,1)} %bitcast.45), calls=%async_computation.2 | async-start | bytes 6291456 | tf_op jit(solution)/shard_map/all_to_all | solution.py:350
  327.6 16.9 %far_0.1.rest_0_ = bf16[512,3328]{1,0:T(8,128)(2,1)} custom-call(bf16[512,10752]{1,0:T(8,128)(2,1)} %bitcast.6.q_ref.x_ref, bf16[4,128,3072]{2,1,0:T(8,128)(2,1)} %get-tuple-element.38.kv_ref, f32[3,128,128]{2,1,0:T(8,128)} %select_select_fusion.1.bias_ref, bf16[128,128]{1,0:T(8,128)(2,1)} %constant.62.clone.order_ref, bf16[128,128]{1,0:T(8,128)(2,1)} %constant.63.clone.back_ref), custom_call_target="tpu_custom_call" | custom-call | flops 402653184 | bytes 7864320 | tf_op jit(solution)/shard_map/far_0/pallas_call | solution.py:221
  344.5 15.2 %project_1.2.kv_ref = bf16[512,3072]{1,0:T(8,128)(2,1)} custom-call(bf16[512,10752]{1,0:T(8,128)(2,1)} %bitcast.6.q_ref.x_ref, bf16[3072,3072]{1,0:T(8,128)(2,1)} %bitcast.51, bf16[128,128]{1,0:T(8,128)(2,1)} %constant.60.clone.order_ref), custom_call_target="tpu_custom_call" | custom-call | flops 9663676416 | bytes 28311552 | tf_op jit(solution)/shard_map/project_1/pallas_call | solution.py:118
  359.7 17.7 %far_2.1 = bf16[512,3328]{1,0:T(8,128)(2,1)} custom-call(bf16[512,10752]{1,0:T(8,128)(2,1)} %bitcast.6.q_ref.x_ref, bf16[512,3072]{1,0:T(8,128)(2,1)} %project_1.2.kv_ref, f32[3,128,128]{2,1,0:T(8,128)} %select_select_fusion.1.bias_ref, bf16[128,128]{1,0:T(8,128)(2,1)} %constant.62.clone.order_ref, ...), custom_call_target="tpu_custom_call", output_to_operand_aliasing={{}: (5, {})} | custom-call | flops 402653184 | bytes 7864320 | tf_op jit(solution)/shard_map/far_2/pallas_call | solution.py:221
  377.4 15.2 %project_1.3.kv_ref = bf16[4,128,3072]{2,1,0:T(8,128)(2,1)} custom-call(bf16[4,3,128,3072]{3,2,1,0:T(8,128)(2,1)} %bitcast.43, bf16[3072,3072]{1,0:T(8,128)(2,1)} %bitcast.52, bf16[128,128]{1,0:T(8,128)(2,1)} %constant.60.clone.order_ref), custom_call_target="tpu_custom_call" | custom-call | flops 9663676416 | bytes 28311552 | tf_op jit(solution)/shard_map/project_1/pallas_call | solution.py:118
  392.7 5.1 all-to-all-done.2
  399.4 4.2 all-to-all-start.4
  405.0 16.1 %near_part_1.1 = (f32[4,128,1536]{2,1,0:T(8,128)}, f32[4,128,128]{2,1,0:T(8,128)}) custom-call(bf16[4,3,128,1536]{3,2,1,0:T(8,128)(2,1)} %bitcast.33, bf16[4,128,3072]{2,1,0:T(8,128)(2,1)} %project_0.2.kv_ref, f32[3,4,128,128]{3,2,1,0:T(8,128)} %select_select_fusion.bias_ref, bf16[128,128]{1,0:T(8,128)(2,1)} %constant.62.clone.order_ref), custom_call_target="tpu_custom_call" | custom-call | flops 402653184 | bytes 7864320 | tf_op jit(solution)/shard_map/near_part_1/pallas_call | solution.py:270
  421.1 15.2 %project_0.3.kv_ref = bf16[512,3072]{1,0:T(8,128)(2,1)} custom-call(bf16[512,10752]{1,0:T(8,128)(2,1)} %bitcast.6.q_ref.x_ref, bf16[3072,3072]{1,0:T(8,128)(2,1)} %bitcast.53, bf16[128,128]{1,0:T(8,128)(2,1)} %constant.60.clone.order_ref), custom_call_target="tpu_custom_call" | custom-call | flops 9663676416 | bytes 28311552 | tf_op jit(solution)/shard_map/project_0/pallas_call | solution.py:118
  436.3 17.1 %near_part_2.1 = (f32[4,128,1536]{2,1,0:T(8,128)}, f32[4,128,128]{2,1,0:T(8,128)}) custom-call(bf16[4,3,128,1536]{3,2,1,0:T(8,128)(2,1)} %bitcast.34, bf16[512,3072]{1,0:T(8,128)(2,1)} %project_0.3.kv_ref, f32[3,4,128,128]{3,2,1,0:T(8,128)} %select_select_fusion.bias_ref, bf16[128,128]{1,0:T(8,128)(2,1)} %constant.62.clone.order_ref), custom_call_target="tpu_custom_call" | custom-call | flops 402653184 | bytes 7864320 | tf_op jit(solution)/shard_map/near_part_2/pallas_call | solution.py:270
  453.3 17.7 %far_1.1 = bf16[512,1664]{1,0:T(8,128)(2,1)} custom-call(bf16[512,10752]{1,0:T(8,128)(2,1)} %bitcast.6.q_ref.x_ref, bf16[512,3072]{1,0:T(8,128)(2,1)} %bitcast.39, f32[3,128,128]{2,1,0:T(8,128)} %select_select_fusion.1.bias_ref, bf16[128,128]{1,0:T(8,128)(2,1)} %constant.62.clone.order_ref, bf16[128,128]{1,0:T(8,128)(2,1)} %constant.63.clone.back_ref), custom_call_target="tpu_custom_call" | custom-call | flops 402653184 | bytes 7864320 | tf_op jit(solution)/shard_map/far_1/pallas_call | solution.py:221
  471.1 9.4 %all-to-all-done.4 = bf16[32,16,3328]{2,1,0:T(8,128)(2,1)S(1)} async-done(((bf16[32,16,3328]{2,1,0:T(8,128)(2,1)}), bf16[32,16,3328]{2,1,0:T(8,128)(2,1)S(1)}, u32[]{:S(2)}, u32[]{:S(2)}) %all-to-all-start.4) | async-done | bytes 3407904 | tf_op jit(solution)/shard_map/all_to_all | solution.py:350
  480.5 4.0 all-to-all-start.3
  484.5 16.1 %near_part_0.1 = (f32[4,128,1536]{2,1,0:T(8,128)}, f32[4,128,128]{2,1,0:T(8,128)}) custom-call(bf16[4,3,128,1536]{3,2,1,0:T(8,128)(2,1)} %bitcast.35, bf16[4,128,3072]{2,1,0:T(8,128)(2,1)} %project_1.3.kv_ref, f32[3,4,128,128]{3,2,1,0:T(8,128)} %select_select_fusion.bias_ref, bf16[128,128]{1,0:T(8,128)(2,1)} %constant.62.clone.order_ref), custom_call_target="tpu_custom_call" | custom-call | flops 402653184 | bytes 7864320 | tf_op jit(solution)/shard_map/near_part_0/pallas_call | solution.py:270
  500.7 6.1 %merge_0.1.rest_0_ = bf16[4,3,128,1536]{3,2,1,0:T(8,128)(2,1)} custom-call(bf16[512,3328]{1,0:T(8,128)(2,1)} %bitcast.37, f32[4,128,1536]{2,1,0:T(8,128)} %get-tuple-element.43.mean_ref, f32[4,128,128]{2,1,0:T(8,128)} %get-tuple-element.44.lse_ref, bf16[128,128]{1,0:T(8,128)(2,1)} %constant.61.clone.back_ref), custom_call_target="tpu_custom_call" | custom-call | flops 201326592 | bytes 7864320 | tf_op jit(solution)/shard_map/merge_0/pallas_call | solution.py:328
  506.8 6.1 %merge_2.1.rest_0_ = bf16[4,3,128,1536]{3,2,1,0:T(8,128)(2,1)} custom-call(bf16[512,3328]{1,0:T(8,128)(2,1)} %bitcast.38, f32[4,128,1536]{2,1,0:T(8,128)} %get-tuple-element.40.mean_ref, f32[4,128,128]{2,1,0:T(8,128)} %get-tuple-element.41.lse_ref, bf16[128,128]{1,0:T(8,128)(2,1)} %constant.61.clone.back_ref, ...), custom_call_target="tpu_custom_call", output_to_operand_aliasing={{}: (4, {})} | custom-call | flops 201326592 | bytes 7864320 | tf_op jit(solution)/shard_map/merge_2/pallas_call | solution.py:328
  512.9 11.9 %all-to-all-done.3 = bf16[32,16,1664]{2,1,0:T(8,128)(2,1)} async-done(((bf16[32,16,1664]{2,1,0:T(8,128)(2,1)}), bf16[32,16,1664]{2,1,0:T(8,128)(2,1)}, u32[]{:S(2)}, u32[]{:S(2)}) %all-to-all-start.3) | async-done | bytes 1703968 | tf_op jit(solution)/shard_map/all_to_all | solution.py:350
  524.8 6.1 %merge_1.1 = bf16[4,3,128,1536]{3,2,1,0:T(8,128)(2,1)} custom-call(bf16[512,1664]{1,0:T(8,128)(2,1)} %bitcast.18.far_ref, f32[4,128,1536]{2,1,0:T(8,128)} %get-tuple-element.36.mean_ref, f32[4,128,128]{2,1,0:T(8,128)} %get-tuple-element.37.lse_ref, bf16[128,128]{1,0:T(8,128)(2,1)} %constant.61.clone.back_ref, ...), custom_call_target="tpu_custom_call", output_to_operand_aliasing={{}: (4, {})} | custom-call | flops 201326592 | bytes 7864320 | tf_op jit(solution)/shard_map/merge_1/pallas_call | solution.py:328
  (28 shorter events, 16.0 us)
Async XLA Ops:
  6.5 55.2 %all-gather.6.cloned.1.call-start = ((), (), s32[]{:S(2)}) async-start(), calls=%async_computation.6 | async-start | bytes 2949120 | tf_op jit(solution)/shard_map/all_gather | solution.py:360
  11.0 18.8 %all-to-all-start = ((s32[32,1,12]{2,1,0:T(1,128)}), s32[32,1,12]{2,1,0:T(1,128)S(1)}, u32[]{:S(2)}, u32[]{:S(2)}) async-start(s32[32,1,12]{2,1,0:T(1,128)} %broadcast_select_fusion), calls=%async_computation | async-start | bytes 32768 | tf_op jit(solution)/shard_map/all_to_all | solution.py:350
  18.3 258.7 %all-gather.4.cloned.1.call-start = ((), (), s32[]{:S(2)}) async-start(), calls=%async_computation.5 | async-start | bytes 21233664 | tf_op jit(solution)/shard_map/all_gather | solution.py:362
  61.8 250.0 %all-to-all-start.1 = ((bf16[32,16,10752]{2,1,0:T(8,128)(2,1)}), bf16[32,16,10752]{2,1,0:T(8,128)(2,1)}, u32[]{:S(2)}, u32[]{:S(2)}) async-start(bf16[32,16,10752]{2,1,0:T(8,128)(2,1)} %bitcast.36), calls=%async_computation.1 | async-start | bytes 22020096 | tf_op jit(solution)/shard_map/all_to_all | solution.py:350
  311.7 86.0 %all-to-all-start.2 = ((bf16[32,16,3072]{2,1,0:T(8,128)(2,1)}), bf16[32,16,3072]{2,1,0:T(8,128)(2,1)S(1)}, u32[]{:S(2)}, u32[]{:S(2)}) async-start(bf16[32,16,3072]{2,1,0:T(8,128)(2,1)} %bitcast.45), calls=%async_computation.2 | async-start | bytes 6291456 | tf_op jit(solution)/shard_map/all_to_all | solution.py:350
  397.8 1.6 copy-start.1
  399.4 81.1 %all-to-all-start.4 = ((bf16[32,16,3328]{2,1,0:T(8,128)(2,1)}), bf16[32,16,3328]{2,1,0:T(8,128)(2,1)S(1)}, u32[]{:S(2)}, u32[]{:S(2)}) async-start(bf16[32,16,3328]{2,1,0:T(8,128)(2,1)} %bitcast.19), calls=%async_computation.4 | async-start | bytes 6815744 | tf_op jit(solution)/shard_map/all_to_all | solution.py:350
  480.5 20.2 %copy-start = (bf16[32,16,3328]{2,1,0:T(8,128)(2,1)}, bf16[32,16,3328]{2,1,0:T(8,128)(2,1)S(1)}, u32[]{:S(2)}) copy-start(bf16[32,16,3328]{2,1,0:T(8,128)(2,1)S(1)} %all-to-all-done.4) | copy-start | bytes 10223620
  480.5 44.4 %all-to-all-start.3 = ((bf16[32,16,1664]{2,1,0:T(8,128)(2,1)}), bf16[32,16,1664]{2,1,0:T(8,128)(2,1)}, u32[]{:S(2)}, u32[]{:S(2)}) async-start(bf16[32,16,1664]{2,1,0:T(8,128)(2,1)} %bitcast.44), calls=%async_computation.3 | async-start | bytes 3407872 | tf_op jit(solution)/shard_map/all_to_all | solution.py:350
Sparse Core Ops, SparseCore 0:
  8.9 52.7 all-gather.5
  63.6 213.3 all-gather.3

commit v5 on v4

--- a/solution.py
+++ b/solution.py
@@ -396,20 +396,19 @@
     near = functools.partial(near_part, queries, bias=near_bias, order=away)
     merge = functools.partial(merge_parts, back=to_home, planes=planes)
     home_2, sent_2 = project(tokens, weight, to_sent, 2, 2 * width)
-    (home_0,) = project(tokens, weight, to_sent, 0, 0)
-    sent_2, home_0 = lax.optimization_barrier((sent_2, home_0))
     moved_2 = exchange(sent_2)
     (moved_1,) = project(moved, weight, to_sent, 1, 0)
-    (home_1,) = project(tokens, weight, to_sent, 1, 0)
+    (home_0,) = project(tokens, weight, to_sent, 0, 0)
     sent = far(kv=home_2, plane=0, slots=2)
     sent = far(kv=moved_1, plane=2, slot=1, slots=2, into=sent)
-    sent, home_1 = lax.optimization_barrier((sent, home_1))
+    sent, home_0 = lax.optimization_barrier((sent, home_0))
     far_02 = exchange(sent)
     (moved_0,) = project(moved, weight, to_sent, 0, 0)
     near_2 = near(kv=moved_0, plane=2)
     near_1 = near(kv=home_0, plane=1)
     sent, near_1, near_2 = lax.optimization_barrier((far(kv=moved_2, plane=1), near_1, near_2))
     far_1 = exchange(sent)
+    (home_1,) = project(tokens, weight, to_sent, 1, 0)
     near_0 = near(kv=home_1, plane=0)
     out = merge(far_02, 0, near_0, plane=0, done=None)
     out = merge(far_02, 1, near_2, plane=2, done=out)

time: 539 us -> 531 us (0.985)
  starting transfers between devices: 34.1 us -> 22 us
    all_to_all x5, starting transfers between devices: 34 us -> 22 us  [exchange(): return lax.all_to_all(rows, 'seq', split_axis=0, concat_axis=0, tiled=True)]
  transfers between devices with their start and end apart: 7 -> 7, of which waited for: 6 -> 5; matrix products, arithmetic and copies ran while one was open for 1% -> 1% of each run, Pallas kernels for 38% -> 38%
where the time goes in v5:
time: 531 us; the launch traced here: 529 us
  waiting for transfers between devices  277 us (52%)
  Pallas kernels  208 us (39%)
  starting transfers between devices  22 us (4%)
  between operations  13.5 us (3%)
  other arithmetic  5.65 us (1%)
    all_gather x1, waiting for transfers between devices, gather_weight(): lax.all_gather(blocks, 'seq', axis=1, tiled=True, axis_index_groups=within)  211 us
    pallas_call x5, Pallas kernels, project(): pl.pallas_call(project_kernel, grid=(width // tile,), in_specs=[x_spec, p...  76.8 us
    pallas_call x3, Pallas kernels, far_attention(): pl.pallas_call(functools.partial(far_kernel, moved_kv, column), grid=(1,)...  52.3 us
    pallas_call x3, Pallas kernels, near_part(): pl.pallas_call(part_kernel, grid=(1,), in_specs=[pl.BlockSpec((lines, Non...  49.2 us
    all_to_all x5, waiting for transfers between devices, exchange(): return lax.all_to_all(rows, 'seq', split_axis=0, concat_axis=0, tiled=True)  33.4 us
    all_gather x1, waiting for transfers between devices, gather_weight(): lax.all_gather(shard[None], 'seq', axis=0, tiled=True, axis_index_groups=...  31.9 us
    all_to_all x5, starting transfers between devices, exchange(): return lax.all_to_all(rows, 'seq', split_axis=0, concat_axis=0, tiled=True)  22 us
    pallas_call x3, Pallas kernels, merge_parts(): pl.pallas_call(merge_kernel, grid=(lines,), in_specs=in_specs, out_specs=...  18.4 us
  transfers between devices with their start and end apart: 7, of which 5 were waited for; matrix products, arithmetic and copies ran while one was open for 1% of the time, Pallas kernels for 38%

profile of v5, /device:TPU:0, one launch (start us, length us, event | category | flops | bytes accessed | tf_op | source)
XLA Modules:
  0.0 529.1 jit_solution(4840294298732588652)
XLA Ops:
  11.0 7.3 %all-to-all-start = ((s32[32,1,12]{2,1,0:T(1,128)}), s32[32,1,12]{2,1,0:T(1,128)S(1)}, u32[]{:S(2)}, u32[]{:S(2)}) async-start(s32[32,1,12]{2,1,0:T(1,128)} %broadcast_select_fusion), calls=%async_computation | async-start | bytes 32768 | tf_op jit(solution)/shard_map/all_to_all | solution.py:350
  18.3 11.4 %order_sent.1 = bf16[512,10752]{1,0:T(8,128)(2,1)} custom-call(bf16[4,3,128,3072]{3,2,1,0:T(8,128)(2,1)} %bitcast.40, bf16[4,3,128,1536]{3,2,1,0:T(8,128)(2,1)} %bitcast.32, bf16[128,128]{1,0:T(8,128)(2,1)} %constant.60.clone.order_ref), custom_call_target="tpu_custom_call" | custom-call | flops 1409286144 | bytes 22020096 | tf_op jit(solution)/shard_map/order_sent/pallas_call | solution.py:69
  29.8 31.9 %all-gather.6.cloned.1.call-done = bf16[384,3072]{1,0:T(8,128)(2,1)} async-done(((bf16[96,3072]{1,0:T(8,128)(2,1)}), bf16[384,3072]{1,0:T(8,128)(2,1)}) %all-gather.6.cloned.1.call-update) | async-done | bytes 2359312 | tf_op jit(solution)/shard_map/all_gather | solution.py:360
  61.8 3.8 all-to-all-start.1
  65.5 211.5 %all-gather.4.cloned.1.call-done = bf16[4,768,3072]{2,1,0:T(8,128)(2,1)} async-done(((bf16[4,96,3072]{2,1,0:T(8,128)(2,1)}), bf16[4,768,3072]{2,1,0:T(8,128)(2,1)}) %all-gather.4.cloned.1.call-update) | async-done | bytes 18874384 | tf_op jit(solution)/shard_map/all_gather | solution.py:362
  277.0 16.1 %project_2.1 = (bf16[4,128,3072]{2,1,0:T(8,128)(2,1)}, bf16[512,3072]{1,0:T(8,128)(2,1)}) custom-call(bf16[4,3,128,3072]{3,2,1,0:T(8,128)(2,1)} %bitcast.41, bf16[3072,3072]{1,0:T(8,128)(2,1)} %bitcast.49, bf16[128,128]{1,0:T(8,128)(2,1)} %constant.60.clone.order_ref), custom_call_target="tpu_custom_call" | custom-call | flops 9663676416 | bytes 28311552 | tf_op jit(solution)/shard_map/project_2/pallas_call | solution.py:118
  293.0 18.7 %all-to-all-done.1 = bf16[32,16,10752]{2,1,0:T(8,128)(2,1)} async-done(((bf16[32,16,10752]{2,1,0:T(8,128)(2,1)}), bf16[32,16,10752]{2,1,0:T(8,128)(2,1)}, u32[]{:S(2)}, u32[]{:S(2)}) %all-to-all-start.1) | async-done | bytes 11010080 | tf_op jit(solution)/shard_map/all_to_all | solution.py:350
  315.7 16.9 %far_0.1.rest_0_ = bf16[512,3328]{1,0:T(8,128)(2,1)} custom-call(bf16[512,10752]{1,0:T(8,128)(2,1)} %bitcast.6.q_ref.x_ref, bf16[4,128,3072]{2,1,0:T(8,128)(2,1)} %get-tuple-element.27.kv_ref, f32[3,128,128]{2,1,0:T(8,128)} %select_select_fusion.1.bias_ref, bf16[128,128]{1,0:T(8,128)(2,1)} %constant.62.clone.order_ref, bf16[128,128]{1,0:T(8,128)(2,1)} %constant.63.clone.back_ref), custom_call_target="tpu_custom_call" | custom-call | flops 402653184 | bytes 7864320 | tf_op jit(solution)/shard_map/far_0/pallas_call | solution.py:221
  332.6 15.2 %project_1.2.kv_ref = bf16[512,3072]{1,0:T(8,128)(2,1)} custom-call(bf16[512,10752]{1,0:T(8,128)(2,1)} %bitcast.6.q_ref.x_ref, bf16[3072,3072]{1,0:T(8,128)(2,1)} %bitcast.50, bf16[128,128]{1,0:T(8,128)(2,1)} %constant.60.clone.order_ref), custom_call_target="tpu_custom_call" | custom-call | flops 9663676416 | bytes 28311552 | tf_op jit(solution)/shard_map/project_1/pallas_call | solution.py:118
  347.8 17.7 %far_2.1 = bf16[512,3328]{1,0:T(8,128)(2,1)} custom-call(bf16[512,10752]{1,0:T(8,128)(2,1)} %bitcast.6.q_ref.x_ref, bf16[512,3072]{1,0:T(8,128)(2,1)} %project_1.2.kv_ref, f32[3,128,128]{2,1,0:T(8,128)} %select_select_fusion.1.bias_ref, bf16[128,128]{1,0:T(8,128)(2,1)} %constant.62.clone.order_ref, ...), custom_call_target="tpu_custom_call", output_to_operand_aliasing={{}: (5, {})} | custom-call | flops 402653184 | bytes 7864320 | tf_op jit(solution)/shard_map/far_2/pallas_call | solution.py:221
  365.5 15.2 %project_0.2.kv_ref = bf16[4,128,3072]{2,1,0:T(8,128)(2,1)} custom-call(bf16[4,3,128,3072]{3,2,1,0:T(8,128)(2,1)} %bitcast.42, bf16[3072,3072]{1,0:T(8,128)(2,1)} %bitcast.51, bf16[128,128]{1,0:T(8,128)(2,1)} %constant.60.clone.order_ref), custom_call_target="tpu_custom_call" | custom-call | flops 9663676416 | bytes 28311552 | tf_op jit(solution)/shard_map/project_0/pallas_call | solution.py:118
  380.7 5.2 all-to-all-done.2
  387.6 4.1 all-to-all-start.4
  393.1 16.0 %near_part_1.1 = (f32[4,128,1536]{2,1,0:T(8,128)}, f32[4,128,128]{2,1,0:T(8,128)}) custom-call(bf16[4,3,128,1536]{3,2,1,0:T(8,128)(2,1)} %bitcast.33, bf16[4,128,3072]{2,1,0:T(8,128)(2,1)} %project_0.2.kv_ref, f32[3,4,128,128]{3,2,1,0:T(8,128)} %select_select_fusion.bias_ref, bf16[128,128]{1,0:T(8,128)(2,1)} %constant.62.clone.order_ref), custom_call_target="tpu_custom_call" | custom-call | flops 402653184 | bytes 7864320 | tf_op jit(solution)/shard_map/near_part_1/pallas_call | solution.py:270
  409.2 15.2 %project_0.3.kv_ref = bf16[512,3072]{1,0:T(8,128)(2,1)} custom-call(bf16[512,10752]{1,0:T(8,128)(2,1)} %bitcast.6.q_ref.x_ref, bf16[3072,3072]{1,0:T(8,128)(2,1)} %bitcast.52, bf16[128,128]{1,0:T(8,128)(2,1)} %constant.60.clone.order_ref), custom_call_target="tpu_custom_call" | custom-call | flops 9663676416 | bytes 28311552 | tf_op jit(solution)/shard_map/project_0/pallas_call | solution.py:118
  424.3 17.0 %near_part_2.1 = (f32[4,128,1536]{2,1,0:T(8,128)}, f32[4,128,128]{2,1,0:T(8,128)}) custom-call(bf16[4,3,128,1536]{3,2,1,0:T(8,128)(2,1)} %bitcast.34, bf16[512,3072]{1,0:T(8,128)(2,1)} %project_0.3.kv_ref, f32[3,4,128,128]{3,2,1,0:T(8,128)} %select_select_fusion.bias_ref, bf16[128,128]{1,0:T(8,128)(2,1)} %constant.62.clone.order_ref), custom_call_target="tpu_custom_call" | custom-call | flops 402653184 | bytes 7864320 | tf_op jit(solution)/shard_map/near_part_2/pallas_call | solution.py:270
  441.4 17.7 %far_1.1 = bf16[512,1664]{1,0:T(8,128)(2,1)} custom-call(bf16[512,10752]{1,0:T(8,128)(2,1)} %bitcast.6.q_ref.x_ref, bf16[512,3072]{1,0:T(8,128)(2,1)} %bitcast.39, f32[3,128,128]{2,1,0:T(8,128)} %select_select_fusion.1.bias_ref, bf16[128,128]{1,0:T(8,128)(2,1)} %constant.62.clone.order_ref, bf16[128,128]{1,0:T(8,128)(2,1)} %constant.63.clone.back_ref), custom_call_target="tpu_custom_call" | custom-call | flops 402653184 | bytes 7864320 | tf_op jit(solution)/shard_map/far_1/pallas_call | solution.py:221
  459.1 9.4 %all-to-all-done.4 = bf16[32,16,3328]{2,1,0:T(8,128)(2,1)S(1)} async-done(((bf16[32,16,3328]{2,1,0:T(8,128)(2,1)}), bf16[32,16,3328]{2,1,0:T(8,128)(2,1)S(1)}, u32[]{:S(2)}, u32[]{:S(2)}) %all-to-all-start.4) | async-done | bytes 3407904 | tf_op jit(solution)/shard_map/all_to_all | solution.py:350
  468.5 4.0 all-to-all-start.3
  472.6 15.2 %project_1.3.kv_ref = bf16[4,128,3072]{2,1,0:T(8,128)(2,1)} custom-call(bf16[4,3,128,3072]{3,2,1,0:T(8,128)(2,1)} %bitcast.43, bf16[3072,3072]{1,0:T(8,128)(2,1)} %bitcast.53, bf16[128,128]{1,0:T(8,128)(2,1)} %constant.60.clone.order_ref), custom_call_target="tpu_custom_call" | custom-call | flops 9663676416 | bytes 28311552 | tf_op jit(solution)/shard_map/project_1/pallas_call | solution.py:118
  487.8 16.1 %near_part_0.1 = (f32[4,128,1536]{2,1,0:T(8,128)}, f32[4,128,128]{2,1,0:T(8,128)}) custom-call(bf16[4,3,128,1536]{3,2,1,0:T(8,128)(2,1)} %bitcast.35, bf16[4,128,3072]{2,1,0:T(8,128)(2,1)} %project_1.3.kv_ref, f32[3,4,128,128]{3,2,1,0:T(8,128)} %select_select_fusion.bias_ref, bf16[128,128]{1,0:T(8,128)(2,1)} %constant.62.clone.order_ref), custom_call_target="tpu_custom_call" | custom-call | flops 402653184 | bytes 7864320 | tf_op jit(solution)/shard_map/near_part_0/pallas_call | solution.py:270
  503.9 6.1 %merge_0.1.rest_0_ = bf16[4,3,128,1536]{3,2,1,0:T(8,128)(2,1)} custom-call(bf16[512,3328]{1,0:T(8,128)(2,1)} %bitcast.37, f32[4,128,1536]{2,1,0:T(8,128)} %get-tuple-element.39.mean_ref, f32[4,128,128]{2,1,0:T(8,128)} %get-tuple-element.40.lse_ref, bf16[128,128]{1,0:T(8,128)(2,1)} %constant.61.clone.back_ref), custom_call_target="tpu_custom_call" | custom-call | flops 201326592 | bytes 7864320 | tf_op jit(solution)/shard_map/merge_0/pallas_call | solution.py:328
  510.0 6.1 %merge_2.1.rest_0_ = bf16[4,3,128,1536]{3,2,1,0:T(8,128)(2,1)} custom-call(bf16[512,3328]{1,0:T(8,128)(2,1)} %bitcast.38, f32[4,128,1536]{2,1,0:T(8,128)} %get-tuple-element.37.mean_ref, f32[4,128,128]{2,1,0:T(8,128)} %get-tuple-element.38.lse_ref, bf16[128,128]{1,0:T(8,128)(2,1)} %constant.61.clone.back_ref, ...), custom_call_target="tpu_custom_call", output_to_operand_aliasing={{}: (4, {})} | custom-call | flops 201326592 | bytes 7864320 | tf_op jit(solution)/shard_map/merge_2/pallas_call | solution.py:328
  516.1 6.1 %merge_1.1 = bf16[4,3,128,1536]{3,2,1,0:T(8,128)(2,1)} custom-call(bf16[512,1664]{1,0:T(8,128)(2,1)} %bitcast.18.far_ref, f32[4,128,1536]{2,1,0:T(8,128)} %get-tuple-element.34.mean_ref, f32[4,128,128]{2,1,0:T(8,128)} %get-tuple-element.35.lse_ref, bf16[128,128]{1,0:T(8,128)(2,1)} %constant.61.clone.back_ref, ...), custom_call_target="tpu_custom_call", output_to_operand_aliasing={{}: (4, {})} | custom-call | flops 201326592 | bytes 7864320 | tf_op jit(solution)/shard_map/merge_1/pallas_call | solution.py:328
  (28 shorter events, 11.5 us)
Async XLA Ops:
  6.5 55.2 %all-gather.6.cloned.1.call-start = ((), (), s32[]{:S(2)}) async-start(), calls=%async_computation.6 | async-start | bytes 2949120 | tf_op jit(solution)/shard_map/all_gather | solution.py:360
  11.0 18.8 %all-to-all-start = ((s32[32,1,12]{2,1,0:T(1,128)}), s32[32,1,12]{2,1,0:T(1,128)S(1)}, u32[]{:S(2)}, u32[]{:S(2)}) async-start(s32[32,1,12]{2,1,0:T(1,128)} %broadcast_select_fusion), calls=%async_computation | async-start | bytes 32768 | tf_op jit(solution)/shard_map/all_to_all | solution.py:350
  18.3 258.7 %all-gather.4.cloned.1.call-start = ((), (), s32[]{:S(2)}) async-start(), calls=%async_computation.5 | async-start | bytes 21233664 | tf_op jit(solution)/shard_map/all_gather | solution.py:362
  61.8 250.0 %all-to-all-start.1 = ((bf16[32,16,10752]{2,1,0:T(8,128)(2,1)}), bf16[32,16,10752]{2,1,0:T(8,128)(2,1)}, u32[]{:S(2)}, u32[]{:S(2)}) async-start(bf16[32,16,10752]{2,1,0:T(8,128)(2,1)} %bitcast.36), calls=%async_computation.1 | async-start | bytes 22020096 | tf_op jit(solution)/shard_map/all_to_all | solution.py:350
  311.7 74.2 %all-to-all-start.2 = ((bf16[32,16,3072]{2,1,0:T(8,128)(2,1)}), bf16[32,16,3072]{2,1,0:T(8,128)(2,1)S(1)}, u32[]{:S(2)}, u32[]{:S(2)}) async-start(bf16[32,16,3072]{2,1,0:T(8,128)(2,1)} %bitcast.45), calls=%async_computation.2 | async-start | bytes 6291456 | tf_op jit(solution)/shard_map/all_to_all | solution.py:350
  386.0 1.6 copy-start.1
  387.6 80.9 %all-to-all-start.4 = ((bf16[32,16,3328]{2,1,0:T(8,128)(2,1)}), bf16[32,16,3328]{2,1,0:T(8,128)(2,1)S(1)}, u32[]{:S(2)}, u32[]{:S(2)}) async-start(bf16[32,16,3328]{2,1,0:T(8,128)(2,1)} %bitcast.19), calls=%async_computation.4 | async-start | bytes 6815744 | tf_op jit(solution)/shard_map/all_to_all | solution.py:350
  468.5 19.2 %copy-start = (bf16[32,16,3328]{2,1,0:T(8,128)(2,1)}, bf16[32,16,3328]{2,1,0:T(8,128)(2,1)S(1)}, u32[]{:S(2)}) copy-start(bf16[32,16,3328]{2,1,0:T(8,128)(2,1)S(1)} %all-to-all-done.4) | copy-start | bytes 10223620
  468.5 47.6 %all-to-all-start.3 = ((bf16[32,16,1664]{2,1,0:T(8,128)(2,1)}), bf16[32,16,1664]{2,1,0:T(8,128)(2,1)}, u32[]{:S(2)}, u32[]{:S(2)}) async-start(bf16[32,16,1664]{2,1,0:T(8,128)(2,1)} %bitcast.44), calls=%async_computation.3 | async-start | bytes 3407872 | tf_op jit(solution)/shard_map/all_to_all | solution.py:350
Sparse Core Ops, SparseCore 0:
  8.9 52.7 all-gather.5
  63.6 213.3 all-gather.3

commit v6 on v4

--- a/solution.py
+++ b/solution.py
@@ -83,47 +83,64 @@
     )(tokens, queries, order)
 
 
-def project_kernel(x_ref, w_ref, order_ref, *out_refs):
-    out = jnp.dot(x_ref[...].reshape(-1, x_ref.shape[-1]), w_ref[...], preferred_element_type=F32)
-    out = out.astype(BF16)
-    tile = w_ref.shape[1]
-    home_ref = out_refs[0]
-    home_ref[...] = out.reshape(home_ref.shape)
-    if len(out_refs) > 1:
-        lines, res, _ = x_ref.shape
-        span = res // lines
-        by_line = out.reshape(lines, res, tile)
-        for i in range(lines):
-            rows = by_line[:, i * span : (i + 1) * span].reshape(res, tile)
-            out_refs[1][pl.ds(i * res, res), :] = pick(order_ref[...], rows)
+def project_kernel(parity_ref, x_ref, own_ref, other_ref, order_ref, *out_refs):
+    def put(w_ref):
+        out = jnp.dot(x_ref[...].reshape(-1, x_ref.shape[-1]), w_ref[...], preferred_element_type=F32)
+        out = out.astype(BF16)
+        tile = w_ref.shape[1]
+        home_ref = out_refs[0]
+        home_ref[...] = out.reshape(home_ref.shape)
+        if len(out_refs) > 1:
+            lines, res, _ = x_ref.shape
+            span = res // lines
+            by_line = out.reshape(lines, res, tile)
+            for i in range(lines):
+                rows = by_line[:, i * span : (i + 1) * span].reshape(res, tile)
+                out_refs[1][pl.ds(i * res, res), :] = pick(order_ref[...], rows)
+
+    first = pl.program_id(0) < pl.num_programs(0) // 2
+    pl.when(first)(lambda: put(own_ref))
+    pl.when(jnp.logical_not(first))(lambda: put(other_ref))
 
 
 def project(tokens, weight, order, plane, sent_width):
-    depth, width = weight.shape
+    parity, own, other = weight
+    depth, half = own.shape
+    width = 2 * half
     tile = 512
+    steps = half // tile
+
+    def column(n, parity_ref):
+        second = (n >= steps).astype(jnp.int32)
+        return (parity_ref[0] + second) % 2 * steps + n % steps
+
     if tokens.ndim == 4:
         lines, planes, res, _ = tokens.shape
-        x_spec = pl.BlockSpec((lines, None, res, depth), lambda n: (0, plane, 0, 0))
+        x_spec = pl.BlockSpec((lines, None, res, depth), lambda n, s: (0, plane, 0, 0))
         rows = lines * res
-        out_specs = [pl.BlockSpec((lines, res, tile), lambda n: (0, 0, n))]
+        out_specs = [pl.BlockSpec((lines, res, tile), lambda n, s: (0, 0, column(n, s)))]
         out_shape = [jax.ShapeDtypeStruct((lines, res, width), BF16)]
     else:
         rows = tokens.shape[0]
-        x_spec = pl.BlockSpec((rows, depth), lambda n: (0, plane))
-        out_specs = [pl.BlockSpec((rows, tile), lambda n: (0, n))]
+        x_spec = pl.BlockSpec((rows, depth), lambda n, s: (0, plane))
+        out_specs = [pl.BlockSpec((rows, tile), lambda n, s: (0, column(n, s)))]
         out_shape = [jax.ShapeDtypeStruct((rows, width), BF16)]
     if sent_width:
-        out_specs.append(pl.BlockSpec((rows, tile), lambda n: (0, n)))
+        out_specs.append(pl.BlockSpec((rows, tile), lambda n, s: (0, column(n, s))))
         out_shape.append(jax.ShapeDtypeStruct((rows, sent_width), BF16))
     return pl.pallas_call(
         project_kernel,
-        grid=(width // tile,),
-        in_specs=[
-            x_spec,
-            pl.BlockSpec((depth, tile), lambda n: (0, n)),
-            pl.BlockSpec(order.shape, lambda n: (0, 0)),
-        ],
-        out_specs=out_specs,
+        grid_spec=pltpu.PrefetchScalarGridSpec(
+            num_scalar_prefetch=1,
+            grid=(2 * steps,),
+            in_specs=[
+                x_spec,
+                pl.BlockSpec((depth, tile), lambda n, s: (0, jnp.minimum(n, steps - 1))),
+                pl.BlockSpec((depth, tile), lambda n, s: (0, jnp.maximum(n - steps, 0))),
+                pl.BlockSpec(order.shape, lambda n, s: (0, 0)),
+            ],
+            out_specs=out_specs,
+        ),
         out_shape=out_shape,
         cost_estimate=pl.CostEstimate(
             flops=2 * rows * depth * width,
@@ -131,7 +148,7 @@
             transcendentals=0,
         ),
         name=f"project_{plane}",
-    )(tokens, weight, order)
+    )(parity, tokens, own, other, order)
 
 
 def to_away(src_ref, order_ref, dst_ref):
@@ -350,17 +367,24 @@
     return lax.all_to_all(rows, "seq", split_axis=0, concat_axis=0, tiled=True)
 
 
-def gather_weight(shard, count, sent, codes):
+def gather_weights(key_weight, value_weight, count, sent, codes):
     outer = 1
     while outer * outer < count // 2:
         outer *= 2
     inner = count // outer
     across = [[o * inner + i for o in range(outer)] for i in range(inner)]
-    within = [[o * inner + i for i in range(inner)] for o in range(outer)]
-    blocks = lax.all_gather(shard[None], "seq", axis=0, tiled=True, axis_index_groups=across)
+    within = [[o * inner + c + i for i in range(0, inner, 2)] for o in range(outer) for c in range(2)]
+    swap = [(i, i ^ 1) for i in range(count)]
+    even = lax.axis_index("seq") % 2 == 0
+    mine = jnp.where(even, key_weight, value_weight)
+    got = lax.ppermute(jnp.where(even, value_weight, key_weight), "seq", swap)
+    block = jnp.stack([jnp.where(even, mine, got), jnp.where(even, got, mine)])
+    block = block.reshape(1, -1, key_weight.shape[-1])
+    blocks = lax.all_gather(block, "seq", axis=0, tiled=True, axis_index_groups=across)
     blocks, sent, codes = lax.optimization_barrier((blocks, sent, codes))
     blocks = lax.all_gather(blocks, "seq", axis=1, tiled=True, axis_index_groups=within)
-    return blocks.reshape(-1, shard.shape[-1]), sent, codes
+    own = blocks.reshape(-1, key_weight.shape[-1])
+    return own, lax.ppermute(own, "seq", swap), sent, codes
 
 
 def on_device(count, tokens, queries, key_weight, value_weight, halves):
@@ -381,7 +405,8 @@
     codes = exchange(sent_codes)
     token_planes = 2
     sent = order_sent(tokens, queries, to_sent, token_planes)
-    weight, sent, codes = gather_weight(jnp.concatenate([key_weight, value_weight], axis=1), count, sent, codes)
+    own, other, sent, codes = gather_weights(key_weight, value_weight, count, sent, codes)
+    weight = ((lax.axis_index("seq") % 2).astype(jnp.int32).reshape(1), own, other)
     codes = codes.reshape(res, planes).T
     far_bias = mask_bias(codes, res)
     home_half = jnp.arange(res) // (res // 2)
@@ -397,18 +422,18 @@
     merge = functools.partial(merge_parts, back=to_home, planes=planes)
     home_2, sent_2 = project(tokens, weight, to_sent, 2, 2 * width)
     (home_0,) = project(tokens, weight, to_sent, 0, 0)
-    sent_2, home_0 = lax.optimization_barrier((sent_2, home_0))
+    (home_1,) = project(tokens, weight, to_sent, 1, 0)
+    sent_2, home_0, home_1 = lax.optimization_barrier((sent_2, home_0, home_1))
     moved_2 = exchange(sent_2)
     (moved_1,) = project(moved, weight, to_sent, 1, 0)
-    (home_1,) = project(tokens, weight, to_sent, 1, 0)
     sent = far(kv=home_2, plane=0, slots=2)
     sent = far(kv=moved_1, plane=2, slot=1, slots=2, into=sent)
-    sent, home_1 = lax.optimization_barrier((sent, home_1))
+    near_1 = near(kv=home_0, plane=1)
+    sent, near_1 = lax.optimization_barrier((sent, near_1))
     far_02 = exchange(sent)
     (moved_0,) = project(moved, weight, to_sent, 0, 0)
     near_2 = near(kv=moved_0, plane=2)
-    near_1 = near(kv=home_0, plane=1)
-    sent, near_1, near_2 = lax.optimization_barrier((far(kv=moved_2, plane=1), near_1, near_2))
+    sent, near_2 = lax.optimization_barrier((far(kv=moved_2, plane=1), near_2))
     far_1 = exchange(sent)
     near_0 = near(kv=home_1, plane=0)
     out = merge(far_02, 0, near_0, plane=0, done=None)

time: 539 us -> 574 us (1.065)
  waiting for transfers between devices: 273 us -> 298 us
  Pallas kernels: 208 us -> 214 us
    ppermute x0 -> x2, waiting for transfers between devices: none -> 16.2 us  [the longest x1 15 us: gather_weights(): return (own, lax.ppermute(own, 'seq', swap), sent, codes)]
    all_to_all x5, waiting for transfers between devices: 29.9 us -> 39.4 us  [exchange(): return lax.all_to_all(rows, 'seq', split_axis=0, concat_axis=0, tiled=True)]
  transfers between devices with their start and end apart: 7 -> 9, of which waited for: 6 -> 7; matrix products, arithmetic and copies ran while one was open for 1% -> 1% of each run, Pallas kernels for 38% -> 36%
where the time goes in v6:
time: 574 us; the launch traced here: 572 us
  waiting for transfers between devices  298 us (52%)
  Pallas kernels  214 us (37%)
  starting transfers between devices  39 us (7%)
  between operations  13.5 us (2%)
  other arithmetic  5.98 us (1%)
    all_gather x1, waiting for transfers between devices, gather_weights(): lax.all_gather(blocks, 'seq', axis=1, tiled=True, axis_index_groups=within)  209 us
    pallas_call x5, Pallas kernels, project(): pl.pallas_call(project_kernel, grid_spec=pltpu.PrefetchScalarGridSpec(num...  82.4 us
    pallas_call x3, Pallas kernels, far_attention(): pl.pallas_call(functools.partial(far_kernel, moved_kv, column), grid=(1,)...  52.3 us
    pallas_call x3, Pallas kernels, near_part(): pl.pallas_call(part_kernel, grid=(1,), in_specs=[pl.BlockSpec((lines, Non...  49.4 us
    all_to_all x5, waiting for transfers between devices, exchange(): return lax.all_to_all(rows, 'seq', split_axis=0, concat_axis=0, tiled=True)  39.4 us
    all_to_all x5, starting transfers between devices, exchange(): return lax.all_to_all(rows, 'seq', split_axis=0, concat_axis=0, tiled=True)  38.4 us
    all_gather x1, waiting for transfers between devices, gather_weights(): lax.all_gather(block, 'seq', axis=0, tiled=True, axis_index_groups=across)  32.9 us
    pallas_call x3, Pallas kernels, merge_parts(): pl.pallas_call(merge_kernel, grid=(lines,), in_specs=in_specs, out_specs=...  18.4 us
  transfers between devices with their start and end apart: 9, of which 7 were waited for; matrix products, arithmetic and copies ran while one was open for 1% of the time, Pallas kernels for 36%

profile of v6, /device:TPU:0, one launch (start us, length us, event | category | flops | bytes accessed | tf_op | source)
XLA Modules:
  0.0 572.4 jit_solution(15186887651153286045)
XLA Ops:
  12.3 7.2 %all-to-all-start = ((s32[32,1,12]{2,1,0:T(1,128)}), s32[32,1,12]{2,1,0:T(1,128)S(1)}, u32[]{:S(2)}, u32[]{:S(2)}) async-start(s32[32,1,12]{2,1,0:T(1,128)} %broadcast_select_fusion.2), calls=%async_computation | async-start | bytes 32768 | tf_op jit(solution)/shard_map/all_to_all | solution.py:367
  19.6 11.5 %order_sent.1 = bf16[512,10752]{1,0:T(8,128)(2,1)} custom-call(bf16[4,3,128,3072]{3,2,1,0:T(8,128)(2,1)} %bitcast.45, bf16[4,3,128,1536]{3,2,1,0:T(8,128)(2,1)} %bitcast.37, bf16[128,128]{1,0:T(8,128)(2,1)} %constant.73.clone.order_ref), custom_call_target="tpu_custom_call" | custom-call | flops 1409286144 | bytes 22020096 | tf_op jit(solution)/shard_map/order_sent/pallas_call | solution.py:69
  31.1 32.9 %all-gather.3.cloned.1.call-done = bf16[4,192,1536]{2,1,0:T(8,128)(2,1)} async-done(((bf16[1,192,1536]{2,1,0:T(8,128)(2,1)}), bf16[4,192,1536]{2,1,0:T(8,128)(2,1)}) %all-gather.3.cloned.1.call-update) | async-done | bytes 2359312 | tf_op jit(solution)/shard_map/all_gather | solution.py:383
  67.8 209.1 %all-gather.5.cloned.1.call-done = bf16[4,768,1536]{2,1,0:T(8,128)(2,1)} async-done(((bf16[4,192,1536]{2,1,0:T(8,128)(2,1)}), bf16[4,768,1536]{2,1,0:T(8,128)(2,1)}) %all-gather.5.cloned.1.call-update) | async-done | bytes 9437200 | tf_op jit(solution)/shard_map/all_gather | solution.py:385
  276.9 15.0 %collective-permute-done.1.other_ref = bf16[3072,1536]{1,0:T(8,128)(2,1)} collective-permute-done((bf16[3072,1536]{1,0:T(8,128)(2,1)}, bf16[3072,1536]{1,0:T(8,128)(2,1)}, u32[]{:S(2)}, u32[]{:S(2)}) %collective-permute-start.1) | collective-permute-done | bytes 9437216 | tf_op jit(solution)/shard_map/ppermute | solution.py:387
  291.9 17.7 %project_2.1 = (bf16[4,128,3072]{2,1,0:T(8,128)(2,1)}, bf16[512,3072]{1,0:T(8,128)(2,1)}) custom-call(s32[1]{0:T(128)} %bitcast.9.parity_ref, bf16[4,3,128,3072]{3,2,1,0:T(8,128)(2,1)} %bitcast.46, bf16[3072,1536]{1,0:T(8,128)(2,1)} %bitcast.55, bf16[3072,1536]{1,0:T(8,128)(2,1)} %collective-permute-done.1.other_ref, bf16[128,128]{1,0:T(8,128)(2,1)} %constant.73.clone.order_ref), custom_call_target="tpu_custom_call" | custom-call | flops 9663676416 | bytes 28311552 | tf_op jit(solution)/shard_map/project_2/pallas_call | solution.py:131
  309.6 16.2 %project_0.2.kv_ref = bf16[4,128,3072]{2,1,0:T(8,128)(2,1)} custom-call(s32[1]{0:T(128)} %bitcast.9.parity_ref, bf16[4,3,128,3072]{3,2,1,0:T(8,128)(2,1)} %bitcast.47, bf16[3072,1536]{1,0:T(8,128)(2,1)} %bitcast.56, bf16[3072,1536]{1,0:T(8,128)(2,1)} %collective-permute-done.1.other_ref, bf16[128,128]{1,0:T(8,128)(2,1)} %constant.73.clone.order_ref), custom_call_target="tpu_custom_call" | custom-call | flops 9663676416 | bytes 28311552 | tf_op jit(solution)/shard_map/project_0/pallas_call | solution.py:131
  325.7 16.2 %project_1.2.kv_ref = bf16[4,128,3072]{2,1,0:T(8,128)(2,1)} custom-call(s32[1]{0:T(128)} %bitcast.9.parity_ref, bf16[4,3,128,3072]{3,2,1,0:T(8,128)(2,1)} %bitcast.48, bf16[3072,1536]{1,0:T(8,128)(2,1)} %bitcast.57, bf16[3072,1536]{1,0:T(8,128)(2,1)} %collective-permute-done.1.other_ref, bf16[128,128]{1,0:T(8,128)(2,1)} %constant.73.clone.order_ref), custom_call_target="tpu_custom_call" | custom-call | flops 9663676416 | bytes 28311552 | tf_op jit(solution)/shard_map/project_1/pallas_call | solution.py:131
  341.9 19.2 %all-to-all-start.2 = ((bf16[32,16,3072]{2,1,0:T(8,128)(2,1)}), bf16[32,16,3072]{2,1,0:T(8,128)(2,1)S(1)}, u32[]{:S(2)}, u32[]{:S(2)}) async-start(bf16[32,16,3072]{2,1,0:T(8,128)(2,1)} %bitcast.50), calls=%async_computation.2 | async-start | bytes 6291456 | tf_op jit(solution)/shard_map/all_to_all | solution.py:367
  363.7 16.9 %far_0.1.rest_0_ = bf16[512,3328]{1,0:T(8,128)(2,1)} custom-call(bf16[512,10752]{1,0:T(8,128)(2,1)} %bitcast.8.q_ref.x_ref, bf16[4,128,3072]{2,1,0:T(8,128)(2,1)} %get-tuple-element.33.kv_ref, f32[3,128,128]{2,1,0:T(8,128)} %select_select_fusion.1.bias_ref, bf16[128,128]{1,0:T(8,128)(2,1)} %constant.75.clone.order_ref, bf16[128,128]{1,0:T(8,128)(2,1)} %constant.76.clone.back_ref), custom_call_target="tpu_custom_call" | custom-call | flops 402653184 | bytes 7864320 | tf_op jit(solution)/shard_map/far_0/pallas_call | solution.py:238
  380.6 16.2 %project_1.3.kv_ref = bf16[512,3072]{1,0:T(8,128)(2,1)} custom-call(s32[1]{0:T(128)} %bitcast.9.parity_ref, bf16[512,10752]{1,0:T(8,128)(2,1)} %bitcast.8.q_ref.x_ref, bf16[3072,1536]{1,0:T(8,128)(2,1)} %bitcast.58, bf16[3072,1536]{1,0:T(8,128)(2,1)} %collective-permute-done.1.other_ref, bf16[128,128]{1,0:T(8,128)(2,1)} %constant.73.clone.order_ref), custom_call_target="tpu_custom_call" | custom-call | flops 9663676416 | bytes 28311552 | tf_op jit(solution)/shard_map/project_1/pallas_call | solution.py:131
  396.8 17.7 %far_2.1 = bf16[512,3328]{1,0:T(8,128)(2,1)} custom-call(bf16[512,10752]{1,0:T(8,128)(2,1)} %bitcast.8.q_ref.x_ref, bf16[512,3072]{1,0:T(8,128)(2,1)} %project_1.3.kv_ref, f32[3,128,128]{2,1,0:T(8,128)} %select_select_fusion.1.bias_ref, bf16[128,128]{1,0:T(8,128)(2,1)} %constant.75.clone.order_ref, ...), custom_call_target="tpu_custom_call", output_to_operand_aliasing={{}: (5, {})} | custom-call | flops 402653184 | bytes 7864320 | tf_op jit(solution)/shard_map/far_2/pallas_call | solution.py:238
  414.5 16.2 %near_part_1.1 = (f32[4,128,1536]{2,1,0:T(8,128)}, f32[4,128,128]{2,1,0:T(8,128)}) custom-call(bf16[4,3,128,1536]{3,2,1,0:T(8,128)(2,1)} %bitcast.38, bf16[4,128,3072]{2,1,0:T(8,128)(2,1)} %project_0.2.kv_ref, f32[3,4,128,128]{3,2,1,0:T(8,128)} %select_select_fusion.bias_ref, bf16[128,128]{1,0:T(8,128)(2,1)} %constant.75.clone.order_ref), custom_call_target="tpu_custom_call" | custom-call | flops 402653184 | bytes 7864320 | tf_op jit(solution)/shard_map/near_part_1/pallas_call | solution.py:287
  434.0 4.2 all-to-all-start.4
  438.2 16.2 %project_0.3.kv_ref = bf16[512,3072]{1,0:T(8,128)(2,1)} custom-call(s32[1]{0:T(128)} %bitcast.9.parity_ref, bf16[512,10752]{1,0:T(8,128)(2,1)} %bitcast.8.q_ref.x_ref, bf16[3072,1536]{1,0:T(8,128)(2,1)} %bitcast.59, bf16[3072,1536]{1,0:T(8,128)(2,1)} %collective-permute-done.1.other_ref, bf16[128,128]{1,0:T(8,128)(2,1)} %constant.73.clone.order_ref), custom_call_target="tpu_custom_call" | custom-call | flops 9663676416 | bytes 28311552 | tf_op jit(solution)/shard_map/project_0/pallas_call | solution.py:131
  454.4 17.1 %near_part_2.1 = (f32[4,128,1536]{2,1,0:T(8,128)}, f32[4,128,128]{2,1,0:T(8,128)}) custom-call(bf16[4,3,128,1536]{3,2,1,0:T(8,128)(2,1)} %bitcast.39, bf16[512,3072]{1,0:T(8,128)(2,1)} %project_0.3.kv_ref, f32[3,4,128,128]{3,2,1,0:T(8,128)} %select_select_fusion.bias_ref, bf16[128,128]{1,0:T(8,128)(2,1)} %constant.75.clone.order_ref), custom_call_target="tpu_custom_call" | custom-call | flops 402653184 | bytes 7864320 | tf_op jit(solution)/shard_map/near_part_2/pallas_call | solution.py:287
  471.5 17.7 %far_1.1 = bf16[512,1664]{1,0:T(8,128)(2,1)} custom-call(bf16[512,10752]{1,0:T(8,128)(2,1)} %bitcast.8.q_ref.x_ref, bf16[512,3072]{1,0:T(8,128)(2,1)} %bitcast.44, f32[3,128,128]{2,1,0:T(8,128)} %select_select_fusion.1.bias_ref, bf16[128,128]{1,0:T(8,128)(2,1)} %constant.75.clone.order_ref, bf16[128,128]{1,0:T(8,128)(2,1)} %constant.76.clone.back_ref), custom_call_target="tpu_custom_call" | custom-call | flops 402653184 | bytes 7864320 | tf_op jit(solution)/shard_map/far_1/pallas_call | solution.py:238
  489.2 25.9 %all-to-all-done.4 = bf16[32,16,3328]{2,1,0:T(8,128)(2,1)S(1)} async-done(((bf16[32,16,3328]{2,1,0:T(8,128)(2,1)}), bf16[32,16,3328]{2,1,0:T(8,128)(2,1)S(1)}, u32[]{:S(2)}, u32[]{:S(2)}) %all-to-all-start.4) | async-done | bytes 3407904 | tf_op jit(solution)/shard_map/all_to_all | solution.py:367
  515.1 4.0 all-to-all-start.3
  519.1 16.1 %near_part_0.1 = (f32[4,128,1536]{2,1,0:T(8,128)}, f32[4,128,128]{2,1,0:T(8,128)}) custom-call(bf16[4,3,128,1536]{3,2,1,0:T(8,128)(2,1)} %bitcast.40, bf16[4,128,3072]{2,1,0:T(8,128)(2,1)} %project_1.2.kv_ref, f32[3,4,128,128]{3,2,1,0:T(8,128)} %select_select_fusion.bias_ref, bf16[128,128]{1,0:T(8,128)(2,1)} %constant.75.clone.order_ref), custom_call_target="tpu_custom_call" | custom-call | flops 402653184 | bytes 7864320 | tf_op jit(solution)/shard_map/near_part_0/pallas_call | solution.py:287
  535.2 6.1 %merge_0.1.rest_0_ = bf16[4,3,128,1536]{3,2,1,0:T(8,128)(2,1)} custom-call(bf16[512,3328]{1,0:T(8,128)(2,1)} %bitcast.42, f32[4,128,1536]{2,1,0:T(8,128)} %get-tuple-element.43.mean_ref, f32[4,128,128]{2,1,0:T(8,128)} %get-tuple-element.44.lse_ref, bf16[128,128]{1,0:T(8,128)(2,1)} %constant.74.clone.back_ref), custom_call_target="tpu_custom_call" | custom-call | flops 201326592 | bytes 7864320 | tf_op jit(solution)/shard_map/merge_0/pallas_call | solution.py:345
  541.3 6.1 %merge_2.1.rest_0_ = bf16[4,3,128,1536]{3,2,1,0:T(8,128)(2,1)} custom-call(bf16[512,3328]{1,0:T(8,128)(2,1)} %bitcast.43, f32[4,128,1536]{2,1,0:T(8,128)} %get-tuple-element.40.mean_ref, f32[4,128,128]{2,1,0:T(8,128)} %get-tuple-element.41.lse_ref, bf16[128,128]{1,0:T(8,128)(2,1)} %constant.74.clone.back_ref, ...), custom_call_target="tpu_custom_call", output_to_operand_aliasing={{}: (4, {})} | custom-call | flops 201326592 | bytes 7864320 | tf_op jit(solution)/shard_map/merge_2/pallas_call | solution.py:345
  547.5 11.9 %all-to-all-done.3 = bf16[32,16,1664]{2,1,0:T(8,128)(2,1)} async-done(((bf16[32,16,1664]{2,1,0:T(8,128)(2,1)}), bf16[32,16,1664]{2,1,0:T(8,128)(2,1)}, u32[]{:S(2)}, u32[]{:S(2)}) %all-to-all-start.3) | async-done | bytes 1703968 | tf_op jit(solution)/shard_map/all_to_all | solution.py:367
  559.4 6.1 %merge_1.1 = bf16[4,3,128,1536]{3,2,1,0:T(8,128)(2,1)} custom-call(bf16[512,1664]{1,0:T(8,128)(2,1)} %bitcast.21.far_ref, f32[4,128,1536]{2,1,0:T(8,128)} %get-tuple-element.37.mean_ref, f32[4,128,128]{2,1,0:T(8,128)} %get-tuple-element.38.lse_ref, bf16[128,128]{1,0:T(8,128)(2,1)} %constant.74.clone.back_ref, ...), custom_call_target="tpu_custom_call", output_to_operand_aliasing={{}: (4, {})} | custom-call | flops 201326592 | bytes 7864320 | tf_op jit(solution)/shard_map/merge_1/pallas_call | solution.py:345
  (38 shorter events, 15.5 us)
Async XLA Ops:
  6.5 5.1 copy-start.3
  6.5 4.7 copy-start.2
  6.5 57.5 %all-gather.3.cloned.1.call-start = ((), (), s32[]{:S(2)}) async-start(), calls=%async_computation.5 | async-start | bytes 2949120 | tf_op jit(solution)/shard_map/all_gather | solution.py:383
  7.6 1.8 collective-permute-start
  12.3 18.7 %all-to-all-start = ((s32[32,1,12]{2,1,0:T(1,128)}), s32[32,1,12]{2,1,0:T(1,128)S(1)}, u32[]{:S(2)}, u32[]{:S(2)}) async-start(s32[32,1,12]{2,1,0:T(1,128)} %broadcast_select_fusion.2), calls=%async_computation | async-start | bytes 32768 | tf_op jit(solution)/shard_map/all_to_all | solution.py:367
  19.6 257.3 %all-gather.5.cloned.1.call-start = ((), (), s32[]{:S(2)}) async-start(), calls=%async_computation.6 | async-start | bytes 11796480 | tf_op jit(solution)/shard_map/all_gather | solution.py:385
  64.0 277.9 %all-to-all-start.1 = ((bf16[32,16,10752]{2,1,0:T(8,128)(2,1)}), bf16[32,16,10752]{2,1,0:T(8,128)(2,1)}, u32[]{:S(2)}, u32[]{:S(2)}) async-start(bf16[32,16,10752]{2,1,0:T(8,128)(2,1)} %bitcast.41), calls=%async_computation.1 | async-start | bytes 22020096 | tf_op jit(solution)/shard_map/all_to_all | solution.py:367
  276.9 15.0 %collective-permute-start.1 = (bf16[3072,1536]{1,0:T(8,128)(2,1)}, bf16[3072,1536]{1,0:T(8,128)(2,1)}, u32[]{:S(2)}, u32[]{:S(2)}) collective-permute-start(bf16[3072,1536]{1,0:T(8,128)(2,1)} %bitcast.54), channel_id=1, source_target_pairs={{0,1},{1,0},{2,3},{3,2},{4,5},{5,4},{6,7},{7,6},{8,9},{9,8},{10,11... | collective-permute-start | bytes 28311560 | tf_op jit(solution)/shard_map/ppermute | solution.py:387
  341.9 90.4 %all-to-all-start.2 = ((bf16[32,16,3072]{2,1,0:T(8,128)(2,1)}), bf16[32,16,3072]{2,1,0:T(8,128)(2,1)S(1)}, u32[]{:S(2)}, u32[]{:S(2)}) async-start(bf16[32,16,3072]{2,1,0:T(8,128)(2,1)} %bitcast.50), calls=%async_computation.2 | async-start | bytes 6291456 | tf_op jit(solution)/shard_map/all_to_all | solution.py:367
  432.3 1.6 copy-start.1
  434.0 81.1 %all-to-all-start.4 = ((bf16[32,16,3328]{2,1,0:T(8,128)(2,1)}), bf16[32,16,3328]{2,1,0:T(8,128)(2,1)S(1)}, u32[]{:S(2)}, u32[]{:S(2)}) async-start(bf16[32,16,3328]{2,1,0:T(8,128)(2,1)} %bitcast.22), calls=%async_computation.4 | async-start | bytes 6815744 | tf_op jit(solution)/shard_map/all_to_all | solution.py:367
  515.1 20.2 %copy-start = (bf16[32,16,3328]{2,1,0:T(8,128)(2,1)}, bf16[32,16,3328]{2,1,0:T(8,128)(2,1)S(1)}, u32[]{:S(2)}) copy-start(bf16[32,16,3328]{2,1,0:T(8,128)(2,1)S(1)} %all-to-all-done.4) | copy-start | bytes 10223620
  515.1 44.3 %all-to-all-start.3 = ((bf16[32,16,1664]{2,1,0:T(8,128)(2,1)}), bf16[32,16,1664]{2,1,0:T(8,128)(2,1)}, u32[]{:S(2)}, u32[]{:S(2)}) async-start(bf16[32,16,1664]{2,1,0:T(8,128)(2,1)} %bitcast.49), calls=%async_computation.3 | async-start | bytes 3407872 | tf_op jit(solution)/shard_map/all_to_all | solution.py:367
Sparse Core Ops, SparseCore 0:
  11.4 52.5 all-gather.2
  65.8 210.9 all-gather.4

commit v7 on v5

--- a/solution.py
+++ b/solution.py
@@ -83,7 +83,8 @@
     )(tokens, queries, order)
 
 
-def project_kernel(x_ref, w_ref, order_ref, *out_refs):
+def project_kernel(outs, x_ref, w_ref, order_ref, *rest):
+    out_refs = rest[-outs:]
     out = jnp.dot(x_ref[...].reshape(-1, x_ref.shape[-1]), w_ref[...], preferred_element_type=F32)
     out = out.astype(BF16)
     tile = w_ref.shape[1]
@@ -98,40 +99,48 @@
             out_refs[1][pl.ds(i * res, res), :] = pick(order_ref[...], rows)
 
 
-def project(tokens, weight, order, plane, sent_width):
+def project(tokens, weight, order, plane, sent_width, part=0, parts=1, into=None):
     depth, width = weight.shape
     tile = 512
+    steps = width // tile // parts
+    skip = part * steps
     if tokens.ndim == 4:
         lines, planes, res, _ = tokens.shape
         x_spec = pl.BlockSpec((lines, None, res, depth), lambda n: (0, plane, 0, 0))
         rows = lines * res
-        out_specs = [pl.BlockSpec((lines, res, tile), lambda n: (0, 0, n))]
+        out_specs = [pl.BlockSpec((lines, res, tile), lambda n: (0, 0, n + skip))]
         out_shape = [jax.ShapeDtypeStruct((lines, res, width), BF16)]
     else:
         rows = tokens.shape[0]
         x_spec = pl.BlockSpec((rows, depth), lambda n: (0, plane))
-        out_specs = [pl.BlockSpec((rows, tile), lambda n: (0, n))]
+        out_specs = [pl.BlockSpec((rows, tile), lambda n: (0, n + skip))]
         out_shape = [jax.ShapeDtypeStruct((rows, width), BF16)]
     if sent_width:
         out_specs.append(pl.BlockSpec((rows, tile), lambda n: (0, n)))
         out_shape.append(jax.ShapeDtypeStruct((rows, sent_width), BF16))
+    in_specs = [
+        x_spec,
+        pl.BlockSpec((depth, tile), lambda n: (0, n + skip)),
+        pl.BlockSpec(order.shape, lambda n: (0, 0)),
+    ]
+    args = (tokens, weight, order)
+    if into is not None:
+        in_specs.append(pl.BlockSpec(memory_space=pl.ANY))
+        args = args + (into,)
     return pl.pallas_call(
-        project_kernel,
-        grid=(width // tile,),
-        in_specs=[
-            x_spec,
-            pl.BlockSpec((depth, tile), lambda n: (0, n)),
-            pl.BlockSpec(order.shape, lambda n: (0, 0)),
-        ],
+        functools.partial(project_kernel, len(out_shape)),
+        grid=(steps,),
+        in_specs=in_specs,
         out_specs=out_specs,
         out_shape=out_shape,
         cost_estimate=pl.CostEstimate(
-            flops=2 * rows * depth * width,
-            bytes_accessed=2 * (rows * (depth + 2 * width) + depth * width),
+            flops=2 * rows * depth * width // parts,
+            bytes_accessed=2 * (rows * (depth + 2 * width) + depth * width) // parts,
             transcendentals=0,
         ),
+        input_output_aliases={} if into is None else {3: 0},
         name=f"project_{plane}",
-    )(tokens, weight, order)
+    )(*args)
 
 
 def to_away(src_ref, order_ref, dst_ref):
@@ -242,49 +251,51 @@
 
 
 def part_kernel(q_ref, kv_ref, bias_ref, order_ref, mean_ref, lse_ref, kv_s):
-    lines, res, width = q_ref.shape
-    heads = width // HDIM
+    _, res, width = q_ref.shape
+    lane = lax.broadcasted_iota(jnp.int32, (res, LANES), 1)
+    at_line = 0
     if len(kv_ref.shape) == 2:
-        to_away(kv_ref, order_ref, kv_s)
+        at_line = pl.program_id(0)
+        pl.when(at_line == 0)(lambda: to_away(kv_ref, order_ref, kv_s))
     else:
         kv_s = kv_ref
-    lane = lax.broadcasted_iota(jnp.int32, (res, LANES), 1)
-
-    def step(i, carry):
-        lse = jnp.zeros((res, LANES), F32)
-        for h in range(heads):
-            at = pl.ds(h * HDIM, HDIM)
-            out, peak, total = attend(
-                q_ref[i, :, at], kv_s[i, :, at], kv_s[i, :, pl.ds(width + h * HDIM, HDIM)], bias_ref[i]
-            )
-            mean_ref[i, :, at] = out * (1.0 / total)
-            lse = jnp.where(lane == h, peak + jnp.log(total), lse)
-        lse_ref[i] = lse
-        return carry
-
-    lax.fori_loop(0, lines, step, 0)
+    lse = jnp.zeros((res, LANES), F32)
+    for h in range(width // HDIM):
+        at = pl.ds(h * HDIM, HDIM)
+        out, peak, total = attend(
+            q_ref[0, :, at], kv_s[at_line, :, at], kv_s[at_line, :, pl.ds(width + h * HDIM, HDIM)], bias_ref[0]
+        )
+        mean_ref[0, :, at] = out * (1.0 / total)
+        lse = jnp.where(lane == h, peak + jnp.log(total), lse)
+    lse_ref[0] = lse
 
 
 def near_part(queries, kv, bias, order, plane):
     lines, planes, res, width = queries.shape
+    if kv.ndim == 2:
+        kv_spec = pl.BlockSpec(kv.shape, lambda i: (0, 0))
+        kv_shape = (lines, res, 2 * width)
+    else:
+        kv_spec = pl.BlockSpec((1, res, 2 * width), lambda i: (i, 0, 0))
+        kv_shape = (1, 16, LANES)
     return pl.pallas_call(
         part_kernel,
-        grid=(1,),
+        grid=(lines,),
         in_specs=[
-            pl.BlockSpec((lines, None, res, width), lambda n: (0, plane, 0, 0)),
-            pl.BlockSpec(kv.shape, lambda n: (0,) * kv.ndim),
-            pl.BlockSpec((None, lines, res, res), lambda n: (plane, 0, 0, 0)),
-            pl.BlockSpec((res, res), lambda n: (0, 0)),
+            pl.BlockSpec((1, None, res, width), lambda i: (i, plane, 0, 0)),
+            kv_spec,
+            pl.BlockSpec((None, 1, res, res), lambda i: (plane, i, 0, 0)),
+            pl.BlockSpec((res, res), lambda i: (0, 0)),
         ],
         out_specs=[
-            pl.BlockSpec((lines, res, width), lambda n: (0, 0, 0)),
-            pl.BlockSpec((lines, res, LANES), lambda n: (0, 0, 0)),
+            pl.BlockSpec((1, res, width), lambda i: (i, 0, 0)),
+            pl.BlockSpec((1, res, LANES), lambda i: (i, 0, 0)),
         ],
         out_shape=[
             jax.ShapeDtypeStruct((lines, res, width), F32),
             jax.ShapeDtypeStruct((lines, res, LANES), F32),
         ],
-        scratch_shapes=[pltpu.VMEM((lines, res, 2 * width) if kv.ndim == 2 else (1, 16, LANES), BF16)],
+        scratch_shapes=[pltpu.VMEM(kv_shape, BF16)],
         cost_estimate=attention_cost(lines, res, width),
         name=f"near_part_{plane}",
     )(queries, kv, bias, order)
@@ -406,9 +417,10 @@
     (moved_0,) = project(moved, weight, to_sent, 0, 0)
     near_2 = near(kv=moved_0, plane=2)
     near_1 = near(kv=home_0, plane=1)
-    sent, near_1, near_2 = lax.optimization_barrier((far(kv=moved_2, plane=1), near_1, near_2))
+    (home_1,) = project(tokens, weight, to_sent, 1, 0, 0, 2)
+    sent, near_1, near_2, home_1 = lax.optimization_barrier((far(kv=moved_2, plane=1), near_1, near_2, home_1))
     far_1 = exchange(sent)
-    (home_1,) = project(tokens, weight, to_sent, 1, 0)
+    (home_1,) = project(tokens, weight, to_sent, 1, 0, 1, 2, home_1)
     near_0 = near(kv=home_1, plane=0)
     out = merge(far_02, 0, near_0, plane=0, done=None)
     out = merge(far_02, 1, near_2, plane=2, done=out)

time: 531 us -> 528 us (level)
    pallas_call x8 -> x9, Pallas kernels: 126 us -> 125 us  [the longest x6 80.5 us: project(): pl.pallas_call(functools.partial(project_kernel, len(out_shape)), grid=(s...]
  transfers between devices with their start and end apart: 7 -> 7, of which waited for: 5 -> 6; matrix products, arithmetic and copies ran while one was open for 1% -> 1% of each run, Pallas kernels for 38% -> 38%
where the time goes in v7:
time: 528 us; the launch traced here: 526 us
  waiting for transfers between devices  274 us (52%)
  Pallas kernels  207 us (39%)
  starting transfers between devices  22.2 us (4%)
  between operations  13.5 us (3%)
  other arithmetic  5.62 us (1%)
    all_gather x1, waiting for transfers between devices, gather_weight(): lax.all_gather(blocks, 'seq', axis=1, tiled=True, axis_index_groups=within)  211 us
    pallas_call x6, Pallas kernels, project(): pl.pallas_call(functools.partial(project_kernel, len(out_shape)), grid=(s...  80.5 us
    pallas_call x3, Pallas kernels, far_attention(): pl.pallas_call(functools.partial(far_kernel, moved_kv, column), grid=(1,)...  52.3 us
    pallas_call x3, Pallas kernels, near_part(): pl.pallas_call(part_kernel, grid=(lines,), in_specs=[pl.BlockSpec((1, Non...  44.8 us
    all_gather x1, waiting for transfers between devices, gather_weight(): lax.all_gather(shard[None], 'seq', axis=0, tiled=True, axis_index_groups=...  31.9 us
    all_to_all x5, waiting for transfers between devices, exchange(): return lax.all_to_all(rows, 'seq', split_axis=0, concat_axis=0, tiled=True)  30.8 us
    all_to_all x5, starting transfers between devices, exchange(): return lax.all_to_all(rows, 'seq', split_axis=0, concat_axis=0, tiled=True)  22.2 us
    pallas_call x3, Pallas kernels, merge_parts(): pl.pallas_call(merge_kernel, grid=(lines,), in_specs=in_specs, out_specs=...  18.4 us
  transfers between devices with their start and end apart: 7, of which 6 were waited for; matrix products, arithmetic and copies ran while one was open for 1% of the time, Pallas kernels for 38%

profile of v7, /device:TPU:0, one launch (start us, length us, event | category | flops | bytes accessed | tf_op | source)
XLA Modules:
  0.0 526.0 jit_solution(8354796313716635997)
XLA Ops:
  11.0 7.3 %all-to-all-start = ((s32[32,1,12]{2,1,0:T(1,128)}), s32[32,1,12]{2,1,0:T(1,128)S(1)}, u32[]{:S(2)}, u32[]{:S(2)}) async-start(s32[32,1,12]{2,1,0:T(1,128)} %broadcast_select_fusion), calls=%async_computation | async-start | bytes 32768 | tf_op jit(solution)/shard_map/all_to_all | solution.py:361
  18.3 11.4 %order_sent.1 = bf16[512,10752]{1,0:T(8,128)(2,1)} custom-call(bf16[4,3,128,3072]{3,2,1,0:T(8,128)(2,1)} %bitcast.32, bf16[4,3,128,1536]{3,2,1,0:T(8,128)(2,1)} %bitcast.43, bf16[128,128]{1,0:T(8,128)(2,1)} %constant.60.clone.order_ref), custom_call_target="tpu_custom_call" | custom-call | flops 1409286144 | bytes 22020096 | tf_op jit(solution)/shard_map/order_sent/pallas_call | solution.py:69
  29.8 31.9 %all-gather.6.cloned.1.call-done = bf16[384,3072]{1,0:T(8,128)(2,1)} async-done(((bf16[96,3072]{1,0:T(8,128)(2,1)}), bf16[384,3072]{1,0:T(8,128)(2,1)}) %all-gather.6.cloned.1.call-update) | async-done | bytes 2359312 | tf_op jit(solution)/shard_map/all_gather | solution.py:371
  65.5 211.5 %all-gather.4.cloned.1.call-done = bf16[4,768,3072]{2,1,0:T(8,128)(2,1)} async-done(((bf16[4,96,3072]{2,1,0:T(8,128)(2,1)}), bf16[4,768,3072]{2,1,0:T(8,128)(2,1)}) %all-gather.4.cloned.1.call-update) | async-done | bytes 18874384 | tf_op jit(solution)/shard_map/all_gather | solution.py:373
  277.0 16.1 %project_2.1 = (bf16[4,128,3072]{2,1,0:T(8,128)(2,1)}, bf16[512,3072]{1,0:T(8,128)(2,1)}) custom-call(bf16[4,3,128,3072]{3,2,1,0:T(8,128)(2,1)} %bitcast.33, bf16[3072,3072]{1,0:T(8,128)(2,1)} %bitcast.37, bf16[128,128]{1,0:T(8,128)(2,1)} %constant.60.clone.order_ref), custom_call_target="tpu_custom_call" | custom-call | flops 9663676416 | bytes 28311552 | tf_op jit(solution)/shard_map/project_2/pallas_call | solution.py:130
  293.0 18.7 %all-to-all-done.1 = bf16[32,16,10752]{2,1,0:T(8,128)(2,1)} async-done(((bf16[32,16,10752]{2,1,0:T(8,128)(2,1)}), bf16[32,16,10752]{2,1,0:T(8,128)(2,1)}, u32[]{:S(2)}, u32[]{:S(2)}) %all-to-all-start.1) | async-done | bytes 11010080 | tf_op jit(solution)/shard_map/all_to_all | solution.py:361
  315.7 16.9 %far_0.1.rest_0_ = bf16[512,3328]{1,0:T(8,128)(2,1)} custom-call(bf16[512,10752]{1,0:T(8,128)(2,1)} %bitcast.6.q_ref.x_ref, bf16[4,128,3072]{2,1,0:T(8,128)(2,1)} %get-tuple-element.28.kv_ref, f32[3,128,128]{2,1,0:T(8,128)} %select_select_fusion.1.bias_ref, bf16[128,128]{1,0:T(8,128)(2,1)} %constant.62.clone.order_ref, bf16[128,128]{1,0:T(8,128)(2,1)} %constant.63.clone.back_ref), custom_call_target="tpu_custom_call" | custom-call | flops 402653184 | bytes 7864320 | tf_op jit(solution)/shard_map/far_0/pallas_call | solution.py:230
  332.6 15.2 %project_1.3.kv_ref = bf16[512,3072]{1,0:T(8,128)(2,1)} custom-call(bf16[512,10752]{1,0:T(8,128)(2,1)} %bitcast.6.q_ref.x_ref, bf16[3072,3072]{1,0:T(8,128)(2,1)} %bitcast.38, bf16[128,128]{1,0:T(8,128)(2,1)} %constant.60.clone.order_ref), custom_call_target="tpu_custom_call" | custom-call | flops 9663676416 | bytes 28311552 | tf_op jit(solution)/shard_map/project_1/pallas_call | solution.py:130
  347.8 17.7 %far_2.1 = bf16[512,3328]{1,0:T(8,128)(2,1)} custom-call(bf16[512,10752]{1,0:T(8,128)(2,1)} %bitcast.6.q_ref.x_ref, bf16[512,3072]{1,0:T(8,128)(2,1)} %project_1.3.kv_ref, f32[3,128,128]{2,1,0:T(8,128)} %select_select_fusion.1.bias_ref, bf16[128,128]{1,0:T(8,128)(2,1)} %constant.62.clone.order_ref, ...), custom_call_target="tpu_custom_call", output_to_operand_aliasing={{}: (5, {})} | custom-call | flops 402653184 | bytes 7864320 | tf_op jit(solution)/shard_map/far_2/pallas_call | solution.py:230
  365.5 15.2 %project_0.2.kv_ref = bf16[4,128,3072]{2,1,0:T(8,128)(2,1)} custom-call(bf16[4,3,128,3072]{3,2,1,0:T(8,128)(2,1)} %bitcast.34, bf16[3072,3072]{1,0:T(8,128)(2,1)} %bitcast.39, bf16[128,128]{1,0:T(8,128)(2,1)} %constant.60.clone.order_ref), custom_call_target="tpu_custom_call" | custom-call | flops 9663676416 | bytes 28311552 | tf_op jit(solution)/shard_map/project_0/pallas_call | solution.py:130
  380.7 5.2 all-to-all-done.2
  387.6 4.1 all-to-all-start.4
  393.1 14.4 %near_part_1.1 = (f32[4,128,1536]{2,1,0:T(8,128)}, f32[4,128,128]{2,1,0:T(8,128)}) custom-call(bf16[4,3,128,1536]{3,2,1,0:T(8,128)(2,1)} %bitcast.44, bf16[4,128,3072]{2,1,0:T(8,128)(2,1)} %project_0.2.kv_ref, f32[3,4,128,128]{3,2,1,0:T(8,128)} %select_select_fusion.bias_ref, bf16[128,128]{1,0:T(8,128)(2,1)} %constant.62.clone.order_ref), custom_call_target="tpu_custom_call" | custom-call | flops 402653184 | bytes 7864320 | tf_op jit(solution)/shard_map/near_part_1/pallas_call | solution.py:281
  407.5 15.2 %project_0.3.kv_ref = bf16[512,3072]{1,0:T(8,128)(2,1)} custom-call(bf16[512,10752]{1,0:T(8,128)(2,1)} %bitcast.6.q_ref.x_ref, bf16[3072,3072]{1,0:T(8,128)(2,1)} %bitcast.40, bf16[128,128]{1,0:T(8,128)(2,1)} %constant.60.clone.order_ref), custom_call_target="tpu_custom_call" | custom-call | flops 9663676416 | bytes 28311552 | tf_op jit(solution)/shard_map/project_0/pallas_call | solution.py:130
  422.7 16.0 %near_part_2.1 = (f32[4,128,1536]{2,1,0:T(8,128)}, f32[4,128,128]{2,1,0:T(8,128)}) custom-call(bf16[4,3,128,1536]{3,2,1,0:T(8,128)(2,1)} %bitcast.45, bf16[512,3072]{1,0:T(8,128)(2,1)} %project_0.3.kv_ref, f32[3,4,128,128]{3,2,1,0:T(8,128)} %select_select_fusion.bias_ref, bf16[128,128]{1,0:T(8,128)(2,1)} %constant.62.clone.order_ref), custom_call_target="tpu_custom_call" | custom-call | flops 402653184 | bytes 7864320 | tf_op jit(solution)/shard_map/near_part_2/pallas_call | solution.py:281
  438.7 9.4 %project_1.4.rest_0_ = bf16[4,128,3072]{2,1,0:T(8,128)(2,1)} custom-call(bf16[4,3,128,3072]{3,2,1,0:T(8,128)(2,1)} %bitcast.35, bf16[3072,3072]{1,0:T(8,128)(2,1)} %bitcast.41, bf16[128,128]{1,0:T(8,128)(2,1)} %constant.60.clone.order_ref), custom_call_target="tpu_custom_call" | custom-call | flops 4831838208 | bytes 14155776 | tf_op jit(solution)/shard_map/project_1/pallas_call | solution.py:130
  448.1 17.8 %far_1.1 = bf16[512,1664]{1,0:T(8,128)(2,1)} custom-call(bf16[512,10752]{1,0:T(8,128)(2,1)} %bitcast.6.q_ref.x_ref, bf16[512,3072]{1,0:T(8,128)(2,1)} %bitcast.50, f32[3,128,128]{2,1,0:T(8,128)} %select_select_fusion.1.bias_ref, bf16[128,128]{1,0:T(8,128)(2,1)} %constant.62.clone.order_ref, bf16[128,128]{1,0:T(8,128)(2,1)} %constant.63.clone.back_ref), custom_call_target="tpu_custom_call" | custom-call | flops 402653184 | bytes 7864320 | tf_op jit(solution)/shard_map/far_1/pallas_call | solution.py:230
  468.5 4.3 all-to-all-start.3
  472.8 9.4 %project_1.5.kv_ref = bf16[4,128,3072]{2,1,0:T(8,128)(2,1)} custom-call(bf16[4,3,128,3072]{3,2,1,0:T(8,128)(2,1)} %bitcast.36, bf16[3072,3072]{1,0:T(8,128)(2,1)} %bitcast.42, bf16[128,128]{1,0:T(8,128)(2,1)} %constant.60.clone.order_ref, bf16[4,128,3072]{2,1,0:T(8,128)(2,1)} %project_1.4.rest_0_), custom_call_target="tpu_custom_call", output_to_operand_aliasing={{}: (3, {})} | custom-call | flops 4831838208 | bytes 14155776 | tf_op jit(solution)/shard_map/project_1/pallas_call | solution.py:130
  482.2 14.3 %near_part_0.1 = (f32[4,128,1536]{2,1,0:T(8,128)}, f32[4,128,128]{2,1,0:T(8,128)}) custom-call(bf16[4,3,128,1536]{3,2,1,0:T(8,128)(2,1)} %bitcast.46, bf16[4,128,3072]{2,1,0:T(8,128)(2,1)} %project_1.5.kv_ref, f32[3,4,128,128]{3,2,1,0:T(8,128)} %select_select_fusion.bias_ref, bf16[128,128]{1,0:T(8,128)(2,1)} %constant.62.clone.order_ref), custom_call_target="tpu_custom_call" | custom-call | flops 402653184 | bytes 7864320 | tf_op jit(solution)/shard_map/near_part_0/pallas_call | solution.py:281
  496.6 6.1 %merge_0.1.rest_0_ = bf16[4,3,128,1536]{3,2,1,0:T(8,128)(2,1)} custom-call(bf16[512,3328]{1,0:T(8,128)(2,1)} %bitcast.48, f32[4,128,1536]{2,1,0:T(8,128)} %get-tuple-element.41.mean_ref, f32[4,128,128]{2,1,0:T(8,128)} %get-tuple-element.42.lse_ref, bf16[128,128]{1,0:T(8,128)(2,1)} %constant.61.clone.back_ref), custom_call_target="tpu_custom_call" | custom-call | flops 201326592 | bytes 7864320 | tf_op jit(solution)/shard_map/merge_0/pallas_call | solution.py:339
  502.7 6.1 %merge_2.1.rest_0_ = bf16[4,3,128,1536]{3,2,1,0:T(8,128)(2,1)} custom-call(bf16[512,3328]{1,0:T(8,128)(2,1)} %bitcast.49, f32[4,128,1536]{2,1,0:T(8,128)} %get-tuple-element.38.mean_ref, f32[4,128,128]{2,1,0:T(8,128)} %get-tuple-element.39.lse_ref, bf16[128,128]{1,0:T(8,128)(2,1)} %constant.61.clone.back_ref, ...), custom_call_target="tpu_custom_call", output_to_operand_aliasing={{}: (4, {})} | custom-call | flops 201326592 | bytes 7864320 | tf_op jit(solution)/shard_map/merge_2/pallas_call | solution.py:339
  508.8 4.2 all-to-all-done.3
  513.1 6.1 %merge_1.1 = bf16[4,3,128,1536]{3,2,1,0:T(8,128)(2,1)} custom-call(bf16[512,1664]{1,0:T(8,128)(2,1)} %bitcast.18.far_ref, f32[4,128,1536]{2,1,0:T(8,128)} %get-tuple-element.35.mean_ref, f32[4,128,128]{2,1,0:T(8,128)} %get-tuple-element.36.lse_ref, bf16[128,128]{1,0:T(8,128)(2,1)} %constant.61.clone.back_ref, ...), custom_call_target="tpu_custom_call", output_to_operand_aliasing={{}: (4, {})} | custom-call | flops 201326592 | bytes 7864320 | tf_op jit(solution)/shard_map/merge_1/pallas_call | solution.py:339
  (29 shorter events, 17.8 us)
Async XLA Ops:
  6.5 55.2 %all-gather.6.cloned.1.call-start = ((), (), s32[]{:S(2)}) async-start(), calls=%async_computation.6 | async-start | bytes 2949120 | tf_op jit(solution)/shard_map/all_gather | solution.py:371
  11.0 18.8 %all-to-all-start = ((s32[32,1,12]{2,1,0:T(1,128)}), s32[32,1,12]{2,1,0:T(1,128)S(1)}, u32[]{:S(2)}, u32[]{:S(2)}) async-start(s32[32,1,12]{2,1,0:T(1,128)} %broadcast_select_fusion), calls=%async_computation | async-start | bytes 32768 | tf_op jit(solution)/shard_map/all_to_all | solution.py:361
  18.3 258.7 %all-gather.4.cloned.1.call-start = ((), (), s32[]{:S(2)}) async-start(), calls=%async_computation.5 | async-start | bytes 21233664 | tf_op jit(solution)/shard_map/all_gather | solution.py:373
  61.8 250.0 %all-to-all-start.1 = ((bf16[32,16,10752]{2,1,0:T(8,128)(2,1)}), bf16[32,16,10752]{2,1,0:T(8,128)(2,1)}, u32[]{:S(2)}, u32[]{:S(2)}) async-start(bf16[32,16,10752]{2,1,0:T(8,128)(2,1)} %bitcast.47), calls=%async_computation.1 | async-start | bytes 22020096 | tf_op jit(solution)/shard_map/all_to_all | solution.py:361
  311.7 74.2 %all-to-all-start.2 = ((bf16[32,16,3072]{2,1,0:T(8,128)(2,1)}), bf16[32,16,3072]{2,1,0:T(8,128)(2,1)S(1)}, u32[]{:S(2)}, u32[]{:S(2)}) async-start(bf16[32,16,3072]{2,1,0:T(8,128)(2,1)} %bitcast.52), calls=%async_computation.2 | async-start | bytes 6291456 | tf_op jit(solution)/shard_map/all_to_all | solution.py:361
  386.0 1.6 copy-start.1
  387.6 80.9 %all-to-all-start.4 = ((bf16[32,16,3328]{2,1,0:T(8,128)(2,1)}), bf16[32,16,3328]{2,1,0:T(8,128)(2,1)S(1)}, u32[]{:S(2)}, u32[]{:S(2)}) async-start(bf16[32,16,3328]{2,1,0:T(8,128)(2,1)} %bitcast.19), calls=%async_computation.4 | async-start | bytes 6815744 | tf_op jit(solution)/shard_map/all_to_all | solution.py:361
  468.5 13.7 %copy-start = (bf16[32,16,3328]{2,1,0:T(8,128)(2,1)}, bf16[32,16,3328]{2,1,0:T(8,128)(2,1)S(1)}, u32[]{:S(2)}) copy-start(bf16[32,16,3328]{2,1,0:T(8,128)(2,1)S(1)} %all-to-all-done.4) | copy-start | bytes 10223620
  468.5 44.5 %all-to-all-start.3 = ((bf16[32,16,1664]{2,1,0:T(8,128)(2,1)}), bf16[32,16,1664]{2,1,0:T(8,128)(2,1)}, u32[]{:S(2)}, u32[]{:S(2)}) async-start(bf16[32,16,1664]{2,1,0:T(8,128)(2,1)} %bitcast.51), calls=%async_computation.3 | async-start | bytes 3407872 | tf_op jit(solution)/shard_map/all_to_all | solution.py:361
Sparse Core Ops, SparseCore 0:
  8.9 52.7 all-gather.5
  63.6 213.3 all-gather.3

commit v8 on v7

--- a/solution.py
+++ b/solution.py
@@ -311,14 +311,12 @@
     top = jnp.maximum(near_lse, far_lse)
     near_w = jnp.exp(near_lse - top)
     far_w = jnp.exp(far_lse - top)
-    scale = 1.0 / (near_w + far_w)
-    near_w = near_w * scale
-    far_w = far_w * scale
+    near_w = near_w * (1.0 / (near_w + far_w))
     for h in range(width // HDIM):
         at = pl.ds(h * HDIM, HDIM)
         near = mean_ref[:, :, at].reshape(res, HDIM)
         far_h = far[:, h * HDIM : (h + 1) * HDIM].astype(F32)
-        mixed = near * near_w[:, h : h + 1] + far_h * far_w[:, h : h + 1]
+        mixed = far_h + (near - far_h) * near_w[:, h : h + 1]
         out_ref[:, :, at] = mixed.astype(BF16).reshape(lines, span, HDIM)
 
 

time: 528 us -> 527 us (level)
  no operation moved by 1% of the time
where the time goes in v8:
time: 527 us; the launch traced here: 525 us
  waiting for transfers between devices  275 us (52%)
  Pallas kernels  206 us (39%)
  starting transfers between devices  22.2 us (4%)
  between operations  13.5 us (3%)
  other arithmetic  5.62 us (1%)
    all_gather x1, waiting for transfers between devices, gather_weight(): lax.all_gather(blocks, 'seq', axis=1, tiled=True, axis_index_groups=within)  211 us
    pallas_call x6, Pallas kernels, project(): pl.pallas_call(functools.partial(project_kernel, len(out_shape)), grid=(s...  80.5 us
    pallas_call x3, Pallas kernels, far_attention(): pl.pallas_call(functools.partial(far_kernel, moved_kv, column), grid=(1,)...  52.3 us
    pallas_call x3, Pallas kernels, near_part(): pl.pallas_call(part_kernel, grid=(lines,), in_specs=[pl.BlockSpec((1, Non...  44.8 us
    all_to_all x5, waiting for transfers between devices, exchange(): return lax.all_to_all(rows, 'seq', split_axis=0, concat_axis=0, tiled=True)  32 us
    all_gather x1, waiting for transfers between devices, gather_weight(): lax.all_gather(shard[None], 'seq', axis=0, tiled=True, axis_index_groups=...  31.9 us
    all_to_all x5, starting transfers between devices, exchange(): return lax.all_to_all(rows, 'seq', split_axis=0, concat_axis=0, tiled=True)  22.2 us
    pallas_call x3, Pallas kernels, merge_parts(): pl.pallas_call(merge_kernel, grid=(lines,), in_specs=in_specs, out_specs=...  16.6 us
  transfers between devices with their start and end apart: 7, of which 6 were waited for; matrix products, arithmetic and copies ran while one was open for 1% of the time, Pallas kernels for 38%

profile of v8, /device:TPU:0, one launch (start us, length us, event | category | flops | bytes accessed | tf_op | source)
XLA Modules:
  0.0 525.4 jit_solution(5128563105776056711)
XLA Ops:
  11.0 7.3 %all-to-all-start = ((s32[32,1,12]{2,1,0:T(1,128)}), s32[32,1,12]{2,1,0:T(1,128)S(1)}, u32[]{:S(2)}, u32[]{:S(2)}) async-start(s32[32,1,12]{2,1,0:T(1,128)} %broadcast_select_fusion), calls=%async_computation | async-start | bytes 32768 | tf_op jit(solution)/shard_map/all_to_all | solution.py:359
  18.3 11.4 %order_sent.1 = bf16[512,10752]{1,0:T(8,128)(2,1)} custom-call(bf16[4,3,128,3072]{3,2,1,0:T(8,128)(2,1)} %bitcast.32, bf16[4,3,128,1536]{3,2,1,0:T(8,128)(2,1)} %bitcast.43, bf16[128,128]{1,0:T(8,128)(2,1)} %constant.60.clone.order_ref), custom_call_target="tpu_custom_call" | custom-call | flops 1409286144 | bytes 22020096 | tf_op jit(solution)/shard_map/order_sent/pallas_call | solution.py:69
  29.8 31.9 %all-gather.6.cloned.1.call-done = bf16[384,3072]{1,0:T(8,128)(2,1)} async-done(((bf16[96,3072]{1,0:T(8,128)(2,1)}), bf16[384,3072]{1,0:T(8,128)(2,1)}) %all-gather.6.cloned.1.call-update) | async-done | bytes 2359312 | tf_op jit(solution)/shard_map/all_gather | solution.py:369
  65.5 211.5 %all-gather.4.cloned.1.call-done = bf16[4,768,3072]{2,1,0:T(8,128)(2,1)} async-done(((bf16[4,96,3072]{2,1,0:T(8,128)(2,1)}), bf16[4,768,3072]{2,1,0:T(8,128)(2,1)}) %all-gather.4.cloned.1.call-update) | async-done | bytes 18874384 | tf_op jit(solution)/shard_map/all_gather | solution.py:371
  277.0 16.1 %project_2.1 = (bf16[4,128,3072]{2,1,0:T(8,128)(2,1)}, bf16[512,3072]{1,0:T(8,128)(2,1)}) custom-call(bf16[4,3,128,3072]{3,2,1,0:T(8,128)(2,1)} %bitcast.33, bf16[3072,3072]{1,0:T(8,128)(2,1)} %bitcast.37, bf16[128,128]{1,0:T(8,128)(2,1)} %constant.60.clone.order_ref), custom_call_target="tpu_custom_call" | custom-call | flops 9663676416 | bytes 28311552 | tf_op jit(solution)/shard_map/project_2/pallas_call | solution.py:130
  293.0 18.7 %all-to-all-done.1 = bf16[32,16,10752]{2,1,0:T(8,128)(2,1)} async-done(((bf16[32,16,10752]{2,1,0:T(8,128)(2,1)}), bf16[32,16,10752]{2,1,0:T(8,128)(2,1)}, u32[]{:S(2)}, u32[]{:S(2)}) %all-to-all-start.1) | async-done | bytes 11010080 | tf_op jit(solution)/shard_map/all_to_all | solution.py:359
  315.7 16.9 %far_0.1.rest_0_ = bf16[512,3328]{1,0:T(8,128)(2,1)} custom-call(bf16[512,10752]{1,0:T(8,128)(2,1)} %bitcast.6.q_ref.x_ref, bf16[4,128,3072]{2,1,0:T(8,128)(2,1)} %get-tuple-element.28.kv_ref, f32[3,128,128]{2,1,0:T(8,128)} %select_select_fusion.1.bias_ref, bf16[128,128]{1,0:T(8,128)(2,1)} %constant.62.clone.order_ref, bf16[128,128]{1,0:T(8,128)(2,1)} %constant.63.clone.back_ref), custom_call_target="tpu_custom_call" | custom-call | flops 402653184 | bytes 7864320 | tf_op jit(solution)/shard_map/far_0/pallas_call | solution.py:230
  332.6 15.2 %project_1.3.kv_ref = bf16[512,3072]{1,0:T(8,128)(2,1)} custom-call(bf16[512,10752]{1,0:T(8,128)(2,1)} %bitcast.6.q_ref.x_ref, bf16[3072,3072]{1,0:T(8,128)(2,1)} %bitcast.38, bf16[128,128]{1,0:T(8,128)(2,1)} %constant.60.clone.order_ref), custom_call_target="tpu_custom_call" | custom-call | flops 9663676416 | bytes 28311552 | tf_op jit(solution)/shard_map/project_1/pallas_call | solution.py:130
  347.8 17.7 %far_2.1 = bf16[512,3328]{1,0:T(8,128)(2,1)} custom-call(bf16[512,10752]{1,0:T(8,128)(2,1)} %bitcast.6.q_ref.x_ref, bf16[512,3072]{1,0:T(8,128)(2,1)} %project_1.3.kv_ref, f32[3,128,128]{2,1,0:T(8,128)} %select_select_fusion.1.bias_ref, bf16[128,128]{1,0:T(8,128)(2,1)} %constant.62.clone.order_ref, ...), custom_call_target="tpu_custom_call", output_to_operand_aliasing={{}: (5, {})} | custom-call | flops 402653184 | bytes 7864320 | tf_op jit(solution)/shard_map/far_2/pallas_call | solution.py:230
  365.5 15.2 %project_0.2.kv_ref = bf16[4,128,3072]{2,1,0:T(8,128)(2,1)} custom-call(bf16[4,3,128,3072]{3,2,1,0:T(8,128)(2,1)} %bitcast.34, bf16[3072,3072]{1,0:T(8,128)(2,1)} %bitcast.39, bf16[128,128]{1,0:T(8,128)(2,1)} %constant.60.clone.order_ref), custom_call_target="tpu_custom_call" | custom-call | flops 9663676416 | bytes 28311552 | tf_op jit(solution)/shard_map/project_0/pallas_call | solution.py:130
  380.7 5.2 all-to-all-done.2
  387.6 4.1 all-to-all-start.4
  393.1 14.4 %near_part_1.1 = (f32[4,128,1536]{2,1,0:T(8,128)}, f32[4,128,128]{2,1,0:T(8,128)}) custom-call(bf16[4,3,128,1536]{3,2,1,0:T(8,128)(2,1)} %bitcast.44, bf16[4,128,3072]{2,1,0:T(8,128)(2,1)} %project_0.2.kv_ref, f32[3,4,128,128]{3,2,1,0:T(8,128)} %select_select_fusion.bias_ref, bf16[128,128]{1,0:T(8,128)(2,1)} %constant.62.clone.order_ref), custom_call_target="tpu_custom_call" | custom-call | flops 402653184 | bytes 7864320 | tf_op jit(solution)/shard_map/near_part_1/pallas_call | solution.py:281
  407.5 15.2 %project_0.3.kv_ref = bf16[512,3072]{1,0:T(8,128)(2,1)} custom-call(bf16[512,10752]{1,0:T(8,128)(2,1)} %bitcast.6.q_ref.x_ref, bf16[3072,3072]{1,0:T(8,128)(2,1)} %bitcast.40, bf16[128,128]{1,0:T(8,128)(2,1)} %constant.60.clone.order_ref), custom_call_target="tpu_custom_call" | custom-call | flops 9663676416 | bytes 28311552 | tf_op jit(solution)/shard_map/project_0/pallas_call | solution.py:130
  422.7 16.0 %near_part_2.1 = (f32[4,128,1536]{2,1,0:T(8,128)}, f32[4,128,128]{2,1,0:T(8,128)}) custom-call(bf16[4,3,128,1536]{3,2,1,0:T(8,128)(2,1)} %bitcast.45, bf16[512,3072]{1,0:T(8,128)(2,1)} %project_0.3.kv_ref, f32[3,4,128,128]{3,2,1,0:T(8,128)} %select_select_fusion.bias_ref, bf16[128,128]{1,0:T(8,128)(2,1)} %constant.62.clone.order_ref), custom_call_target="tpu_custom_call" | custom-call | flops 402653184 | bytes 7864320 | tf_op jit(solution)/shard_map/near_part_2/pallas_call | solution.py:281
  438.7 9.4 %project_1.4.rest_0_ = bf16[4,128,3072]{2,1,0:T(8,128)(2,1)} custom-call(bf16[4,3,128,3072]{3,2,1,0:T(8,128)(2,1)} %bitcast.35, bf16[3072,3072]{1,0:T(8,128)(2,1)} %bitcast.41, bf16[128,128]{1,0:T(8,128)(2,1)} %constant.60.clone.order_ref), custom_call_target="tpu_custom_call" | custom-call | flops 4831838208 | bytes 14155776 | tf_op jit(solution)/shard_map/project_1/pallas_call | solution.py:130
  448.1 17.8 %far_1.1 = bf16[512,1664]{1,0:T(8,128)(2,1)} custom-call(bf16[512,10752]{1,0:T(8,128)(2,1)} %bitcast.6.q_ref.x_ref, bf16[512,3072]{1,0:T(8,128)(2,1)} %bitcast.50, f32[3,128,128]{2,1,0:T(8,128)} %select_select_fusion.1.bias_ref, bf16[128,128]{1,0:T(8,128)(2,1)} %constant.62.clone.order_ref, bf16[128,128]{1,0:T(8,128)(2,1)} %constant.63.clone.back_ref), custom_call_target="tpu_custom_call" | custom-call | flops 402653184 | bytes 7864320 | tf_op jit(solution)/shard_map/far_1/pallas_call | solution.py:230
  468.5 4.3 all-to-all-start.3
  472.8 9.4 %project_1.5.kv_ref = bf16[4,128,3072]{2,1,0:T(8,128)(2,1)} custom-call(bf16[4,3,128,3072]{3,2,1,0:T(8,128)(2,1)} %bitcast.36, bf16[3072,3072]{1,0:T(8,128)(2,1)} %bitcast.42, bf16[128,128]{1,0:T(8,128)(2,1)} %constant.60.clone.order_ref, bf16[4,128,3072]{2,1,0:T(8,128)(2,1)} %project_1.4.rest_0_), custom_call_target="tpu_custom_call", output_to_operand_aliasing={{}: (3, {})} | custom-call | flops 4831838208 | bytes 14155776 | tf_op jit(solution)/shard_map/project_1/pallas_call | solution.py:130
  482.2 14.3 %near_part_0.1 = (f32[4,128,1536]{2,1,0:T(8,128)}, f32[4,128,128]{2,1,0:T(8,128)}) custom-call(bf16[4,3,128,1536]{3,2,1,0:T(8,128)(2,1)} %bitcast.46, bf16[4,128,3072]{2,1,0:T(8,128)(2,1)} %project_1.5.kv_ref, f32[3,4,128,128]{3,2,1,0:T(8,128)} %select_select_fusion.bias_ref, bf16[128,128]{1,0:T(8,128)(2,1)} %constant.62.clone.order_ref), custom_call_target="tpu_custom_call" | custom-call | flops 402653184 | bytes 7864320 | tf_op jit(solution)/shard_map/near_part_0/pallas_call | solution.py:281
  496.6 5.5 %merge_0.1.rest_0_ = bf16[4,3,128,1536]{3,2,1,0:T(8,128)(2,1)} custom-call(bf16[512,3328]{1,0:T(8,128)(2,1)} %bitcast.48, f32[4,128,1536]{2,1,0:T(8,128)} %get-tuple-element.41.mean_ref, f32[4,128,128]{2,1,0:T(8,128)} %get-tuple-element.42.lse_ref, bf16[128,128]{1,0:T(8,128)(2,1)} %constant.61.clone.back_ref), custom_call_target="tpu_custom_call" | custom-call | flops 201326592 | bytes 7864320 | tf_op jit(solution)/shard_map/merge_0/pallas_call | solution.py:337
  502.1 5.5 %merge_2.1.rest_0_ = bf16[4,3,128,1536]{3,2,1,0:T(8,128)(2,1)} custom-call(bf16[512,3328]{1,0:T(8,128)(2,1)} %bitcast.49, f32[4,128,1536]{2,1,0:T(8,128)} %get-tuple-element.38.mean_ref, f32[4,128,128]{2,1,0:T(8,128)} %get-tuple-element.39.lse_ref, bf16[128,128]{1,0:T(8,128)(2,1)} %constant.61.clone.back_ref, ...), custom_call_target="tpu_custom_call", output_to_operand_aliasing={{}: (4, {})} | custom-call | flops 201326592 | bytes 7864320 | tf_op jit(solution)/shard_map/merge_2/pallas_call | solution.py:337
  507.6 5.4 %all-to-all-done.3 = bf16[32,16,1664]{2,1,0:T(8,128)(2,1)} async-done(((bf16[32,16,1664]{2,1,0:T(8,128)(2,1)}), bf16[32,16,1664]{2,1,0:T(8,128)(2,1)}, u32[]{:S(2)}, u32[]{:S(2)}) %all-to-all-start.3) | async-done | bytes 1703968 | tf_op jit(solution)/shard_map/all_to_all | solution.py:359
  513.1 5.5 %merge_1.1 = bf16[4,3,128,1536]{3,2,1,0:T(8,128)(2,1)} custom-call(bf16[512,1664]{1,0:T(8,128)(2,1)} %bitcast.18.far_ref, f32[4,128,1536]{2,1,0:T(8,128)} %get-tuple-element.35.mean_ref, f32[4,128,128]{2,1,0:T(8,128)} %get-tuple-element.36.lse_ref, bf16[128,128]{1,0:T(8,128)(2,1)} %constant.61.clone.back_ref, ...), custom_call_target="tpu_custom_call", output_to_operand_aliasing={{}: (4, {})} | custom-call | flops 201326592 | bytes 7864320 | tf_op jit(solution)/shard_map/merge_1/pallas_call | solution.py:337
  (29 shorter events, 17.8 us)
Async XLA Ops:
  6.5 55.2 %all-gather.6.cloned.1.call-start = ((), (), s32[]{:S(2)}) async-start(), calls=%async_computation.6 | async-start | bytes 2949120 | tf_op jit(solution)/shard_map/all_gather | solution.py:369
  11.0 18.8 %all-to-all-start = ((s32[32,1,12]{2,1,0:T(1,128)}), s32[32,1,12]{2,1,0:T(1,128)S(1)}, u32[]{:S(2)}, u32[]{:S(2)}) async-start(s32[32,1,12]{2,1,0:T(1,128)} %broadcast_select_fusion), calls=%async_computation | async-start | bytes 32768 | tf_op jit(solution)/shard_map/all_to_all | solution.py:359
  18.3 258.7 %all-gather.4.cloned.1.call-start = ((), (), s32[]{:S(2)}) async-start(), calls=%async_computation.5 | async-start | bytes 21233664 | tf_op jit(solution)/shard_map/all_gather | solution.py:371
  61.8 250.0 %all-to-all-start.1 = ((bf16[32,16,10752]{2,1,0:T(8,128)(2,1)}), bf16[32,16,10752]{2,1,0:T(8,128)(2,1)}, u32[]{:S(2)}, u32[]{:S(2)}) async-start(bf16[32,16,10752]{2,1,0:T(8,128)(2,1)} %bitcast.47), calls=%async_computation.1 | async-start | bytes 22020096 | tf_op jit(solution)/shard_map/all_to_all | solution.py:359
  311.7 74.2 %all-to-all-start.2 = ((bf16[32,16,3072]{2,1,0:T(8,128)(2,1)}), bf16[32,16,3072]{2,1,0:T(8,128)(2,1)S(1)}, u32[]{:S(2)}, u32[]{:S(2)}) async-start(bf16[32,16,3072]{2,1,0:T(8,128)(2,1)} %bitcast.52), calls=%async_computation.2 | async-start | bytes 6291456 | tf_op jit(solution)/shard_map/all_to_all | solution.py:359
  386.0 1.6 copy-start.1
  387.6 80.9 %all-to-all-start.4 = ((bf16[32,16,3328]{2,1,0:T(8,128)(2,1)}), bf16[32,16,3328]{2,1,0:T(8,128)(2,1)S(1)}, u32[]{:S(2)}, u32[]{:S(2)}) async-start(bf16[32,16,3328]{2,1,0:T(8,128)(2,1)} %bitcast.19), calls=%async_computation.4 | async-start | bytes 6815744 | tf_op jit(solution)/shard_map/all_to_all | solution.py:359
  468.5 13.7 %copy-start = (bf16[32,16,3328]{2,1,0:T(8,128)(2,1)}, bf16[32,16,3328]{2,1,0:T(8,128)(2,1)S(1)}, u32[]{:S(2)}) copy-start(bf16[32,16,3328]{2,1,0:T(8,128)(2,1)S(1)} %all-to-all-done.4) | copy-start | bytes 10223620
  468.5 44.5 %all-to-all-start.3 = ((bf16[32,16,1664]{2,1,0:T(8,128)(2,1)}), bf16[32,16,1664]{2,1,0:T(8,128)(2,1)}, u32[]{:S(2)}, u32[]{:S(2)}) async-start(bf16[32,16,1664]{2,1,0:T(8,128)(2,1)} %bitcast.51), calls=%async_computation.3 | async-start | bytes 3407872 | tf_op jit(solution)/shard_map/all_to_all | solution.py:359
Sparse Core Ops, SparseCore 0:
  8.9 52.7 all-gather.5
  63.6 213.3 all-gather.3

commit v9 on v8

--- a/solution.py
+++ b/solution.py
@@ -175,14 +175,16 @@
     lane = lax.broadcasted_iota(jnp.int32, (res, LANES), 1)
 
     def step(i, carry):
-        lse = jnp.zeros((res, LANES), F32)
+        peaks, totals = jnp.zeros((res, LANES), F32), jnp.ones((res, LANES), F32)
         for h in range(heads):
             at = pl.ds(h * HDIM, HDIM)
             out, peak, total = attend(
                 q_s[i, :, at], kv_s[i, :, at], kv_s[i, :, pl.ds(width + h * HDIM, HDIM)], bias_ref[...]
             )
             mean_s[i, :, at] = (out * (1.0 / total)).astype(BF16)
-            lse = jnp.where(lane == h, peak + jnp.log(total), lse)
+            peaks = jnp.where(lane == h, peak, peaks)
+            totals = jnp.where(lane == h, total, totals)
+        lse = peaks + jnp.log(totals)
         high = lse.astype(BF16).astype(F32)
         mid = (lse - high).astype(BF16).astype(F32)
         low = (lse - high - mid).astype(BF16).astype(F32)
@@ -259,15 +261,16 @@
         pl.when(at_line == 0)(lambda: to_away(kv_ref, order_ref, kv_s))
     else:
         kv_s = kv_ref
-    lse = jnp.zeros((res, LANES), F32)
+    peaks, totals = jnp.zeros((res, LANES), F32), jnp.ones((res, LANES), F32)
     for h in range(width // HDIM):
         at = pl.ds(h * HDIM, HDIM)
         out, peak, total = attend(
             q_ref[0, :, at], kv_s[at_line, :, at], kv_s[at_line, :, pl.ds(width + h * HDIM, HDIM)], bias_ref[0]
         )
         mean_ref[0, :, at] = out * (1.0 / total)
-        lse = jnp.where(lane == h, peak + jnp.log(total), lse)
-    lse_ref[0] = lse
+        peaks = jnp.where(lane == h, peak, peaks)
+        totals = jnp.where(lane == h, total, totals)
+    lse_ref[0] = peaks + jnp.log(totals)
 
 
 def near_part(queries, kv, bias, order, plane):

time: 527 us -> 527 us (level)
  no operation moved by 1% of the time
where the time goes in v9:
time: 527 us; the launch traced here: 525 us
  waiting for transfers between devices  275 us (52%)
  Pallas kernels  206 us (39%)
  starting transfers between devices  22.2 us (4%)
  between operations  13.5 us (3%)
  other arithmetic  5.62 us (1%)
    all_gather x1, waiting for transfers between devices, gather_weight(): lax.all_gather(blocks, 'seq', axis=1, tiled=True, axis_index_groups=within)  211 us
    pallas_call x6, Pallas kernels, project(): pl.pallas_call(functools.partial(project_kernel, len(out_shape)), grid=(s...  80.5 us
    pallas_call x3, Pallas kernels, far_attention(): pl.pallas_call(functools.partial(far_kernel, moved_kv, column), grid=(1,)...  52.3 us
    pallas_call x3, Pallas kernels, near_part(): pl.pallas_call(part_kernel, grid=(lines,), in_specs=[pl.BlockSpec((1, Non...  44.8 us
    all_to_all x5, waiting for transfers between devices, exchange(): return lax.all_to_all(rows, 'seq', split_axis=0, concat_axis=0, tiled=True)  32 us
    all_gather x1, waiting for transfers between devices, gather_weight(): lax.all_gather(shard[None], 'seq', axis=0, tiled=True, axis_index_groups=...  31.9 us
    all_to_all x5, starting transfers between devices, exchange(): return lax.all_to_all(rows, 'seq', split_axis=0, concat_axis=0, tiled=True)  22.2 us
    pallas_call x3, Pallas kernels, merge_parts(): pl.pallas_call(merge_kernel, grid=(lines,), in_specs=in_specs, out_specs=...  16.6 us
  transfers between devices with their start and end apart: 7, of which 6 were waited for; matrix products, arithmetic and copies ran while one was open for 1% of the time, Pallas kernels for 38%

profile of v9, /device:TPU:0, one launch (start us, length us, event | category | flops | bytes accessed | tf_op | source)
XLA Modules:
  0.0 525.4 jit_solution(8237721730759002600)
XLA Ops:
  11.0 7.3 %all-to-all-start = ((s32[32,1,12]{2,1,0:T(1,128)}), s32[32,1,12]{2,1,0:T(1,128)S(1)}, u32[]{:S(2)}, u32[]{:S(2)}) async-start(s32[32,1,12]{2,1,0:T(1,128)} %broadcast_select_fusion), calls=%async_computation | async-start | bytes 32768 | tf_op jit(solution)/shard_map/all_to_all | solution.py:362
  18.3 11.4 %order_sent.1 = bf16[512,10752]{1,0:T(8,128)(2,1)} custom-call(bf16[4,3,128,3072]{3,2,1,0:T(8,128)(2,1)} %bitcast.32, bf16[4,3,128,1536]{3,2,1,0:T(8,128)(2,1)} %bitcast.43, bf16[128,128]{1,0:T(8,128)(2,1)} %constant.60.clone.order_ref), custom_call_target="tpu_custom_call" | custom-call | flops 1409286144 | bytes 22020096 | tf_op jit(solution)/shard_map/order_sent/pallas_call | solution.py:69
  29.8 31.9 %all-gather.6.cloned.1.call-done = bf16[384,3072]{1,0:T(8,128)(2,1)} async-done(((bf16[96,3072]{1,0:T(8,128)(2,1)}), bf16[384,3072]{1,0:T(8,128)(2,1)}) %all-gather.6.cloned.1.call-update) | async-done | bytes 2359312 | tf_op jit(solution)/shard_map/all_gather | solution.py:372
  65.5 211.5 %all-gather.4.cloned.1.call-done = bf16[4,768,3072]{2,1,0:T(8,128)(2,1)} async-done(((bf16[4,96,3072]{2,1,0:T(8,128)(2,1)}), bf16[4,768,3072]{2,1,0:T(8,128)(2,1)}) %all-gather.4.cloned.1.call-update) | async-done | bytes 18874384 | tf_op jit(solution)/shard_map/all_gather | solution.py:374
  277.0 16.1 %project_2.1 = (bf16[4,128,3072]{2,1,0:T(8,128)(2,1)}, bf16[512,3072]{1,0:T(8,128)(2,1)}) custom-call(bf16[4,3,128,3072]{3,2,1,0:T(8,128)(2,1)} %bitcast.33, bf16[3072,3072]{1,0:T(8,128)(2,1)} %bitcast.37, bf16[128,128]{1,0:T(8,128)(2,1)} %constant.60.clone.order_ref), custom_call_target="tpu_custom_call" | custom-call | flops 9663676416 | bytes 28311552 | tf_op jit(solution)/shard_map/project_2/pallas_call | solution.py:130
  293.0 18.7 %all-to-all-done.1 = bf16[32,16,10752]{2,1,0:T(8,128)(2,1)} async-done(((bf16[32,16,10752]{2,1,0:T(8,128)(2,1)}), bf16[32,16,10752]{2,1,0:T(8,128)(2,1)}, u32[]{:S(2)}, u32[]{:S(2)}) %all-to-all-start.1) | async-done | bytes 11010080 | tf_op jit(solution)/shard_map/all_to_all | solution.py:362
  315.7 16.9 %far_0.1.rest_0_ = bf16[512,3328]{1,0:T(8,128)(2,1)} custom-call(bf16[512,10752]{1,0:T(8,128)(2,1)} %bitcast.6.q_ref.x_ref, bf16[4,128,3072]{2,1,0:T(8,128)(2,1)} %get-tuple-element.28.kv_ref, f32[3,128,128]{2,1,0:T(8,128)} %select_select_fusion.1.bias_ref, bf16[128,128]{1,0:T(8,128)(2,1)} %constant.62.clone.order_ref, bf16[128,128]{1,0:T(8,128)(2,1)} %constant.63.clone.back_ref), custom_call_target="tpu_custom_call" | custom-call | flops 402653184 | bytes 7864320 | tf_op jit(solution)/shard_map/far_0/pallas_call | solution.py:232
  332.6 15.2 %project_1.3.kv_ref = bf16[512,3072]{1,0:T(8,128)(2,1)} custom-call(bf16[512,10752]{1,0:T(8,128)(2,1)} %bitcast.6.q_ref.x_ref, bf16[3072,3072]{1,0:T(8,128)(2,1)} %bitcast.38, bf16[128,128]{1,0:T(8,128)(2,1)} %constant.60.clone.order_ref), custom_call_target="tpu_custom_call" | custom-call | flops 9663676416 | bytes 28311552 | tf_op jit(solution)/shard_map/project_1/pallas_call | solution.py:130
  347.8 17.7 %far_2.1 = bf16[512,3328]{1,0:T(8,128)(2,1)} custom-call(bf16[512,10752]{1,0:T(8,128)(2,1)} %bitcast.6.q_ref.x_ref, bf16[512,3072]{1,0:T(8,128)(2,1)} %project_1.3.kv_ref, f32[3,128,128]{2,1,0:T(8,128)} %select_select_fusion.1.bias_ref, bf16[128,128]{1,0:T(8,128)(2,1)} %constant.62.clone.order_ref, ...), custom_call_target="tpu_custom_call", output_to_operand_aliasing={{}: (5, {})} | custom-call | flops 402653184 | bytes 7864320 | tf_op jit(solution)/shard_map/far_2/pallas_call | solution.py:232
  365.5 15.2 %project_0.2.kv_ref = bf16[4,128,3072]{2,1,0:T(8,128)(2,1)} custom-call(bf16[4,3,128,3072]{3,2,1,0:T(8,128)(2,1)} %bitcast.34, bf16[3072,3072]{1,0:T(8,128)(2,1)} %bitcast.39, bf16[128,128]{1,0:T(8,128)(2,1)} %constant.60.clone.order_ref), custom_call_target="tpu_custom_call" | custom-call | flops 9663676416 | bytes 28311552 | tf_op jit(solution)/shard_map/project_0/pallas_call | solution.py:130
  380.7 5.3 %all-to-all-done.2 = bf16[32,16,3072]{2,1,0:T(8,128)(2,1)S(1)} async-done(((bf16[32,16,3072]{2,1,0:T(8,128)(2,1)}), bf16[32,16,3072]{2,1,0:T(8,128)(2,1)S(1)}, u32[]{:S(2)}, u32[]{:S(2)}) %all-to-all-start.2) | async-done | bytes 3145760 | tf_op jit(solution)/shard_map/all_to_all | solution.py:362
  387.6 4.1 all-to-all-start.4
  393.1 14.4 %near_part_1.1 = (f32[4,128,1536]{2,1,0:T(8,128)}, f32[4,128,128]{2,1,0:T(8,128)}) custom-call(bf16[4,3,128,1536]{3,2,1,0:T(8,128)(2,1)} %bitcast.44, bf16[4,128,3072]{2,1,0:T(8,128)(2,1)} %project_0.2.kv_ref, f32[3,4,128,128]{3,2,1,0:T(8,128)} %select_select_fusion.bias_ref, bf16[128,128]{1,0:T(8,128)(2,1)} %constant.62.clone.order_ref), custom_call_target="tpu_custom_call" | custom-call | flops 402653184 | bytes 7864320 | tf_op jit(solution)/shard_map/near_part_1/pallas_call | solution.py:284
  407.5 15.2 %project_0.3.kv_ref = bf16[512,3072]{1,0:T(8,128)(2,1)} custom-call(bf16[512,10752]{1,0:T(8,128)(2,1)} %bitcast.6.q_ref.x_ref, bf16[3072,3072]{1,0:T(8,128)(2,1)} %bitcast.40, bf16[128,128]{1,0:T(8,128)(2,1)} %constant.60.clone.order_ref), custom_call_target="tpu_custom_call" | custom-call | flops 9663676416 | bytes 28311552 | tf_op jit(solution)/shard_map/project_0/pallas_call | solution.py:130
  422.7 16.0 %near_part_2.1 = (f32[4,128,1536]{2,1,0:T(8,128)}, f32[4,128,128]{2,1,0:T(8,128)}) custom-call(bf16[4,3,128,1536]{3,2,1,0:T(8,128)(2,1)} %bitcast.45, bf16[512,3072]{1,0:T(8,128)(2,1)} %project_0.3.kv_ref, f32[3,4,128,128]{3,2,1,0:T(8,128)} %select_select_fusion.bias_ref, bf16[128,128]{1,0:T(8,128)(2,1)} %constant.62.clone.order_ref), custom_call_target="tpu_custom_call" | custom-call | flops 402653184 | bytes 7864320 | tf_op jit(solution)/shard_map/near_part_2/pallas_call | solution.py:284
  438.7 9.4 %project_1.4.rest_0_ = bf16[4,128,3072]{2,1,0:T(8,128)(2,1)} custom-call(bf16[4,3,128,3072]{3,2,1,0:T(8,128)(2,1)} %bitcast.35, bf16[3072,3072]{1,0:T(8,128)(2,1)} %bitcast.41, bf16[128,128]{1,0:T(8,128)(2,1)} %constant.60.clone.order_ref), custom_call_target="tpu_custom_call" | custom-call | flops 4831838208 | bytes 14155776 | tf_op jit(solution)/shard_map/project_1/pallas_call | solution.py:130
  448.2 17.7 %far_1.1 = bf16[512,1664]{1,0:T(8,128)(2,1)} custom-call(bf16[512,10752]{1,0:T(8,128)(2,1)} %bitcast.6.q_ref.x_ref, bf16[512,3072]{1,0:T(8,128)(2,1)} %bitcast.50, f32[3,128,128]{2,1,0:T(8,128)} %select_select_fusion.1.bias_ref, bf16[128,128]{1,0:T(8,128)(2,1)} %constant.62.clone.order_ref, bf16[128,128]{1,0:T(8,128)(2,1)} %constant.63.clone.back_ref), custom_call_target="tpu_custom_call" | custom-call | flops 402653184 | bytes 7864320 | tf_op jit(solution)/shard_map/far_1/pallas_call | solution.py:232
  468.5 4.3 all-to-all-start.3
  472.8 9.4 %project_1.5.kv_ref = bf16[4,128,3072]{2,1,0:T(8,128)(2,1)} custom-call(bf16[4,3,128,3072]{3,2,1,0:T(8,128)(2,1)} %bitcast.36, bf16[3072,3072]{1,0:T(8,128)(2,1)} %bitcast.42, bf16[128,128]{1,0:T(8,128)(2,1)} %constant.60.clone.order_ref, bf16[4,128,3072]{2,1,0:T(8,128)(2,1)} %project_1.4.rest_0_), custom_call_target="tpu_custom_call", output_to_operand_aliasing={{}: (3, {})} | custom-call | flops 4831838208 | bytes 14155776 | tf_op jit(solution)/shard_map/project_1/pallas_call | solution.py:130
  482.2 14.4 %near_part_0.1 = (f32[4,128,1536]{2,1,0:T(8,128)}, f32[4,128,128]{2,1,0:T(8,128)}) custom-call(bf16[4,3,128,1536]{3,2,1,0:T(8,128)(2,1)} %bitcast.46, bf16[4,128,3072]{2,1,0:T(8,128)(2,1)} %project_1.5.kv_ref, f32[3,4,128,128]{3,2,1,0:T(8,128)} %select_select_fusion.bias_ref, bf16[128,128]{1,0:T(8,128)(2,1)} %constant.62.clone.order_ref), custom_call_target="tpu_custom_call" | custom-call | flops 402653184 | bytes 7864320 | tf_op jit(solution)/shard_map/near_part_0/pallas_call | solution.py:284
  496.6 5.5 %merge_0.1.rest_0_ = bf16[4,3,128,1536]{3,2,1,0:T(8,128)(2,1)} custom-call(bf16[512,3328]{1,0:T(8,128)(2,1)} %bitcast.48, f32[4,128,1536]{2,1,0:T(8,128)} %get-tuple-element.41.mean_ref, f32[4,128,128]{2,1,0:T(8,128)} %get-tuple-element.42.lse_ref, bf16[128,128]{1,0:T(8,128)(2,1)} %constant.61.clone.back_ref), custom_call_target="tpu_custom_call" | custom-call | flops 201326592 | bytes 7864320 | tf_op jit(solution)/shard_map/merge_0/pallas_call | solution.py:340
  502.1 5.5 %merge_2.1.rest_0_ = bf16[4,3,128,1536]{3,2,1,0:T(8,128)(2,1)} custom-call(bf16[512,3328]{1,0:T(8,128)(2,1)} %bitcast.49, f32[4,128,1536]{2,1,0:T(8,128)} %get-tuple-element.38.mean_ref, f32[4,128,128]{2,1,0:T(8,128)} %get-tuple-element.39.lse_ref, bf16[128,128]{1,0:T(8,128)(2,1)} %constant.61.clone.back_ref, ...), custom_call_target="tpu_custom_call", output_to_operand_aliasing={{}: (4, {})} | custom-call | flops 201326592 | bytes 7864320 | tf_op jit(solution)/shard_map/merge_2/pallas_call | solution.py:340
  507.6 5.4 %all-to-all-done.3 = bf16[32,16,1664]{2,1,0:T(8,128)(2,1)} async-done(((bf16[32,16,1664]{2,1,0:T(8,128)(2,1)}), bf16[32,16,1664]{2,1,0:T(8,128)(2,1)}, u32[]{:S(2)}, u32[]{:S(2)}) %all-to-all-start.3) | async-done | bytes 1703968 | tf_op jit(solution)/shard_map/all_to_all | solution.py:362
  513.1 5.5 %merge_1.1 = bf16[4,3,128,1536]{3,2,1,0:T(8,128)(2,1)} custom-call(bf16[512,1664]{1,0:T(8,128)(2,1)} %bitcast.18.far_ref, f32[4,128,1536]{2,1,0:T(8,128)} %get-tuple-element.35.mean_ref, f32[4,128,128]{2,1,0:T(8,128)} %get-tuple-element.36.lse_ref, bf16[128,128]{1,0:T(8,128)(2,1)} %constant.61.clone.back_ref, ...), custom_call_target="tpu_custom_call", output_to_operand_aliasing={{}: (4, {})} | custom-call | flops 201326592 | bytes 7864320 | tf_op jit(solution)/shard_map/merge_1/pallas_call | solution.py:340
  (29 shorter events, 17.9 us)
Async XLA Ops:
  6.5 55.2 %all-gather.6.cloned.1.call-start = ((), (), s32[]{:S(2)}) async-start(), calls=%async_computation.6 | async-start | bytes 2949120 | tf_op jit(solution)/shard_map/all_gather | solution.py:372
  11.0 18.8 %all-to-all-start = ((s32[32,1,12]{2,1,0:T(1,128)}), s32[32,1,12]{2,1,0:T(1,128)S(1)}, u32[]{:S(2)}, u32[]{:S(2)}) async-start(s32[32,1,12]{2,1,0:T(1,128)} %broadcast_select_fusion), calls=%async_computation | async-start | bytes 32768 | tf_op jit(solution)/shard_map/all_to_all | solution.py:362
  18.3 258.7 %all-gather.4.cloned.1.call-start = ((), (), s32[]{:S(2)}) async-start(), calls=%async_computation.5 | async-start | bytes 21233664 | tf_op jit(solution)/shard_map/all_gather | solution.py:374
  61.8 250.0 %all-to-all-start.1 = ((bf16[32,16,10752]{2,1,0:T(8,128)(2,1)}), bf16[32,16,10752]{2,1,0:T(8,128)(2,1)}, u32[]{:S(2)}, u32[]{:S(2)}) async-start(bf16[32,16,10752]{2,1,0:T(8,128)(2,1)} %bitcast.47), calls=%async_computation.1 | async-start | bytes 22020096 | tf_op jit(solution)/shard_map/all_to_all | solution.py:362
  311.7 74.2 %all-to-all-start.2 = ((bf16[32,16,3072]{2,1,0:T(8,128)(2,1)}), bf16[32,16,3072]{2,1,0:T(8,128)(2,1)S(1)}, u32[]{:S(2)}, u32[]{:S(2)}) async-start(bf16[32,16,3072]{2,1,0:T(8,128)(2,1)} %bitcast.52), calls=%async_computation.2 | async-start | bytes 6291456 | tf_op jit(solution)/shard_map/all_to_all | solution.py:362
  386.0 1.6 copy-start.1
  387.6 80.9 %all-to-all-start.4 = ((bf16[32,16,3328]{2,1,0:T(8,128)(2,1)}), bf16[32,16,3328]{2,1,0:T(8,128)(2,1)S(1)}, u32[]{:S(2)}, u32[]{:S(2)}) async-start(bf16[32,16,3328]{2,1,0:T(8,128)(2,1)} %bitcast.19), calls=%async_computation.4 | async-start | bytes 6815744 | tf_op jit(solution)/shard_map/all_to_all | solution.py:362
  468.5 13.7 %copy-start = (bf16[32,16,3328]{2,1,0:T(8,128)(2,1)}, bf16[32,16,3328]{2,1,0:T(8,128)(2,1)S(1)}, u32[]{:S(2)}) copy-start(bf16[32,16,3328]{2,1,0:T(8,128)(2,1)S(1)} %all-to-all-done.4) | copy-start | bytes 10223620
  468.5 44.5 %all-to-all-start.3 = ((bf16[32,16,1664]{2,1,0:T(8,128)(2,1)}), bf16[32,16,1664]{2,1,0:T(8,128)(2,1)}, u32[]{:S(2)}, u32[]{:S(2)}) async-start(bf16[32,16,1664]{2,1,0:T(8,128)(2,1)} %bitcast.51), calls=%async_computation.3 | async-start | bytes 3407872 | tf_op jit(solution)/shard_map/all_to_all | solution.py:362
Sparse Core Ops, SparseCore 0:
  8.9 52.7 all-gather.5
  63.6 213.3 all-gather.3
